TPU v7x, 128 devices: a whole 4x4x4 slice. The times are simulated.
128 devices in a mesh: gy: 8 (over z, core), gx: 16 (over x, y).
Axes of the slice: x: 4, y: 4, z: 4, core: 2. Of those that a mesh axis runs over, the one named last changes fastest.
Arguments:
- tokens_in: bfloat16 [512, 768, 256], P('gy', 'gx'), may hold values from -6 to 6
- saved_mid: bfloat16 [512, 768, 256], P('gy', 'gx'), may hold values from -6 to 6
- grad_out: bfloat16 [512, 768, 256], P('gy', 'gx'), may hold values from -6 to 6
- attn_gain: float32 [256], replicated, may hold values from 0.1 to 1.9
- mlp_gain: float32 [256], replicated, may hold values from 0.1 to 1.9
- w_query: bfloat16 [256, 256], replicated, may hold values from -1 to 1
- w_key: bfloat16 [256, 256], replicated, may hold values from -1 to 1
- w_value: bfloat16 [256, 256], replicated, may hold values from -0.375 to 0.375
- w_out: bfloat16 [256, 256], replicated, may hold values from -0.375 to 0.375
- w_up: bfloat16 [256, 1024], replicated, may hold values from -0.375 to 0.375
- conv_kernel: float32 [9, 1024], replicated, may hold values from -2 to 2
- w_down: bfloat16 [1024, 256], replicated, may hold values from -0.1875 to 0.1875
- row_mask: int32 [6, 6], replicated, may hold values from 0 to 1, as said below
- col_mask: int32 [4, 4], replicated, may hold values from 0 to 1, as said below
Outputs:
- grad_tokens: bfloat16 [512, 768, 256], P('gy', 'gx')
Inputs may be any that keep to these rules, and one draw needn't show every extreme that they name: `row_mask`: every diagonal entry is 1, so each query block sees at least itself. `col_mask`: every diagonal entry is 1, so each query block sees at least itself.
All inputs are finite; a program needn't handle non-finite values.
Results may differ from a plain program's by a relative error of at most 0.04.
Values may be sent and summed in bfloat16 or wider, within the bound.
No kernel may reach another device: no remote copies, remote signals or barrier semaphores. Data moves between devices by JAX's collectives and lax.ppermute only.
A program may use at most 128 MiB of HBM per device.

v0:
```python
import jax
import jax.numpy as jnp
from jax import lax
from jax.sharding import PartitionSpec as P

HEADS = 8
BLK = 128


EPSILON = 1e-05
GELU_C = 0.7978845608028654


def with_halo(shard, sides, width):
    for axis, dim in sides:
        count, length = (lax.axis_size(axis), shard.shape[dim])
        up = [(i, (i + 1) % count) for i in range(count - 1)]
        down = [(j, i) for i, j in up]
        last = lax.slice_in_dim(shard, length - width, length, axis=dim)
        initial = lax.slice_in_dim(shard, 0, width, axis=dim)
        before = lax.ppermute(last, axis, up)
        after = lax.ppermute(initial, axis, down)
        shard = jnp.concatenate([before, shard, after], axis=dim)
    return shard


def layer_norm(values, gain_vec):
    values = values.astype(jnp.float32)
    center = values - jnp.mean(values, axis=-1, keepdims=True)
    inv_std = lax.rsqrt(jnp.mean(center * center, axis=-1, keepdims=True) + EPSILON)
    normed = center * inv_std
    return (normed * gain_vec, normed, inv_std)


def norm_backward(grad_norm, gain_vec, normed, inv_std):
    grad_hat = grad_norm * gain_vec
    return inv_std * (
        grad_hat
        - jnp.mean(grad_hat, axis=-1, keepdims=True)
        - normed * jnp.mean(grad_hat * normed, axis=-1, keepdims=True)
    )


def gelu_slope(value):
    inside_term = GELU_C * (value + 0.044715 * value * value * value)
    tanh_val = jnp.tanh(inside_term)
    return 0.5 * (1.0 + tanh_val) + 0.5 * value * (1.0 - tanh_val * tanh_val) * GELU_C * (
        1.0 + 3.0 * 0.044715 * value * value
    )


def mlp_band(mid_pad, grad_pad, mlp_gain, w_up, conv_kernel, w_down):
    rows_in = mid_pad.shape[0] - 4
    cols_in = mid_pad.shape[1] - 4
    mid_norm, mid_hat, mid_inv = layer_norm(mid_pad, mlp_gain)
    hidden = jnp.dot(
        mid_norm.astype(jnp.bfloat16), w_up, preferred_element_type=jnp.float32
    ).astype(jnp.bfloat16)
    pre_act = jnp.zeros((rows_in + 2, cols_in + 2, hidden.shape[-1]), jnp.float32)
    for row_shift in range(3):
        for col_shift in range(3):
            pre_act = (
                pre_act
                + conv_kernel[3 * row_shift + col_shift]
                * hidden[row_shift : row_shift + rows_in + 2, col_shift : col_shift + cols_in + 2]
            )
    grad_act = jnp.dot(grad_pad[1:-1, 1:-1], w_down.T, preferred_element_type=jnp.float32)
    grad_pre = (grad_act * gelu_slope(pre_act)).astype(jnp.bfloat16)
    grad_hidden = jnp.zeros((rows_in, cols_in, hidden.shape[-1]), jnp.float32)
    for row_shift in range(3):
        for col_shift in range(3):
            grad_hidden = (
                grad_hidden
                + conv_kernel[3 * row_shift + col_shift]
                * grad_pre[
                    2 - row_shift : 2 - row_shift + rows_in, 2 - col_shift : 2 - col_shift + cols_in
                ]
            )
    grad_hidden = grad_hidden.astype(jnp.bfloat16)
    grad_norm = jnp.dot(grad_hidden, w_up.T, preferred_element_type=jnp.float32)
    norm_grad = norm_backward(grad_norm, mlp_gain, mid_hat[2:-2, 2:-2], mid_inv[2:-2, 2:-2])
    return (grad_pad[2:-2, 2:-2].astype(jnp.float32) + norm_grad).astype(jnp.bfloat16)


def block_allowed(mask_table):
    return jnp.repeat(jnp.repeat(mask_table > 0, BLK, axis=0), BLK, axis=1)


def line_grads(qkv_line, grad_line, allowed, head_count):
    length = qkv_line.shape[0]
    half_width = grad_line.shape[-1]
    head_dim = half_width // head_count
    qkv_parts = qkv_line.reshape(length, 3, head_count, head_dim)
    queries = qkv_parts[:, 0]
    key_heads = qkv_parts[:, 1]
    value_heads = qkv_parts[:, 2]
    grad_heads = grad_line.reshape(length, head_count, head_dim)
    factor = head_dim ** (-0.5)
    scores = (
        jnp.einsum("qhd,khd->hqk", queries, key_heads, preferred_element_type=jnp.float32) * factor
    )
    scores = jnp.where(allowed[None], scores, -jnp.inf)
    row_top = jnp.max(scores, axis=-1, keepdims=True)
    exp_terms = jnp.exp(scores - row_top)
    prob_rows = exp_terms / jnp.sum(exp_terms, axis=-1, keepdims=True)
    prob_low = prob_rows.astype(jnp.bfloat16)
    attended = jnp.einsum(
        "hqk,khd->qhd", prob_low, value_heads, preferred_element_type=jnp.float32
    ).astype(jnp.bfloat16)
    row_delta = jnp.sum(grad_heads.astype(jnp.float32) * attended.astype(jnp.float32), axis=-1)
    grad_probs = jnp.einsum(
        "qhd,khd->hqk", grad_heads, value_heads, preferred_element_type=jnp.float32
    )
    grad_scores = (prob_rows * (grad_probs - jnp.transpose(row_delta)[:, :, None])).astype(
        jnp.bfloat16
    )
    grad_query = (
        jnp.einsum("hqk,khd->qhd", grad_scores, key_heads, preferred_element_type=jnp.float32)
        * factor
    ).astype(jnp.bfloat16)
    grad_key = (
        jnp.einsum("hqk,qhd->khd", grad_scores, queries, preferred_element_type=jnp.float32)
        * factor
    ).astype(jnp.bfloat16)
    grad_value = jnp.einsum(
        "hqk,qhd->khd", prob_low, grad_heads, preferred_element_type=jnp.float32
    ).astype(jnp.bfloat16)
    return jnp.stack([grad_query, grad_key, grad_value], axis=1).reshape(length, 3 * half_width)


def make_payload(normed_in, grad_heads, w_heads):
    head_inputs = jnp.dot(normed_in, w_heads, preferred_element_type=jnp.float32).astype(
        jnp.bfloat16
    )
    return jnp.concatenate([head_inputs, grad_heads], axis=-1)


def line_work(line_data, w_heads, allowed):
    half_width = w_heads.shape[1] // 3
    grad_parts = line_grads(
        line_data[:, : 3 * half_width], line_data[:, 3 * half_width :], allowed, HEADS // 2
    )
    return grad_parts


def finish_heads(returned, w_heads):
    return jnp.dot(returned, w_heads.T, preferred_element_type=jnp.float32).astype(jnp.bfloat16)


def per_device(
    tokens_in,
    saved_mid,
    grad_out,
    attn_gain,
    mlp_gain,
    w_query,
    w_key,
    w_value,
    w_out,
    w_up,
    conv_kernel,
    w_down,
    row_mask,
    col_mask,
):
    model_width = tokens_in.shape[-1]
    half_width = model_width // 2
    tile_rows = tokens_in.shape[0]
    tile_cols = tokens_in.shape[1]
    count_gx = lax.axis_size("gx")
    count_gy = lax.axis_size("gy")
    joined = jnp.concatenate([saved_mid, grad_out], axis=-1)
    padded = with_halo(joined, (("gy", 0), ("gx", 1)), 2)
    grad_mid = mlp_band(
        padded[..., :model_width], padded[..., model_width:], mlp_gain, w_up, conv_kernel, w_down
    )
    grad_attn = jnp.dot(grad_mid, w_out.T, preferred_element_type=jnp.float32).astype(jnp.bfloat16)
    in_norm, in_hat, in_inv = layer_norm(tokens_in, attn_gain)
    normed_in = in_norm.astype(jnp.bfloat16)
    w_row = jnp.concatenate(
        [w_query[:, :half_width], w_key[:, :half_width], w_value[:, :half_width]], axis=1
    )
    w_col = jnp.concatenate(
        [w_query[:, half_width:], w_key[:, half_width:], w_value[:, half_width:]], axis=1
    )
    allowed_row = block_allowed(row_mask)
    allowed_col = block_allowed(col_mask)
    row_payload = make_payload(normed_in, grad_attn[..., :half_width], w_row)
    row_payload = row_payload.reshape(
        count_gx, tile_rows // count_gx, tile_cols, row_payload.shape[-1]
    )

    def row_single(line_data):
        return line_work(line_data, w_row, allowed_row)

    row_result = lax.map(
        row_single, lax.all_to_all(row_payload, "gx", split_axis=0, concat_axis=2, tiled=True)[0]
    )[None]
    row_back = lax.all_to_all(row_result, "gx", split_axis=2, concat_axis=0, tiled=True)
    row_back = row_back.reshape(tile_rows, tile_cols, row_back.shape[-1])
    col_payload = make_payload(normed_in, grad_attn[..., half_width:], w_col)
    col_payload = col_payload.reshape(
        tile_rows, count_gy, tile_cols // count_gy, col_payload.shape[-1]
    )

    def col_single(line_data):
        return line_work(line_data, w_col, allowed_col)

    lines = jnp.swapaxes(
        lax.all_to_all(col_payload, "gy", split_axis=1, concat_axis=0, tiled=True)[:, 0], 0, 1
    )
    col_result = jnp.swapaxes(lax.map(col_single, lines), 0, 1)[:, None]
    col_back = lax.all_to_all(col_result, "gy", split_axis=0, concat_axis=1, tiled=True)
    col_back = col_back.reshape(tile_rows, tile_cols, col_back.shape[-1])
    grad_row_in = finish_heads(row_back, w_row)
    grad_col_in = finish_heads(col_back, w_col)
    norm_grad = norm_backward(
        grad_row_in.astype(jnp.float32) + grad_col_in.astype(jnp.float32), attn_gain, in_hat, in_inv
    )
    return (grad_mid.astype(jnp.float32) + norm_grad).astype(jnp.bfloat16)


def solution(mesh):
    in_specs = (
        P("gy", "gx", None),
        P("gy", "gx", None),
        P("gy", "gx", None),
        P(),
        P(),
        P(),
        P(),
        P(),
        P(),
        P(),
        P(),
        P(),
        P(),
        P(),
    )
    out_specs = P("gy", "gx", None)
    return jax.shard_map(
        per_device, mesh=mesh, in_specs=in_specs, out_specs=out_specs, check_vma=False
    )
```

profile of v0, /device:TPU:1, one launch (start us, length us, event | category | flops | bytes accessed | tf_op | source)
XLA Modules:
  0.0 389.5 jit_solution(10555201473155276179)
XLA Ops:
  0.0 2.0 copy_dynamic-update-slice_fusion
  2.8 3.3 collective-permute-start.1
  6.2 3.5 collective-permute-start
  16.4 4.5 %collective-permute-start.2 = (bf16[68,2,512]{2,0,1:T(8,128)(2,1)S(1)}, bf16[68,2,512]{2,0,1:T(8,128)(2,1)S(1)}, u32[]{:S(2)}, u32[]{:S(2)}) collective-permute-start(bf16[68,2,512]{2,0,1:T(8,128)(2,1)S(1)} %get-tuple-element.113), channel_id=1, source_target_pairs={{0,1},{1,2},{2,3},{3,4},{4,5},{5,6},{6,7},{7,8},{8,9},{9,10},{10,1... | collective-permute-start | bytes 417800 | tf_op jit(solution)/shard_map/ppermute | solution.py:21
  21.9 1.8 collective-permute-done.2
  23.7 2.0 pad_maximum_fusion.2
  26.7 1.7 fusion.54
  28.5 3.1 fusion.52
  31.6 2.5 convolution_convert_fusion.4
  34.2 28.5 %fusion.50 = bf16[66,50,1024]{2,0,1:T(8,128)(2,1)} fusion(bf16[68,52,1024]{2,0,1:T(8,128)(2,1)S(1)} %convolution_convert_fusion.4, f32[1024]{0:T(1024)S(1)} %bitcast.333, f32[1024]{0:T(1024)S(1)} %bitcast.335, f32[1024]{0:T(1024)S(1)} %bitcast.321, f32[1024]{0:T(1024)S(1)} %bitcast.323, f32[1024]{0:T(1024)S(1)} %bitcast.325, f32[1024]{0:T(1024)S(1)} %bitcast.327, ...), kind=kOutput, calls=%fused_computation.76 | convolution fusion | flops 1890662400 | bytes 71766016 | tf_op jit(solution)/shard_map/dot_general | solution.py:67
  62.7 33.7 %multiply_reduce_fusion.1 = (f32[64,48]{0,1:T(8,128)S(1)}, f32[64,48]{0,1:T(8,128)S(1)}, f32[64,48,256]{2,0,1:T(8,128)}) fusion(f32[256]{0:T(256)S(1)} %copy-done.34, f32[68,52,256]{2,0,1:T(8,128)} %fusion.52, bf16[256,1024]{1,0:T(8,128)(2,1)S(1)} %copy-done, bf16[66,50,1024]{2,0,1:T(8,128)(2,1)} %fusion.50, f32[1024]{0:T(1024)S(1)} %bitcast.334, ...), kind=kOutput, calls=%fused_computation.106 | convolution fusion | flops 1698686976 | bytes 63501312 | tf_op jit(solution)/shard_map/dot_general | solution.py:80
  96.4 4.6 %add_convert_fusion.2 = bf16[64,48,256]{2,0,1:T(8,128)(2,1)S(1)} fusion(f32[68,52,256]{2,0,1:T(8,128)} %fusion.52, f32[64,48,256]{2,0,1:T(8,128)} %get-tuple-element.136, f32[64,48]{0,1:T(8,128)S(1)} %get-tuple-element.138, f32[64,48]{0,1:T(8,128)S(1)} %get-tuple-element.139, f32[256]{0:T(256)S(1)} %copy-done.34, f32[64,48]{0,1:T(8,128)S(1)} %slice_bitcast_fusion.34, ...), kind=kLoop, calls=%fused_computation.104 | loop fusion | flops 6291456 | bytes 9475072 | tf_op jit(solution)/shard_map/convert_element_type | solution.py:82
  104.0 3.4 copy.103
  107.5 5.8 %all-to-all-start.2 = ((bf16[64,8,6,512]{3,0,2,1:T(8,128)(2,1)}), bf16[64,8,6,512]{3,0,2,1:T(8,128)(2,1)}, u32[]{:S(2)}, u32[]{:S(2)}) async-start(bf16[64,8,6,512]{3,0,2,1:T(8,128)(2,1)} %bitcast.307), calls=%async_computation.2 | async-start | bytes 6291456 | tf_op jit(solution)/shard_map/all_to_all | solution.py:210
  113.7 1.4 convolution_convert_fusion.6
  115.1 2.1 pad_maximum_fusion.3
  117.2 33.7 %all-to-all-done.2 = bf16[64,8,6,512]{3,0,2,1:T(8,128)(2,1)} async-done(((bf16[64,8,6,512]{3,0,2,1:T(8,128)(2,1)}), bf16[64,8,6,512]{3,0,2,1:T(8,128)(2,1)}, u32[]{:S(2)}, u32[]{:S(2)}) %all-to-all-start.2) | async-done | bytes 3145760 | tf_op jit(solution)/shard_map/all_to_all | solution.py:210
  150.9 10.0 %all-to-all-start = ((bf16[16,4,48,512]{3,2,1,0:T(8,128)(2,1)}), bf16[16,4,48,512]{3,2,1,0:T(8,128)(2,1)}, u32[]{:S(2)}, u32[]{:S(2)}) async-start(bf16[16,4,48,512]{3,2,1,0:T(8,128)(2,1)} %bitcast.306), calls=%async_computation | async-start | bytes 6291456 | tf_op jit(solution)/shard_map/all_to_all | solution.py:197
  160.9 4.0 %copy.104 = bf16[8,64,1,6,512]{4,1,0,3,2:T(8,128)(2,1)} copy(bf16[8,64,1,6,512]{4,1,3,0,2:T(8,128)(2,1)} %bitcast.26) | data formatting | bytes 6291456 | tf_op jit(solution)/shard_map/all_to_all | solution.py:210
  164.9 76.5 %while.23 = (s32[]{:T(128)}, bf16[6,512,384]{1,2,0:T(8,128)(2,1)}, bf16[6,512,512]{2,1,0:T(8,128)(2,1)}, pred[512,4]{0,1:T(4,128)(4,1)S(1)}, s32[]{:T(128)}) while((s32[]{:T(128)}, bf16[6,512,384]{1,2,0:T(8,128)(2,1)}, bf16[6,512,512]{2,1,0:T(8,128)(2,1)}, pred[512,4]{0,1:T(4,128)(4,1)S(1)}, s32[]{:T(128)}) %tuple.78), condition=%wide.region_15.16_spmd.clone, body=%wide.region_11.15_spmd.clone.sunk | while | flops 414185984 | bytes 48801896 | solution.py:212
  166.3 3.6 fusion.160
  169.9 2.8 fusion.161
  179.1 3.6 fusion.160
  182.7 2.8 fusion.161
  191.8 3.6 fusion.160
  195.4 2.8 fusion.161
  204.6 3.6 fusion.160
  208.2 2.8 fusion.161
  217.3 3.6 fusion.160
  220.9 2.8 fusion.161
  230.1 3.6 fusion.160
  233.7 2.8 fusion.161
  241.4 4.8 %copy.107 = bf16[6,512,384]{2,0,1:T(8,128)(2,1)} copy(bf16[6,512,384]{1,2,0:T(8,128)(2,1)} %get-tuple-element.50) | data formatting | bytes 4718592 | tf_op jit(solution)/shard_map/while | solution.py:212
  246.2 5.5 %all-to-all-start.3 = ((bf16[512,1,6,384]{3,2,1,0:T(8,128)(2,1)}), bf16[512,1,6,384]{3,2,1,0:T(8,128)(2,1)}, u32[]{:S(2)}, u32[]{:S(2)}) async-start(bf16[512,1,6,384]{3,2,1,0:T(8,128)(2,1)} %bitcast.308), calls=%async_computation.3 | async-start | bytes 6291456 | tf_op jit(solution)/shard_map/all_to_all | solution.py:213
  251.7 3.8 copy.95
  255.5 79.5 %while.22 = (s32[]{:T(128)}, bf16[4,768,384]{1,2,0:T(8,128)(2,1)}, bf16[4,768,512]{2,1,0:T(8,128)(2,1)}, pred[768,6]{0,1:T(8,128)(4,1)S(1)}, s32[]{:T(128)}) while((s32[]{:T(128)}, bf16[4,768,384]{1,2,0:T(8,128)(2,1)}, bf16[4,768,512]{2,1,0:T(8,128)(2,1)}, pred[768,6]{0,1:T(8,128)(4,1)S(1)}, s32[]{:T(128)}) %tuple.77), condition=%wide.region_10.11_spmd.clone, body=%wide.region_6.10_spmd.clone.sunk | while | flops 931133184 | bytes 95617680 | solution.py:196
  257.2 6.0 %fusion.148 = (f32[4,768]{1,0:T(4,128)S(1)}, f32[4,768,768]{1,2,0:T(8,128)}) fusion(pred[768,768]{0,1:T(8,128)(4,1)S(1)} %bitcast.305, bf16[768,3,4,32]{0,3,2,1:T(8,128)(2,1)S(1)} %bitcast.282), kind=kOutput, calls=%fused_computation.160.clone.1 | convolution fusion | flops 160432896 | bytes 10432512 | tf_op jit(solution)/shard_map/while/body/eval_jaxpr/sub | solution.py:104
  263.2 4.6 %fusion.149 = bf16[4,768,768]{1,2,0:T(8,128)(2,1)S(1)} fusion(f32[4,768,768]{1,2,0:T(8,128)} %get-tuple-element.192, f32[4,768]{1,0:T(4,128)S(1)} %get-tuple-element.193), kind=kLoop, calls=%fused_computation.11.clone.1 | loop fusion | flops 4718592 | bytes 14168064 | tf_op jit(solution)/shard_map/while/body/eval_jaxpr/convert_element_type | solution.py:106
  267.9 1.5 fusion.150
  270.3 1.7 multiply_convert_fusion.6
  272.1 1.5 fusion.152
  277.1 6.0 %fusion.148 = (f32[4,768]{1,0:T(4,128)S(1)}, f32[4,768,768]{1,2,0:T(8,128)}) fusion(pred[768,768]{0,1:T(8,128)(4,1)S(1)} %bitcast.305, bf16[768,3,4,32]{0,3,2,1:T(8,128)(2,1)S(1)} %bitcast.282), kind=kOutput, calls=%fused_computation.160.clone.1 | convolution fusion | flops 160432896 | bytes 10432512 | tf_op jit(solution)/shard_map/while/body/eval_jaxpr/sub | solution.py:104
  283.1 4.6 %fusion.149 = bf16[4,768,768]{1,2,0:T(8,128)(2,1)S(1)} fusion(f32[4,768,768]{1,2,0:T(8,128)} %get-tuple-element.192, f32[4,768]{1,0:T(4,128)S(1)} %get-tuple-element.193), kind=kLoop, calls=%fused_computation.11.clone.1 | loop fusion | flops 4718592 | bytes 14168064 | tf_op jit(solution)/shard_map/while/body/eval_jaxpr/convert_element_type | solution.py:106
  287.8 1.5 fusion.150
  290.2 1.7 multiply_convert_fusion.6
  292.0 1.5 fusion.152
  297.0 6.0 %fusion.148 = (f32[4,768]{1,0:T(4,128)S(1)}, f32[4,768,768]{1,2,0:T(8,128)}) fusion(pred[768,768]{0,1:T(8,128)(4,1)S(1)} %bitcast.305, bf16[768,3,4,32]{0,3,2,1:T(8,128)(2,1)S(1)} %bitcast.282), kind=kOutput, calls=%fused_computation.160.clone.1 | convolution fusion | flops 160432896 | bytes 10432512 | tf_op jit(solution)/shard_map/while/body/eval_jaxpr/sub | solution.py:104
  303.0 4.6 %fusion.149 = bf16[4,768,768]{1,2,0:T(8,128)(2,1)S(1)} fusion(f32[4,768,768]{1,2,0:T(8,128)} %get-tuple-element.192, f32[4,768]{1,0:T(4,128)S(1)} %get-tuple-element.193), kind=kLoop, calls=%fused_computation.11.clone.1 | loop fusion | flops 4718592 | bytes 14168064 | tf_op jit(solution)/shard_map/while/body/eval_jaxpr/convert_element_type | solution.py:106
  307.6 1.5 fusion.150
  310.1 1.7 multiply_convert_fusion.6
  311.8 1.5 fusion.152
  316.9 6.0 %fusion.148 = (f32[4,768]{1,0:T(4,128)S(1)}, f32[4,768,768]{1,2,0:T(8,128)}) fusion(pred[768,768]{0,1:T(8,128)(4,1)S(1)} %bitcast.305, bf16[768,3,4,32]{0,3,2,1:T(8,128)(2,1)S(1)} %bitcast.282), kind=kOutput, calls=%fused_computation.160.clone.1 | convolution fusion | flops 160432896 | bytes 10432512 | tf_op jit(solution)/shard_map/while/body/eval_jaxpr/sub | solution.py:104
  322.8 4.6 %fusion.149 = bf16[4,768,768]{1,2,0:T(8,128)(2,1)S(1)} fusion(f32[4,768,768]{1,2,0:T(8,128)} %get-tuple-element.192, f32[4,768]{1,0:T(4,128)S(1)} %get-tuple-element.193), kind=kLoop, calls=%fused_computation.11.clone.1 | loop fusion | flops 4718592 | bytes 14168064 | tf_op jit(solution)/shard_map/while/body/eval_jaxpr/convert_element_type | solution.py:106
  327.5 1.5 fusion.150
  329.9 1.7 multiply_convert_fusion.6
  331.7 1.5 fusion.152
  335.0 5.4 %copy.98 = bf16[4,768,384]{2,0,1:T(4,128)(2,1)} copy(bf16[4,768,384]{1,2,0:T(8,128)(2,1)} %get-tuple-element.49) | data formatting | bytes 4718592 | tf_op jit(solution)/shard_map/while | solution.py:196
  340.5 7.0 %all-to-all-start.1 = ((bf16[1,4,768,384]{3,1,0,2:T(4,128)(2,1)}), bf16[1,4,768,384]{3,1,0,2:T(4,128)(2,1)S(1)}, u32[]{:S(2)}, u32[]{:S(2)}) async-start(bf16[1,4,768,384]{3,1,0,2:T(4,128)(2,1)} %bitcast.19), calls=%async_computation.1 | async-start | bytes 4718592 | tf_op jit(solution)/shard_map/all_to_all | solution.py:199
  347.5 2.2 copy.108
  349.7 1.7 copy.109
  351.4 28.0 %all-to-all-done.1 = bf16[1,4,768,384]{3,1,0,2:T(4,128)(2,1)S(1)} async-done(((bf16[1,4,768,384]{3,1,0,2:T(4,128)(2,1)}), bf16[1,4,768,384]{3,1,0,2:T(4,128)(2,1)S(1)}, u32[]{:S(2)}, u32[]{:S(2)}) %all-to-all-start.1) | async-done | bytes 2359328 | tf_op jit(solution)/shard_map/all_to_all | solution.py:199
  381.9 2.8 fusion.67
  384.8 2.4 fusion.65
  387.2 2.0 copy.112
  (259 shorter events, 71.0 us)
Async XLA Ops:
  0.0 31.6 %copy-start = (bf16[256,1024]{1,0:T(8,128)(2,1)S(1)}, bf16[256,1024]{1,0:T(8,128)(2,1)}, u32[]{:S(2)}) copy-start(bf16[256,1024]{1,0:T(8,128)(2,1)} %param.27) | copy-start | bytes 1572868
  0.0 2.1 copy-start.7
  0.0 9.7 %copy-start.3 = (bf16[64,48,256]{2,1,0:T(8,128)(2,1)S(1)}, bf16[64,48,256]{2,1,0:T(8,128)(2,1)}, u32[]{:S(2)}) copy-start(bf16[64,48,256]{2,1,0:T(8,128)(2,1)} %param.18) | copy-start | bytes 4718596
  2.1 9.4 %copy-start.26 = (bf16[256,256]{1,0:T(8,128)(2,1)S(1)}, bf16[256,256]{1,0:T(8,128)(2,1)}, u32[]{:S(2)}) copy-start(bf16[256,256]{1,0:T(8,128)(2,1)} %param.25) | copy-start | bytes 393220
  2.1 10.0 %copy-start.30 = (f32[256]{0:T(256)S(1)}, f32[256]{0:T(256)}, u32[]{:S(2)}) copy-start(f32[256]{0:T(256)} %param.21) | copy-start | bytes 3076
  2.6 10.8 %copy-start.27 = (bf16[256,256]{1,0:T(8,128)(2,1)S(1)}, bf16[256,256]{1,0:T(8,128)(2,1)}, u32[]{:S(2)}) copy-start(bf16[256,256]{1,0:T(8,128)(2,1)} %param.23) | copy-start | bytes 393220
  2.7 10.8 %copy-start.28 = (bf16[256,256]{1,0:T(8,128)(2,1)S(1)}, bf16[256,256]{1,0:T(8,128)(2,1)}, u32[]{:S(2)}) copy-start(bf16[256,256]{1,0:T(8,128)(2,1)} %param.24) | copy-start | bytes 393220
  2.8 12.1 %collective-permute-start.1 = (bf16[2,48,512]{2,0,1:T(2,128)(2,1)S(1)}, bf16[2,48,512]{2,0,1:T(2,128)(2,1)S(1)}, u32[]{:S(2)}, u32[]{:S(2)}) collective-permute-start(bf16[2,48,512]{2,0,1:T(2,128)(2,1)S(1)} %get-tuple-element.116), channel_id=1, source_target_pairs={{16,0},{32,16},{48,32},{64,48},{80,64},{96,80},{112,96},{17,1},{33... | collective-permute-start | bytes 294920 | tf_op jit(solution)/shard_map/ppermute | solution.py:22
  6.2 8.8 %collective-permute-start = (bf16[2,48,512]{2,0,1:T(2,128)(2,1)S(1)}, bf16[2,48,512]{2,0,1:T(2,128)(2,1)S(1)}, u32[]{:S(2)}, u32[]{:S(2)}) collective-permute-start(bf16[2,48,512]{2,0,1:T(2,128)(2,1)S(1)} %get-tuple-element.115), channel_id=1, source_target_pairs={{0,16},{16,32},{32,48},{48,64},{64,80},{80,96},{96,112},{1,17},{17... | collective-permute-start | bytes 294920 | tf_op jit(solution)/shard_map/ppermute | solution.py:21
  10.2 4.7 %copy-start.9 = (f32[64,48]{0,1:T(8,128)}, f32[64,48]{0,1:T(8,128)S(1)}, u32[]{:S(2)}) copy-start(f32[64,48]{0,1:T(8,128)S(1)} %broadcast_multiply_fusion.3) | copy-start | bytes 36868
  11.5 0.6 copy-start.23
  12.1 2.9 copy-start.11
  12.1 101.6 %copy-start.13 = (bf16[256,128]{1,0:T(8,128)(2,1)}, bf16[256,128]{1,0:T(8,128)(2,1)S(1)}, u32[]{:S(2)}) copy-start(bf16[256,128]{1,0:T(8,128)(2,1)S(1)} %get-tuple-element.123) | copy-start | bytes 196612
  13.5 1.6 copy-start.15
  13.5 1.6 copy-start.17
  13.5 100.1 %copy-start.19 = (bf16[256,128]{1,0:T(8,128)(2,1)}, bf16[256,128]{1,0:T(8,128)(2,1)S(1)}, u32[]{:S(2)}) copy-start(bf16[256,128]{1,0:T(8,128)(2,1)S(1)} %get-tuple-element.119) | copy-start | bytes 196612
  13.5 100.1 %copy-start.21 = (bf16[256,128]{1,0:T(8,128)(2,1)}, bf16[256,128]{1,0:T(8,128)(2,1)S(1)}, u32[]{:S(2)}) copy-start(bf16[256,128]{1,0:T(8,128)(2,1)S(1)} %get-tuple-element.141) | copy-start | bytes 196612
  13.6 7.3 %copy-start.29 = (f32[9,1024]{1,0:T(8,128)S(1)}, f32[9,1024]{1,0:T(8,128)}, u32[]{:S(2)}) copy-start(f32[9,1024]{1,0:T(8,128)} %param.28) | copy-start | bytes 110596
  15.1 6.8 %collective-permute-start.3 = (bf16[68,2,512]{2,0,1:T(8,128)(2,1)S(1)}, bf16[68,2,512]{2,0,1:T(8,128)(2,1)S(1)}, u32[]{:S(2)}, u32[]{:S(2)}) collective-permute-start(bf16[68,2,512]{2,0,1:T(8,128)(2,1)S(1)} %get-tuple-element.114), channel_id=1, source_target_pairs={{1,0},{2,1},{3,2},{4,3},{5,4},{6,5},{7,6},{8,7},{9,8},{10,9},{11,1... | collective-permute-start | bytes 417800 | tf_op jit(solution)/shard_map/ppermute | solution.py:22
  16.4 7.3 %collective-permute-start.2 = (bf16[68,2,512]{2,0,1:T(8,128)(2,1)S(1)}, bf16[68,2,512]{2,0,1:T(8,128)(2,1)S(1)}, u32[]{:S(2)}, u32[]{:S(2)}) collective-permute-start(bf16[68,2,512]{2,0,1:T(8,128)(2,1)S(1)} %get-tuple-element.113), channel_id=1, source_target_pairs={{0,1},{1,2},{2,3},{3,4},{4,5},{5,6},{6,7},{7,8},{8,9},{9,10},{10,1... | collective-permute-start | bytes 417800 | tf_op jit(solution)/shard_map/ppermute | solution.py:21
  26.7 4.9 %copy-start.34 = (f32[256]{0:T(256)S(1)}, f32[256]{0:T(256)}, u32[]{:S(2)}) copy-start(f32[256]{0:T(256)} %param.22) | copy-start | bytes 3076
  31.6 2.6 copy-start.35
  96.3 5.8 %copy-start.25 = (bf16[256,256]{1,0:T(8,128)(2,1)S(1)}, bf16[256,256]{1,0:T(8,128)(2,1)}, u32[]{:S(2)}) copy-start(bf16[256,256]{1,0:T(8,128)(2,1)} %param.26) | copy-start | bytes 393220
  101.0 1.1 copy-start.5
  107.5 5.8 %copy-start.32 = (s32[6,6]{1,0:T(8,128)S(1)}, s32[6,6]{1,0:T(8,128)}, u32[]{:S(2)}) copy-start(s32[6,6]{1,0:T(8,128)} %param.30) | copy-start | bytes 436
  107.5 6.0 %copy-start.33 = (s32[4,4]{1,0:T(4,128)S(1)}, s32[4,4]{1,0:T(4,128)}, u32[]{:S(2)}) copy-start(s32[4,4]{1,0:T(4,128)} %param.31) | copy-start | bytes 196
  107.5 43.4 %all-to-all-start.2 = ((bf16[64,8,6,512]{3,0,2,1:T(8,128)(2,1)}), bf16[64,8,6,512]{3,0,2,1:T(8,128)(2,1)}, u32[]{:S(2)}, u32[]{:S(2)}) async-start(bf16[64,8,6,512]{3,0,2,1:T(8,128)(2,1)} %bitcast.307), calls=%async_computation.2 | async-start | bytes 6291456 | tf_op jit(solution)/shard_map/all_to_all | solution.py:210
  150.9 95.3 %all-to-all-start = ((bf16[16,4,48,512]{3,2,1,0:T(8,128)(2,1)}), bf16[16,4,48,512]{3,2,1,0:T(8,128)(2,1)}, u32[]{:S(2)}, u32[]{:S(2)}) async-start(bf16[16,4,48,512]{3,2,1,0:T(8,128)(2,1)} %bitcast.306), calls=%async_computation | async-start | bytes 6291456 | tf_op jit(solution)/shard_map/all_to_all | solution.py:197
  172.7 2.2 copy-start.2
  185.4 2.2 copy-start.2
  198.2 2.2 copy-start.2
  210.9 2.2 copy-start.2
  223.7 2.2 copy-start.2
  236.4 2.2 copy-start.2
  246.2 94.3 %all-to-all-start.3 = ((bf16[512,1,6,384]{3,2,1,0:T(8,128)(2,1)}), bf16[512,1,6,384]{3,2,1,0:T(8,128)(2,1)}, u32[]{:S(2)}, u32[]{:S(2)}) async-start(bf16[512,1,6,384]{3,2,1,0:T(8,128)(2,1)} %bitcast.308), calls=%async_computation.3 | async-start | bytes 6291456 | tf_op jit(solution)/shard_map/all_to_all | solution.py:213
  263.2 7.1 %slice-start = ((s8[9437184]{0:T(1024)(128)(4,1)}), s8[4194304]{0:T(1024)(128)(4,1)S(1)}, s32[]{:S(2)}) async-start(s8[9437184]{0:T(1024)(128)(4,1)} %bitcast.280), calls=%async_computation.4 | async-start | bytes 8388608 | tf_op jit(solution)/shard_map/while
  263.2 7.1 %slice-start.1 = ((s8[9437184]{0:T(1024)(128)(4,1)}), s8[4194304]{0:T(1024)(128)(4,1)S(1)}, s32[]{:S(2)}) async-start(s8[9437184]{0:T(1024)(128)(4,1)} %bitcast.280), calls=%async_computation.5 | async-start | bytes 8388608 | tf_op jit(solution)/shard_map/while
  267.8 2.4 slice-start.2
  283.1 7.1 %slice-start = ((s8[9437184]{0:T(1024)(128)(4,1)}), s8[4194304]{0:T(1024)(128)(4,1)S(1)}, s32[]{:S(2)}) async-start(s8[9437184]{0:T(1024)(128)(4,1)} %bitcast.280), calls=%async_computation.4 | async-start | bytes 8388608 | tf_op jit(solution)/shard_map/while
  283.1 7.1 %slice-start.1 = ((s8[9437184]{0:T(1024)(128)(4,1)}), s8[4194304]{0:T(1024)(128)(4,1)S(1)}, s32[]{:S(2)}) async-start(s8[9437184]{0:T(1024)(128)(4,1)} %bitcast.280), calls=%async_computation.5 | async-start | bytes 8388608 | tf_op jit(solution)/shard_map/while
  287.7 2.5 slice-start.2
  303.0 7.1 %slice-start = ((s8[9437184]{0:T(1024)(128)(4,1)}), s8[4194304]{0:T(1024)(128)(4,1)S(1)}, s32[]{:S(2)}) async-start(s8[9437184]{0:T(1024)(128)(4,1)} %bitcast.280), calls=%async_computation.4 | async-start | bytes 8388608 | tf_op jit(solution)/shard_map/while
  303.0 7.1 %slice-start.1 = ((s8[9437184]{0:T(1024)(128)(4,1)}), s8[4194304]{0:T(1024)(128)(4,1)S(1)}, s32[]{:S(2)}) async-start(s8[9437184]{0:T(1024)(128)(4,1)} %bitcast.280), calls=%async_computation.5 | async-start | bytes 8388608 | tf_op jit(solution)/shard_map/while
  307.6 2.5 slice-start.2
  322.8 7.1 %slice-start = ((s8[9437184]{0:T(1024)(128)(4,1)}), s8[4194304]{0:T(1024)(128)(4,1)S(1)}, s32[]{:S(2)}) async-start(s8[9437184]{0:T(1024)(128)(4,1)} %bitcast.280), calls=%async_computation.4 | async-start | bytes 8388608 | tf_op jit(solution)/shard_map/while
  322.8 7.1 %slice-start.1 = ((s8[9437184]{0:T(1024)(128)(4,1)}), s8[4194304]{0:T(1024)(128)(4,1)S(1)}, s32[]{:S(2)}) async-start(s8[9437184]{0:T(1024)(128)(4,1)} %bitcast.280), calls=%async_computation.5 | async-start | bytes 8388608 | tf_op jit(solution)/shard_map/while
  327.5 2.5 slice-start.2
  340.5 39.0 %all-to-all-start.1 = ((bf16[1,4,768,384]{3,1,0,2:T(4,128)(2,1)}), bf16[1,4,768,384]{3,1,0,2:T(4,128)(2,1)S(1)}, u32[]{:S(2)}, u32[]{:S(2)}) async-start(bf16[1,4,768,384]{3,1,0,2:T(4,128)(2,1)} %bitcast.19), calls=%async_computation.1 | async-start | bytes 4718592 | tf_op jit(solution)/shard_map/all_to_all | solution.py:199
  351.4 28.8 %copy-start.14 = (bf16[256,128]{1,0:T(8,128)(2,1)S(1)}, bf16[256,128]{1,0:T(8,128)(2,1)}, u32[]{:S(2)}) copy-start(bf16[256,128]{1,0:T(8,128)(2,1)} %copy-done.13) | copy-start | bytes 196612
  351.4 28.8 %copy-start.20 = (bf16[256,128]{1,0:T(8,128)(2,1)S(1)}, bf16[256,128]{1,0:T(8,128)(2,1)}, u32[]{:S(2)}) copy-start(bf16[256,128]{1,0:T(8,128)(2,1)} %copy-done.19) | copy-start | bytes 196612
  351.4 28.8 %copy-start.22 = (bf16[256,128]{1,0:T(8,128)(2,1)S(1)}, bf16[256,128]{1,0:T(8,128)(2,1)}, u32[]{:S(2)}) copy-start(bf16[256,128]{1,0:T(8,128)(2,1)} %copy-done.21) | copy-start | bytes 196612
  379.7 1.5 copy-start.4
  379.7 2.1 copy-start.8
  379.8 2.1 copy-start.10
  379.8 2.1 copy-start.12
  379.8 2.1 copy-start.16
  379.8 2.1 copy-start.18
  379.8 2.1 copy-start.24
  379.8 2.1 copy-start.31
  381.9 2.9 copy-start.6
  384.8 4.5 %copy-start.1 = (bf16[256,1024]{1,0:T(8,128)(2,1)S(1)}, bf16[256,1024]{1,0:T(8,128)(2,1)}, u32[]{:S(2)}) copy-start(bf16[256,1024]{1,0:T(8,128)(2,1)} %param.27) | copy-start | bytes 1572868
where the time goes:
time: 396 us; the launch traced here: 389 us
  matrix products  162 us (41%)
  waiting for transfers between devices  64.5 us (16%)
  local copies, waits for them, and re-layouts  63.5 us (16%)
  other arithmetic  56.4 us (14%)
  starting transfers between devices  40.9 us (10%)
    sub x10, matrix products, line_grads(): exp_terms = jnp.exp(scores - row_top)  45.4 us
    convert_element_type x10, other arithmetic, line_grads(): prob_low = prob_rows.astype(jnp.bfloat16)  35.2 us
    all_to_all x1, waiting for transfers between devices, per_device(): lax.all_to_all(col_payload, 'gy', split_axis=1, concat_axis=0, tiled=True)  33.7 us
    dot_general x1, matrix products, mlp_band(): grad_norm = jnp.dot(grad_hidden, w_up.T, preferred_element_type=jnp.float32)  33.7 us
    dot_general x1, matrix products, mlp_band(): jnp.dot(grad_pad[1:-1, 1:-1], w_down.T, preferred_element_type=jnp.float32)  28.5 us
    all_to_all x1, waiting for transfers between devices, per_device(): lax.all_to_all(row_result, 'gx', split_axis=2, concat_axis=0, tiled=True)  28 us
    dot_general x10, matrix products, line_grads(): jnp.einsum('qhd,khd->hqk', grad_heads, value_heads, preferred_element_typ...  11.5 us
    dot_general x10, matrix products, line_grads(): jnp.einsum('hqk,qhd->khd', grad_scores, queries, preferred_element_type=j...  10.1 us
  transfers between devices with their start and end apart: 8, of which 4 were waited for; matrix products, arithmetic and copies ran while one was open for 46% of the time, Pallas kernels for 0%

commit v1 on v0

v1 whole, which is shorter than its diff:
```python
import functools
import jax
import jax.numpy as jnp
from jax import lax
from jax.experimental import pallas as pl
from jax.experimental.pallas import tpu as pltpu
from jax.sharding import PartitionSpec as P

HEADS = 8
BLK = 128
EPSILON = 1e-05
LOG2E = 1.4426950408889634
LN2 = 0.6931471805599453
F32 = jnp.float32
BF16 = jnp.bfloat16


def attn_kernel(nl, nk, mask_ref, x_ref, g_ref, gain_ref, w_ref, wt_ref, out_ref,
                q_s, k_s, v_s, g_s, kt_s, qmt_s, qm_s, gmt_s, gm_s, e_s, dp_s, st_s, dq_s, dk_s, dv_s):
    heads = HEADS // 2
    hw = 128
    hd = hw // heads
    length = nk * BLK
    factor = hd ** -0.5
    gain = gain_ref[...]
    wide = heads * BLK

    qmt_s[...] = jnp.zeros_like(qmt_s)
    gmt_s[...] = jnp.zeros_like(gmt_s)
    dk_s[...] = jnp.zeros_like(dk_s)
    dv_s[...] = jnp.zeros_like(dv_s)

    def prepare(line, carry):
        xv = x_ref[:, line].reshape(length, 2 * hw).astype(F32)
        mean = jnp.mean(xv, axis=-1, keepdims=True)
        center = xv - mean
        inv = lax.rsqrt(jnp.mean(center * center, axis=-1, keepdims=True) + EPSILON)
        normed = (center * inv * gain).astype(BF16)
        qkv = jnp.dot(normed, w_ref[...], preferred_element_type=F32)
        kf = qkv[:, hw:2 * hw]
        q_s[line] = (qkv[:, :hw] * (factor * LOG2E)).astype(BF16)
        k_s[line] = kf.astype(BF16)
        v_s[line] = qkv[:, 2 * hw:].astype(BF16)
        kt_s[line] = kf.T.astype(BF16)
        g_s[line] = g_ref[:, line].reshape(length, hw)
        return carry

    lax.fori_loop(0, nl, prepare, 0)
    lane = lax.broadcasted_iota(jnp.int32, (BLK, hw), 1)

    def query_block(qb, carry):
        qs = pl.ds(pl.multiple_of(qb * BLK, BLK), BLK)
        for line in range(nl):
            for src, dt, dm in ((q_s, qmt_s, qm_s), (g_s, gmt_s, gm_s)):
                blk = src[line, qs, :]
                blk_f = blk.astype(F32)
                blk_t = blk_f.T.astype(BF16)
                for h in range(heads):
                    dt[line, h * hd:(h + 1) * hd, h * BLK:(h + 1) * BLK] = blk_t[h * hd:(h + 1) * hd]
                    inside = (lane >= h * hd) & (lane < (h + 1) * hd)
                    dm[line, h * BLK:(h + 1) * BLK, :] = jnp.where(inside, blk_f, 0.0).astype(BF16)

        def phase_a(kb, c):
            allowed = mask_ref[qb, kb] > 0
            ks = pl.ds(pl.multiple_of(kb * BLK, BLK), BLK)

            @pl.when(jnp.logical_not(allowed))
            def _():
                for line in range(nl):
                    st_s[kb, line] = jnp.concatenate(
                        [jnp.full((1, wide), -jnp.inf, F32), jnp.zeros((7, wide), F32)], axis=0)

            @pl.when(allowed)
            def _():
                for line in range(nl):
                    s = jnp.dot(k_s[line, ks, :], qmt_s[line], preferred_element_type=F32)
                    dp = jnp.dot(v_s[line, ks, :], gmt_s[line], preferred_element_type=F32)
                    top = jnp.max(s, axis=0, keepdims=True)
                    e = jnp.exp2(s - top)
                    e_s[kb, line] = e.astype(BF16)
                    dp_s[kb, line] = dp
                    st_s[kb, line, 0:1] = top
                    st_s[kb, line, 1:2] = jnp.sum(e, axis=0, keepdims=True)
                    st_s[kb, line, 2:3] = jnp.sum(e * dp, axis=0, keepdims=True)
            return c

        lax.fori_loop(0, nk, phase_a, 0)

        for line in range(nl):
            top = st_s[0, line, 0:1]
            for kb in range(1, nk):
                top = jnp.maximum(top, st_s[kb, line, 0:1])
            total = jnp.zeros((1, wide), F32)
            moment = jnp.zeros((1, wide), F32)
            weights = []
            for kb in range(nk):
                wk = jnp.exp2(st_s[kb, line, 0:1] - top)
                weights.append(wk)
                total = total + wk * st_s[kb, line, 1:2]
                moment = moment + wk * st_s[kb, line, 2:3]
            inv = 1.0 / total
            delta = moment * inv
            for kb in range(nk):
                st_s[kb, line, 3:4] = weights[kb] * inv
                st_s[kb, line, 4:5] = delta
            dq_s[line] = jnp.zeros((hd, wide), F32)

        def phase_b(kb, c):
            ks = pl.ds(pl.multiple_of(kb * BLK, BLK), BLK)

            @pl.when(mask_ref[qb, kb] > 0)
            def _():
                for line in range(nl):
                    p = e_s[kb, line].astype(F32) * st_s[kb, line, 3:4]
                    ds = (p * (dp_s[kb, line] - st_s[kb, line, 4:5])).astype(BF16)
                    dv_s[line, ks, :] += jnp.dot(p.astype(BF16), gm_s[line], preferred_element_type=F32)
                    dk_s[line, ks, :] += jnp.dot(ds, qm_s[line], preferred_element_type=F32)
                    for h in range(heads):
                        dq_s[line, :, h * BLK:(h + 1) * BLK] += jnp.dot(
                            kt_s[line, h * hd:(h + 1) * hd, ks], ds[:, h * BLK:(h + 1) * BLK],
                            preferred_element_type=F32)
            return c

        lax.fori_loop(0, nk, phase_b, 0)
        for line in range(nl):
            full = jnp.concatenate([dq_s[line, :, h * BLK:(h + 1) * BLK] for h in range(heads)], axis=0)
            q_s[line, qs, :] = (full.T * factor).astype(BF16)
        return carry

    lax.fori_loop(0, nk, query_block, 0)

    def finish(line, carry):
        grads = jnp.concatenate(
            [q_s[line], (dk_s[line] * LN2).astype(BF16), dv_s[line].astype(BF16)], axis=1)
        res = jnp.dot(grads, wt_ref[...], preferred_element_type=F32).astype(BF16)
        out_ref[:, line] = res.reshape(out_ref.shape[0], out_ref.shape[2], out_ref.shape[3])
        return carry

    lax.fori_loop(0, nl, finish, 0)


def attention(x, g, gain, w, mask):
    srcs, nl, span, width = x.shape
    length = srcs * span
    nk = length // BLK
    hw = width // 2
    heads = HEADS // 2
    wide = heads * BLK
    vm = pl.BlockSpec(memory_space=pltpu.VMEM)
    return pl.pallas_call(
        functools.partial(attn_kernel, nl, nk),
        out_shape=jax.ShapeDtypeStruct(x.shape, BF16),
        in_specs=[pl.BlockSpec(memory_space=pltpu.SMEM), vm, vm, vm, vm, vm],
        out_specs=vm,
        scratch_shapes=[
            pltpu.VMEM((nl, length, hw), BF16),
            pltpu.VMEM((nl, length, hw), BF16),
            pltpu.VMEM((nl, length, hw), BF16),
            pltpu.VMEM((nl, length, hw), BF16),
            pltpu.VMEM((nl, hw, length), BF16),
            pltpu.VMEM((nl, hw, wide), BF16),
            pltpu.VMEM((nl, wide, hw), BF16),
            pltpu.VMEM((nl, hw, wide), BF16),
            pltpu.VMEM((nl, wide, hw), BF16),
            pltpu.VMEM((nk, nl, BLK, wide), BF16),
            pltpu.VMEM((nk, nl, BLK, wide), F32),
            pltpu.VMEM((nk, nl, 8, wide), F32),
            pltpu.VMEM((nl, hw // heads, wide), F32),
            pltpu.VMEM((nl, length, hw), F32),
            pltpu.VMEM((nl, length, hw), F32),
        ],
        compiler_params=pltpu.CompilerParams(vmem_limit_bytes=48 * 1024 * 1024),
        name="axial_attention",
    )(mask, x, g, gain.reshape(1, -1), w, w.T)


GELU_C = 0.7978845608028654


def with_halo(shard, sides, width):
    for axis, dim in sides:
        count, length = (lax.axis_size(axis), shard.shape[dim])
        up = [(i, (i + 1) % count) for i in range(count - 1)]
        down = [(j, i) for i, j in up]
        last = lax.slice_in_dim(shard, length - width, length, axis=dim)
        initial = lax.slice_in_dim(shard, 0, width, axis=dim)
        before = lax.ppermute(last, axis, up)
        after = lax.ppermute(initial, axis, down)
        shard = jnp.concatenate([before, shard, after], axis=dim)
    return shard


def layer_norm(values, gain_vec):
    values = values.astype(jnp.float32)
    center = values - jnp.mean(values, axis=-1, keepdims=True)
    inv_std = lax.rsqrt(jnp.mean(center * center, axis=-1, keepdims=True) + EPSILON)
    normed = center * inv_std
    return (normed * gain_vec, normed, inv_std)


def norm_backward(grad_norm, gain_vec, normed, inv_std):
    grad_hat = grad_norm * gain_vec
    return inv_std * (
        grad_hat
        - jnp.mean(grad_hat, axis=-1, keepdims=True)
        - normed * jnp.mean(grad_hat * normed, axis=-1, keepdims=True)
    )


def gelu_slope(value):
    inside_term = GELU_C * (value + 0.044715 * value * value * value)
    tanh_val = jnp.tanh(inside_term)
    return 0.5 * (1.0 + tanh_val) + 0.5 * value * (1.0 - tanh_val * tanh_val) * GELU_C * (
        1.0 + 3.0 * 0.044715 * value * value
    )


def mlp_band(mid_pad, grad_pad, mlp_gain, w_up, conv_kernel, w_down):
    rows_in = mid_pad.shape[0] - 4
    cols_in = mid_pad.shape[1] - 4
    mid_norm, mid_hat, mid_inv = layer_norm(mid_pad, mlp_gain)
    hidden = jnp.dot(
        mid_norm.astype(jnp.bfloat16), w_up, preferred_element_type=jnp.float32
    ).astype(jnp.bfloat16)
    pre_act = jnp.zeros((rows_in + 2, cols_in + 2, hidden.shape[-1]), jnp.float32)
    for row_shift in range(3):
        for col_shift in range(3):
            pre_act = (
                pre_act
                + conv_kernel[3 * row_shift + col_shift]
                * hidden[row_shift : row_shift + rows_in + 2, col_shift : col_shift + cols_in + 2]
            )
    grad_act = jnp.dot(grad_pad[1:-1, 1:-1], w_down.T, preferred_element_type=jnp.float32)
    grad_pre = (grad_act * gelu_slope(pre_act)).astype(jnp.bfloat16)
    grad_hidden = jnp.zeros((rows_in, cols_in, hidden.shape[-1]), jnp.float32)
    for row_shift in range(3):
        for col_shift in range(3):
            grad_hidden = (
                grad_hidden
                + conv_kernel[3 * row_shift + col_shift]
                * grad_pre[
                    2 - row_shift : 2 - row_shift + rows_in, 2 - col_shift : 2 - col_shift + cols_in
                ]
            )
    grad_hidden = grad_hidden.astype(jnp.bfloat16)
    grad_norm = jnp.dot(grad_hidden, w_up.T, preferred_element_type=jnp.float32)
    norm_grad = norm_backward(grad_norm, mlp_gain, mid_hat[2:-2, 2:-2], mid_inv[2:-2, 2:-2])
    return (grad_pad[2:-2, 2:-2].astype(jnp.float32) + norm_grad).astype(jnp.bfloat16)


def to_lines(blocks, axis):
    return lax.all_to_all(blocks, axis, split_axis=0, concat_axis=0, tiled=True)


def cut_cols(tile, count):
    rows, cols, width = tile.shape
    return jnp.transpose(tile.reshape(rows, count, cols // count, width), (1, 2, 0, 3))


def per_device(
    tokens_in,
    saved_mid,
    grad_out,
    attn_gain,
    mlp_gain,
    w_query,
    w_key,
    w_value,
    w_out,
    w_up,
    conv_kernel,
    w_down,
    row_mask,
    col_mask,
):
    model_width = tokens_in.shape[-1]
    half_width = model_width // 2
    tile_rows = tokens_in.shape[0]
    tile_cols = tokens_in.shape[1]
    count_gx = lax.axis_size("gx")
    count_gy = lax.axis_size("gy")
    joined = jnp.concatenate([saved_mid, grad_out], axis=-1)
    padded = with_halo(joined, (("gy", 0), ("gx", 1)), 2)
    grad_mid = mlp_band(
        padded[..., :model_width], padded[..., model_width:], mlp_gain, w_up, conv_kernel, w_down
    )
    grad_attn = jnp.dot(grad_mid, w_out.T, preferred_element_type=jnp.float32).astype(jnp.bfloat16)
    in_norm, in_hat, in_inv = layer_norm(tokens_in, attn_gain)
    w_row = jnp.concatenate(
        [w_query[:, :half_width], w_key[:, :half_width], w_value[:, :half_width]], axis=1
    )
    w_col = jnp.concatenate(
        [w_query[:, half_width:], w_key[:, half_width:], w_value[:, half_width:]], axis=1
    )
    row_shape = (count_gx, tile_rows // count_gx, tile_cols)
    row_tokens = to_lines(tokens_in.reshape(*row_shape, model_width), "gx")
    row_grads = to_lines(grad_attn[..., :half_width].reshape(*row_shape, half_width), "gx")
    col_tokens = to_lines(cut_cols(tokens_in, count_gy), "gy")
    col_grads = to_lines(cut_cols(grad_attn[..., half_width:], count_gy), "gy")
    row_out = attention(row_tokens, row_grads, attn_gain, w_row, row_mask)
    grad_row_in = to_lines(row_out, "gx").reshape(tile_rows, tile_cols, model_width)
    col_out = attention(col_tokens, col_grads, attn_gain, w_col, col_mask)
    col_back = to_lines(col_out, "gy")
    grad_col_in = jnp.transpose(col_back, (2, 0, 1, 3)).reshape(tile_rows, tile_cols, model_width)
    norm_grad = norm_backward(
        grad_row_in.astype(jnp.float32) + grad_col_in.astype(jnp.float32), attn_gain, in_hat, in_inv
    )
    return (grad_mid.astype(jnp.float32) + norm_grad).astype(jnp.bfloat16)


def solution(mesh):
    in_specs = (
        P("gy", "gx", None),
        P("gy", "gx", None),
        P("gy", "gx", None),
        P(),
        P(),
        P(),
        P(),
        P(),
        P(),
        P(),
        P(),
        P(),
        P(),
        P(),
    )
    out_specs = P("gy", "gx", None)
    return jax.shard_map(
        per_device, mesh=mesh, in_specs=in_specs, out_specs=out_specs, check_vma=False
    )
```

time: 396 us -> 303 us (0.77); the launches traced: 389 us -> 301 us
  matrix products: 162 us -> 66 us
  Pallas kernels: 0 us -> 63.1 us
  blocking collectives: 0 us -> 45.8 us
  local copies, waits for them, and re-layouts: 63.5 us -> 24.8 us
  waiting for transfers between devices: 64.5 us -> 28.6 us
  other arithmetic: 56.4 us -> 33.9 us
    pallas_call x0 -> x2, Pallas kernels: none -> 63.1 us  [attention(): pl.pallas_call(functools.partial(attn_kernel, nl, nk), out_shape=jax.Shap...]
    dot_general x54 -> x0, matrix products: 51.1 us -> none  [the longest x10 11.5 us: line_grads(): jnp.einsum('qhd,khd->hqk', grad_heads, value_heads, preferred_element_typ...]
    all_to_all x0 -> x2, blocking collectives: none -> 45.8 us  [to_lines(): return lax.all_to_all(blocks, axis, split_axis=0, concat_axis=0, tiled=True)]
    sub x10 -> x0, matrix products: 45.4 us -> none  [line_grads(): exp_terms = jnp.exp(scores - row_top)]
    all_to_all x4, waiting for transfers between devices: 61.7 us -> 24.5 us  [to_lines(): return lax.all_to_all(blocks, axis, split_axis=0, concat_axis=0, tiled=True)]
    convert_element_type x11 -> x2, other arithmetic: 36.5 us -> 5.31 us  [the longest x1 3.5 us: per_device(): grad_col_in.astype(jnp.float32)]
    while x38 -> x0, local copies, waits for them, and re-layouts: 16.3 us -> none
    dynamic_slice x20 -> x0, local copies, waits for them, and re-layouts: 13.6 us -> none  [the longest x12 7.73 us: per_device(): col_result = jnp.swapaxes(lax.map(col_single, lines), 0, 1)[:, None]]
  transfers between devices with their start and end apart: 8 -> 8, of which waited for: 4 -> 6; matrix products, arithmetic and copies ran while one was open for 46% -> 7% of each run, Pallas kernels for 0% -> 21%
where the time goes in v1:
time: 303 us; the launch traced here: 301 us
  matrix products  66 us (22%)
  Pallas kernels  63.1 us (21%)
  blocking collectives  45.8 us (15%)
  starting transfers between devices  38 us (13%)
  other arithmetic  33.9 us (11%)
  waiting for transfers between devices  28.6 us (9%)
  local copies, waits for them, and re-layouts  24.8 us (8%)
    pallas_call x2, Pallas kernels, attention(): pl.pallas_call(functools.partial(attn_kernel, nl, nk), out_shape=jax.Shap...  63.1 us
    all_to_all x2, blocking collectives, to_lines(): return lax.all_to_all(blocks, axis, split_axis=0, concat_axis=0, tiled=True)  45.8 us
    dot_general x1, matrix products, mlp_band(): grad_norm = jnp.dot(grad_hidden, w_up.T, preferred_element_type=jnp.float32)  33.9 us
    dot_general x1, matrix products, mlp_band(): jnp.dot(grad_pad[1:-1, 1:-1], w_down.T, preferred_element_type=jnp.float32)  28.4 us
    all_to_all x4, starting transfers between devices, to_lines(): return lax.all_to_all(blocks, axis, split_axis=0, concat_axis=0, tiled=True)  25.8 us
    all_to_all x4, waiting for transfers between devices, to_lines(): return lax.all_to_all(blocks, axis, split_axis=0, concat_axis=0, tiled=True)  24.5 us
    unnamed x48, local copies, waits for them, and re-layouts  11.8 us
    ppermute x2, starting transfers between devices, with_halo(): before = lax.ppermute(last, axis, up)  7.52 us
  transfers between devices with their start and end apart: 8, of which 6 were waited for; matrix products, arithmetic and copies ran while one was open for 7% of the time, Pallas kernels for 21%

profile of v1, /device:TPU:1, one launch (start us, length us, event | category | flops | bytes accessed | tf_op | source)
XLA Modules:
  0.0 300.7 jit_solution(13367831294192265920)
XLA Ops:
  0.0 2.0 copy_dynamic-update-slice_fusion
  2.1 0.0 copy-start.17
  2.1 0.5 copy_dynamic-update-slice_fusion.1
  2.6 0.2 fusion.43
  2.8 3.3 %collective-permute-start.1 = (bf16[2,48,512]{2,0,1:T(2,128)(2,1)S(1)}, bf16[2,48,512]{2,0,1:T(2,128)(2,1)S(1)}, u32[]{:S(2)}, u32[]{:S(2)}) collective-permute-start(bf16[2,48,512]{2,0,1:T(2,128)(2,1)S(1)} %get-tuple-element.10), channel_id=1, source_target_pairs={{16,0},{32,16},{48,32},{64,48},{80,64},{96,80},{112,96},{17,1},{33... | collective-permute-start | bytes 294920 | tf_op jit(solution)/shard_map/ppermute | solution.py:188
  6.1 3.5 %collective-permute-start = (bf16[2,48,512]{2,0,1:T(2,128)(2,1)S(1)}, bf16[2,48,512]{2,0,1:T(2,128)(2,1)S(1)}, u32[]{:S(2)}, u32[]{:S(2)}) collective-permute-start(bf16[2,48,512]{2,0,1:T(2,128)(2,1)S(1)} %get-tuple-element.9), channel_id=1, source_target_pairs={{0,16},{16,32},{32,48},{48,64},{64,80},{80,96},{96,112},{1,17},{17... | collective-permute-start | bytes 294920 | tf_op jit(solution)/shard_map/ppermute | solution.py:187
  9.6 0.4 collective-permute-done.1
  10.0 1.3 collective-permute-done
  11.2 0.1 pad_maximum_fusion.5
  11.3 1.3 collective-permute-start.3
  12.6 4.0 %collective-permute-start.2 = (bf16[68,2,512]{2,0,1:T(8,128)(2,1)S(1)}, bf16[68,2,512]{2,0,1:T(8,128)(2,1)S(1)}, u32[]{:S(2)}, u32[]{:S(2)}) collective-permute-start(bf16[68,2,512]{2,0,1:T(8,128)(2,1)S(1)} %get-tuple-element.7), channel_id=1, source_target_pairs={{0,1},{1,2},{2,3},{3,4},{4,5},{5,6},{6,7},{7,8},{8,9},{9,10},{10,1... | collective-permute-start | bytes 417800 | tf_op jit(solution)/shard_map/ppermute | solution.py:187
  16.7 0.8 collective-permute-done.3
  17.5 1.8 collective-permute-done.2
  19.2 2.0 pad_maximum_fusion
  21.3 0.9 convert_reduce_fusion
  22.2 0.0 copy-start.18
  22.2 1.7 fusion.10
  24.0 3.1 %fusion.8 = f32[68,52,256]{2,0,1:T(8,128)} fusion(f32[68,52]{0,1:T(8,128)S(1)} %get-tuple-element.33, f32[68,52]{0,1:T(8,128)S(1)} %broadcast_multiply_fusion.1, bf16[68,52,512]{2,0,1:T(8,128)(2,1)S(1)} %pad_maximum_fusion), kind=kLoop, calls=%fused_computation.14 | loop fusion | flops 2715648 | bytes 5459584 | tf_op jit(solution)/shard_map/mul | solution.py:197
  27.1 0.1 slice_bitcast_fusion
  27.2 2.5 convolution_convert_fusion
  29.7 28.4 %fusion.6 = bf16[66,50,1024]{2,0,1:T(8,128)(2,1)} fusion(bf16[68,52,1024]{2,0,1:T(8,128)(2,1)S(1)} %convolution_convert_fusion, f32[1024]{0:T(1024)S(1)} %bitcast.72, f32[1024]{0:T(1024)S(1)} %bitcast.74, f32[1024]{0:T(1024)S(1)} %bitcast.60, f32[1024]{0:T(1024)S(1)} %bitcast.62, f32[1024]{0:T(1024)S(1)} %bitcast.64, f32[1024]{0:T(1024)S(1)} %bitcast.66, ...), kind=kOutput, calls=%fused_computation.8 | convolution fusion | flops 1890662400 | bytes 71766016 | tf_op jit(solution)/shard_map/dot_general | solution.py:233
  58.2 33.9 %multiply_reduce_fusion.1 = (f32[64,48]{0,1:T(8,128)S(1)}, f32[64,48]{0,1:T(8,128)S(1)}, f32[64,48,256]{2,0,1:T(8,128)}) fusion(f32[256]{0:T(256)S(1)} %copy-done.18, f32[68,52,256]{2,0,1:T(8,128)} %fusion.8, bf16[256,1024]{1,0:T(8,128)(2,1)S(1)} %copy-done, bf16[66,50,1024]{2,0,1:T(8,128)(2,1)} %fusion.6, f32[1024]{0:T(1024)S(1)} %bitcast.73, ...), kind=kOutput, calls=%fused_computation.37 | convolution fusion | flops 1698686976 | bytes 63501312 | tf_op jit(solution)/shard_map/dot_general | solution.py:246
  92.1 4.6 %add_convert_fusion.2 = bf16[64,48,256]{2,0,1:T(8,128)(2,1)S(1)} fusion(f32[68,52,256]{2,0,1:T(8,128)} %fusion.8, f32[64,48,256]{2,0,1:T(8,128)} %get-tuple-element.34, f32[64,48]{0,1:T(8,128)S(1)} %get-tuple-element.35, f32[64,48]{0,1:T(8,128)S(1)} %get-tuple-element.36, f32[256]{0:T(256)S(1)} %copy-done.18, f32[64,48]{0,1:T(8,128)S(1)} %slice_bitcast_fusion, ...), kind=kLoop, calls=%fused_computation.35 | loop fusion | flops 6291456 | bytes 9475072 | tf_op jit(solution)/shard_map/convert_element_type | solution.py:248
  96.7 1.1 copy-done.11
  97.8 1.2 convolution_convert_fusion.1
  99.0 1.1 fusion.44
  100.2 0.2 copy.47
  100.4 18.9 %all_to_all.30.g_ref = bf16[8,6,64,128]{3,2,1,0:T(8,128)(2,1)} all-to-all(bf16[8,6,64,128]{3,2,1,0:T(8,128)(2,1)S(1)} %bitcast.56), channel_id=1, replica_groups=mesh['gy'=8,'gx'=16] {'gy'}, dimensions={0} | all-to-all | bytes 1572864 | tf_op jit(solution)/shard_map/all_to_all | solution.py:252
  119.3 9.7 %all-to-all-start.1 = ((bf16[16,4,48,128]{3,2,1,0:T(8,128)(2,1)}), bf16[16,4,48,128]{3,2,1,0:T(8,128)(2,1)S(1)}, u32[]{:S(2)}, u32[]{:S(2)}) async-start(bf16[16,4,48,128]{3,2,1,0:T(8,128)(2,1)} %bitcast.15), calls=%async_computation.1 | async-start | bytes 1572864 | tf_op jit(solution)/shard_map/all_to_all | solution.py:252
  129.0 1.7 copy.40
  130.7 11.0 %all-to-all-done.1.g_ref = bf16[16,4,48,128]{3,2,1,0:T(8,128)(2,1)S(1)} async-done(((bf16[16,4,48,128]{3,2,1,0:T(8,128)(2,1)}), bf16[16,4,48,128]{3,2,1,0:T(8,128)(2,1)S(1)}, u32[]{:S(2)}, u32[]{:S(2)}) %all-to-all-start.1) | async-done | bytes 786464 | tf_op jit(solution)/shard_map/all_to_all | solution.py:252
  141.8 0.9 copy-done.2
  142.7 26.9 %all_to_all.31.x_ref = bf16[8,6,64,256]{3,2,1,0:T(8,128)(2,1)S(1)} all-to-all(bf16[8,6,64,256]{3,2,1,0:T(8,128)(2,1)} %bitcast.55), channel_id=1, replica_groups=mesh['gy'=8,'gx'=16] {'gy'}, dimensions={0} | all-to-all | bytes 3145728 | tf_op jit(solution)/shard_map/all_to_all | solution.py:252
  169.5 3.9 %all-to-all-start = ((bf16[16,4,48,256]{3,2,1,0:T(8,128)(2,1)}), bf16[16,4,48,256]{3,2,1,0:T(8,128)(2,1)S(1)}, u32[]{:S(2)}, u32[]{:S(2)}) async-start(bf16[16,4,48,256]{3,2,1,0:T(8,128)(2,1)} %bitcast.54), calls=%async_computation | async-start | bytes 3145728 | tf_op jit(solution)/shard_map/all_to_all | solution.py:252
  173.5 0.6 fusion.47
  174.1 0.1 copy.63
  174.2 0.6 fusion.46
  174.9 0.1 copy.62
  175.0 1.5 fusion.45
  176.5 0.1 copy.61
  176.6 0.7 fusion.41
  177.3 1.1 copy.51.w_ref
  178.4 1.1 copy-done.4
  179.6 28.4 %axial_attention.3 = bf16[8,6,64,256]{3,2,1,0:T(8,128)(2,1)} custom-call(s32[4,4]{1,0:T(4,128)S(1)} %copy-done.7, bf16[8,6,64,256]{3,2,1,0:T(8,128)(2,1)S(1)} %all_to_all.31.x_ref, bf16[8,6,64,128]{3,2,1,0:T(8,128)(2,1)S(1)} %copy-done.4, f32[1,256]{1,0:T(1,128)S(1)} %bitcast.52, bf16[256,384]{1,0:T(8,128)(2,1)S(1)} %copy.51.w_ref, ...), custom_call_target="tpu_custom_call" | custom-call | tf_op jit(solution)/shard_map/axial_attention/pallas_call | solution.py:150
  208.0 5.3 %all-to-all-start.5 = ((bf16[8,6,64,256]{3,2,1,0:T(8,128)(2,1)}), bf16[8,6,64,256]{3,2,1,0:T(8,128)(2,1)}, u32[]{:S(2)}, u32[]{:S(2)}) async-start(bf16[8,6,64,256]{3,2,1,0:T(8,128)(2,1)} %axial_attention.3), calls=%async_computation.5 | async-start | bytes 3145728 | tf_op jit(solution)/shard_map/all_to_all | solution.py:252
  213.3 0.9 copy.60
  214.3 0.9 copy.59
  215.2 0.9 copy.58
  216.2 0.2 copy.45.w_ref
  216.4 34.6 %axial_attention.2 = bf16[16,4,48,256]{3,2,1,0:T(8,128)(2,1)} custom-call(s32[6,6]{1,0:T(8,128)S(1)} %copy-done.6, bf16[16,4,48,256]{3,2,1,0:T(8,128)(2,1)S(1)} %all-to-all-done.x_ref, bf16[16,4,48,128]{3,2,1,0:T(8,128)(2,1)S(1)} %copy-done.3, f32[1,256]{1,0:T(1,128)S(1)} %bitcast.53, bf16[256,384]{1,0:T(8,128)(2,1)S(1)} %copy.45.w_ref, ...), custom_call_target="tpu_custom_call" | custom-call | tf_op jit(solution)/shard_map/axial_attention/pallas_call | solution.py:150
  251.0 6.8 %all-to-all-start.2 = ((bf16[16,4,48,256]{3,2,1,0:T(8,128)(2,1)}), bf16[16,4,48,256]{3,2,1,0:T(8,128)(2,1)}, u32[]{:S(2)}, u32[]{:S(2)}) async-start(bf16[16,4,48,256]{3,2,1,0:T(8,128)(2,1)} %axial_attention.2), calls=%async_computation.2 | async-start | bytes 3145728 | tf_op jit(solution)/shard_map/all_to_all | solution.py:252
  257.9 0.5 convert_reduce_fusion.1
  258.4 1.2 fusion.20
  259.6 3.5 %convert_bitcast_fusion = f32[64,8,6,256]{3,0,2,1:T(8,128)} fusion(bf16[8,6,64,256]{3,2,1,0:T(8,128)(2,1)} %all-to-all-done.5), kind=kLoop, calls=%fused_computation.52 | loop fusion | flops 786432 | bytes 4718592 | tf_op jit(solution)/shard_map/convert_element_type | solution.py:306
  263.1 4.8 %reshape.102 = f32[16,4,48,256]{3,1,0,2:T(4,128)} reshape(f32[64,8,6,256]{3,0,2,1:T(8,128)} %convert_bitcast_fusion) | data formatting | bytes 6291456 | tf_op jit(solution)/shard_map/convert_element_type | solution.py:306
  267.9 13.4 %all-to-all-done.2 = bf16[16,4,48,256]{3,2,1,0:T(8,128)(2,1)} async-done(((bf16[16,4,48,256]{3,2,1,0:T(8,128)(2,1)}), bf16[16,4,48,256]{3,2,1,0:T(8,128)(2,1)}, u32[]{:S(2)}, u32[]{:S(2)}) %all-to-all-start.2) | async-done | bytes 1572896 | tf_op jit(solution)/shard_map/all_to_all | solution.py:252
  281.4 1.8 bitcast_convert_fusion
  283.2 3.3 %bitcast_add_fusion = f32[64,48,256]{2,0,1:T(8,128)S(1)} fusion(f32[64,48,256]{2,1,0:T(8,128)S(1)} %bitcast_convert_fusion, bf16[8,6,64,256]{3,2,1,0:T(8,128)(2,1)} %all-to-all-done.5), kind=kLoop, calls=%fused_computation.31 | loop fusion | flops 1572864 | bytes 7864320 | tf_op jit(solution)/shard_map/add | solution.py:306
  286.5 1.7 copy-done.10
  288.2 2.4 fusion.15
  290.6 3.3 %fusion.22 = f32[16,4,48]{2,1,0:T(4,128)S(1)} fusion(f32[16,4,48,256]{3,1,0,2:T(4,128)S(1)} %copy-done.12, f32[256]{0:T(256)S(1)} %copy-done.5, bf16[16,4,48,256]{3,2,1,0:T(8,128)(2,1)} %all-to-all-done.2), kind=kLoop, calls=%fused_computation.34 | loop fusion | flops 3142656 | bytes 4731904 | tf_op jit(solution)/shard_map/reduce_sum | solution.py:205
  293.9 0.1 copy.54
  294.0 4.6 %fusion.19 = bf16[64,48,256]{2,0,1:T(8,128)(2,1)S(1)} fusion(bf16[64,48,256]{2,0,1:T(8,128)(2,1)} %copy-done.11, f32[64,48,256]{2,0,1:T(8,128)} %copy-done.10, f32[64,48]{0,1:T(8,128)S(1)} %broadcast_multiply_fusion.2, f32[64,48]{0,1:T(8,128)S(1)} %copy.54, f32[256]{0:T(256)S(1)} %copy-done.5, f32[64,48]{0,1:T(8,128)S(1)} %add_rsqrt_fusion.1, ...), kind=kLoop, calls=%fused_computation.29 | loop fusion | flops 8650752 | bytes 7914496 | tf_op jit(solution)/shard_map/convert_element_type | solution.py:308
  298.6 2.0 copy.55
  (45 shorter events, 0.2 us)
Async XLA Ops:
  0.0 27.2 %copy-start = (bf16[256,1024]{1,0:T(8,128)(2,1)S(1)}, bf16[256,1024]{1,0:T(8,128)(2,1)}, u32[]{:S(2)}) copy-start(bf16[256,1024]{1,0:T(8,128)(2,1)} %param.23) | copy-start | bytes 1572868
  0.0 2.1 copy-start.13
  2.1 14.6 %copy-start.17 = (f32[9,1024]{1,0:T(8,128)S(1)}, f32[9,1024]{1,0:T(8,128)}, u32[]{:S(2)}) copy-start(f32[9,1024]{1,0:T(8,128)} %param.24) | copy-start | bytes 110596
  2.8 7.2 %collective-permute-start.1 = (bf16[2,48,512]{2,0,1:T(2,128)(2,1)S(1)}, bf16[2,48,512]{2,0,1:T(2,128)(2,1)S(1)}, u32[]{:S(2)}, u32[]{:S(2)}) collective-permute-start(bf16[2,48,512]{2,0,1:T(2,128)(2,1)S(1)} %get-tuple-element.10), channel_id=1, source_target_pairs={{16,0},{32,16},{48,32},{64,48},{80,64},{96,80},{112,96},{17,1},{33... | collective-permute-start | bytes 294920 | tf_op jit(solution)/shard_map/ppermute | solution.py:188
  6.1 5.2 %collective-permute-start = (bf16[2,48,512]{2,0,1:T(2,128)(2,1)S(1)}, bf16[2,48,512]{2,0,1:T(2,128)(2,1)S(1)}, u32[]{:S(2)}, u32[]{:S(2)}) collective-permute-start(bf16[2,48,512]{2,0,1:T(2,128)(2,1)S(1)} %get-tuple-element.9), channel_id=1, source_target_pairs={{0,16},{16,32},{32,48},{48,64},{64,80},{80,96},{96,112},{1,17},{17... | collective-permute-start | bytes 294920 | tf_op jit(solution)/shard_map/ppermute | solution.py:187
  11.3 6.1 %collective-permute-start.3 = (bf16[68,2,512]{2,0,1:T(8,128)(2,1)S(1)}, bf16[68,2,512]{2,0,1:T(8,128)(2,1)S(1)}, u32[]{:S(2)}, u32[]{:S(2)}) collective-permute-start(bf16[68,2,512]{2,0,1:T(8,128)(2,1)S(1)} %get-tuple-element.8), channel_id=1, source_target_pairs={{1,0},{2,1},{3,2},{4,3},{5,4},{6,5},{7,6},{8,7},{9,8},{10,9},{11,1... | collective-permute-start | bytes 417800 | tf_op jit(solution)/shard_map/ppermute | solution.py:188
  12.6 6.6 %collective-permute-start.2 = (bf16[68,2,512]{2,0,1:T(8,128)(2,1)S(1)}, bf16[68,2,512]{2,0,1:T(8,128)(2,1)S(1)}, u32[]{:S(2)}, u32[]{:S(2)}) collective-permute-start(bf16[68,2,512]{2,0,1:T(8,128)(2,1)S(1)} %get-tuple-element.7), channel_id=1, source_target_pairs={{0,1},{1,2},{2,3},{3,4},{4,5},{5,6},{6,7},{7,8},{8,9},{9,10},{10,1... | collective-permute-start | bytes 417800 | tf_op jit(solution)/shard_map/ppermute | solution.py:187
  22.2 4.9 %copy-start.18 = (f32[256]{0:T(256)S(1)}, f32[256]{0:T(256)}, u32[]{:S(2)}) copy-start(f32[256]{0:T(256)} %param.18) | copy-start | bytes 3076
  27.2 2.6 copy-start.19
  92.0 5.8 %copy-start.14 = (bf16[256,256]{1,0:T(8,128)(2,1)S(1)}, bf16[256,256]{1,0:T(8,128)(2,1)}, u32[]{:S(2)}) copy-start(bf16[256,256]{1,0:T(8,128)(2,1)} %param.22) | copy-start | bytes 393220
  96.7 1.1 copy-start.11
  99.0 30.0 %copy-start.8 = (bf16[64,48,256]{2,1,0:T(8,128)(2,1)S(1)}, bf16[64,48,256]{2,1,0:T(8,128)(2,1)}, u32[]{:S(2)}) copy-start(bf16[64,48,256]{2,1,0:T(8,128)(2,1)} %param.14) | copy-start | bytes 4718596
  119.3 22.5 %all-to-all-start.1 = ((bf16[16,4,48,128]{3,2,1,0:T(8,128)(2,1)}), bf16[16,4,48,128]{3,2,1,0:T(8,128)(2,1)S(1)}, u32[]{:S(2)}, u32[]{:S(2)}) async-start(bf16[16,4,48,128]{3,2,1,0:T(8,128)(2,1)} %bitcast.15), calls=%async_computation.1 | async-start | bytes 1572864 | tf_op jit(solution)/shard_map/all_to_all | solution.py:252
  130.7 42.7 %copy-start.15 = (bf16[256,256]{1,0:T(8,128)(2,1)S(1)}, bf16[256,256]{1,0:T(8,128)(2,1)}, u32[]{:S(2)}) copy-start(bf16[256,256]{1,0:T(8,128)(2,1)} %param.21) | copy-start | bytes 393220
  130.7 43.5 %copy-start.16 = (bf16[256,256]{1,0:T(8,128)(2,1)S(1)}, bf16[256,256]{1,0:T(8,128)(2,1)}, u32[]{:S(2)}) copy-start(bf16[256,256]{1,0:T(8,128)(2,1)} %param.20) | copy-start | bytes 393220
  141.8 0.9 copy-start.2
  142.7 35.7 %copy-start.5 = (f32[256]{0:T(256)S(1)}, f32[256]{0:T(256)}, u32[]{:S(2)}) copy-start(f32[256]{0:T(256)} %param.17) | copy-start | bytes 3076
  142.7 35.8 %copy-start.7 = (s32[4,4]{1,0:T(4,128)S(1)}, s32[4,4]{1,0:T(4,128)}, u32[]{:S(2)}) copy-start(s32[4,4]{1,0:T(4,128)} %mask_ref.3) | copy-start | bytes 196
  169.5 38.5 %all-to-all-start = ((bf16[16,4,48,256]{3,2,1,0:T(8,128)(2,1)}), bf16[16,4,48,256]{3,2,1,0:T(8,128)(2,1)S(1)}, u32[]{:S(2)}, u32[]{:S(2)}) async-start(bf16[16,4,48,256]{3,2,1,0:T(8,128)(2,1)} %bitcast.54), calls=%async_computation | async-start | bytes 3145728 | tf_op jit(solution)/shard_map/all_to_all | solution.py:252
  178.4 1.1 copy-start.4
  179.6 36.8 %copy-start.6 = (s32[6,6]{1,0:T(8,128)S(1)}, s32[6,6]{1,0:T(8,128)}, u32[]{:S(2)}) copy-start(s32[6,6]{1,0:T(8,128)} %mask_ref.2) | copy-start | bytes 436
  208.0 8.4 %copy-start.3 = (bf16[16,4,48,128]{3,2,1,0:T(8,128)(2,1)S(1)}, bf16[16,4,48,128]{3,2,1,0:T(8,128)(2,1)}, u32[]{:S(2)}) copy-start(bf16[16,4,48,128]{3,2,1,0:T(8,128)(2,1)} %copy-done.2) | copy-start | bytes 2359300
  208.0 43.1 %all-to-all-start.5 = ((bf16[8,6,64,256]{3,2,1,0:T(8,128)(2,1)}), bf16[8,6,64,256]{3,2,1,0:T(8,128)(2,1)}, u32[]{:S(2)}, u32[]{:S(2)}) async-start(bf16[8,6,64,256]{3,2,1,0:T(8,128)(2,1)} %axial_attention.3), calls=%async_computation.5 | async-start | bytes 3145728 | tf_op jit(solution)/shard_map/all_to_all | solution.py:252
  251.0 6.9 %copy-start.9 = (bf16[64,48,256]{2,1,0:T(8,128)(2,1)S(1)}, bf16[64,48,256]{2,1,0:T(8,128)(2,1)}, u32[]{:S(2)}) copy-start(bf16[64,48,256]{2,1,0:T(8,128)(2,1)} %param.14) | copy-start | bytes 4718596
  251.0 30.3 %all-to-all-start.2 = ((bf16[16,4,48,256]{3,2,1,0:T(8,128)(2,1)}), bf16[16,4,48,256]{3,2,1,0:T(8,128)(2,1)}, u32[]{:S(2)}, u32[]{:S(2)}) async-start(bf16[16,4,48,256]{3,2,1,0:T(8,128)(2,1)} %axial_attention.2), calls=%async_computation.2 | async-start | bytes 3145728 | tf_op jit(solution)/shard_map/all_to_all | solution.py:252
  286.5 1.7 copy-start.10
  288.2 2.4 copy-start.12
  293.9 6.8 %copy-start.1 = (bf16[256,1024]{1,0:T(8,128)(2,1)S(1)}, bf16[256,1024]{1,0:T(8,128)(2,1)}, u32[]{:S(2)}) copy-start(bf16[256,1024]{1,0:T(8,128)(2,1)} %param.23) | copy-start | bytes 1572868

commit v2 on v1

v2 whole, which is shorter than its diff:
```python
import functools

import jax
import jax.numpy as jnp
from jax import lax
from jax.experimental import pallas as pl
from jax.experimental.pallas import tpu as pltpu
from jax.sharding import PartitionSpec as P

HEADS = 8
BLK = 128
EPSILON = 1e-05
GELU_C = 0.7978845608028654
LOG2E = 1.4426950408889634
LN2 = 0.6931471805599453
F32 = jnp.float32
BF16 = jnp.bfloat16
STRIDE = 64
GROUP = 4
CHUNK = GROUP * STRIDE
BIG = 8
GUARD = 2 * GROUP + 4
FC = 256


def dot_nt(a, b):
    return lax.dot_general(a, b, (((1,), (1,)), ((), ())), preferred_element_type=F32)


def gelu_slope(v):
    k = lambda x: jnp.asarray(x, v.dtype)
    u = v * v
    t = jnp.tanh(v * (k(GELU_C) + k(GELU_C * 0.044715) * u))
    poly = v * (k(0.5 * GELU_C) + k(1.5 * 0.044715 * GELU_C) * u)
    return (k(0.5) + k(0.5) * t) + (k(1.0) - t * t) * poly


def normalize(x):
    center = x - jnp.mean(x, axis=-1, keepdims=True)
    inv = lax.rsqrt(jnp.mean(center * center, axis=-1, keepdims=True) + EPSILON)
    return center * inv, inv


def mlp_kernel(rows, cols, mid_ref, gout_ref, rowh_ref, edge_ref, gain_ref, wup_ref, conv_ref, wdown_ref, wout_ref,
               gm_ref, grow_ref, gcol_ref, x_s, h_s, gp_s, y_s, wdt_s, wut_s, grad_s):
    step = pl.program_id(0)
    width = mid_ref.shape[-1]
    gain = gain_ref[...]
    held = rows + 8
    trips = (rows + 4 + GROUP) // GROUP + 2
    tall = BIG * STRIDE

    def rows_at(row):
        return pl.multiple_of(row * STRIDE, STRIDE)

    @pl.when(step == 0)
    def _():
        edges = STRIDE - cols

        def place(ref, lead, row, values, count):
            for j in range(values.shape[0] // count):
                start = (row + j) * STRIDE + (0 if count == cols else cols)
                ref[lead + (pl.ds(pl.multiple_of(start, 16), count), slice(None))] = values[j * count:(j + 1) * count]

        def scaled(values):
            return normalize(values.astype(F32))[0] * gain

        none = jnp.zeros((cols, width), F32)
        for row in (0, 1, rows + 6, rows + 7, rows + 8, rows + 9):
            place(y_s, (0,), row, none, cols)
            place(grad_s, (), row, none.astype(BF16), cols)
        halo = rowh_ref[...].reshape(4 * cols, 2 * width)
        for part, row in ((0, 2), (1, rows + 4)):
            values = halo[part * 2 * cols:(part + 1) * 2 * cols]
            place(y_s, (0,), row, scaled(values[:, :width]), cols)
            place(grad_s, (), row, values[:, width:], cols)

        def edge_block(i, c):
            n = (rows + 10) // 2
            values = edge_ref[pl.ds(i * n, n)].reshape(n * edges, 2 * width)
            place(y_s, (0,), i * n, scaled(values[:, :width]), edges)
            place(grad_s, (), i * n, values[:, width:], edges)
            return c
        lax.fori_loop(0, 2, edge_block, 0)

        def norm_block(i, c):
            src = pl.ds(i * BIG, BIG)
            place(y_s, (0,), i * BIG + 4, scaled(mid_ref[src].reshape(BIG * cols, width)), cols)
            place(grad_s, (), i * BIG + 4, gout_ref[src].reshape(BIG * cols, width), cols)
            return c
        lax.fori_loop(0, rows // BIG, norm_block, 0)

        def shift_block(i, c):
            at = rows_at(i * BIG + 1)
            xv = y_s[0, pl.ds(at, tall + 8), :]
            lv = y_s[0, pl.ds(at - 8, tall + 8), :]
            dst = pl.ds(rows_at(i * BIG), tall)
            x_s[0, dst, :] = lv[7:7 + tall].astype(BF16)
            x_s[1, dst, :] = xv[:tall].astype(BF16)
            x_s[2, dst, :] = xv[1:1 + tall].astype(BF16)
            return c
        lax.fori_loop(0, held // BIG, shift_block, 0)

    wdt_s[...] = wdown_ref[...].astype(F32).T.astype(BF16)
    wut_s[...] = wup_ref[...].astype(F32).T.astype(BF16)
    taps = [conv_ref[t:t + 1, :].astype(BF16) for t in range(9)]
    first = step == 0

    def body(i, c):
        z0 = GROUP * (i - 2) - 2 + GUARD
        for b in range(3):
            parts = []
            for sub in range(GROUP):
                z = None
                for a in range(3):
                    term = gp_s[pl.ds(rows_at(z0 + 1 - a + sub), STRIDE), :] * taps[3 * a + b]
                    z = term if z is None else z + term
                parts.append(z)
            old = y_s[b, pl.ds(rows_at(z0), CHUNK), :]
            y_s[b, pl.ds(rows_at(z0), CHUNK), :] = jnp.where(first, 0.0, old) + jnp.dot(
                jnp.concatenate(parts, axis=0), wut_s[...], preferred_element_type=F32)
        g0 = GROUP * (i - 1) - 1
        ga = jnp.dot(grad_s[pl.ds(rows_at(jnp.clip(g0 + 1, 0, held + 2 - GROUP)), CHUNK), :], wdt_s[...],
                     preferred_element_type=F32)
        for sub in range(GROUP):
            pre = None
            for a in range(3):
                for b in range(3):
                    term = h_s[b, pl.ds(rows_at(g0 + GUARD + a - 1 + sub), STRIDE), :] * taps[3 * a + b]
                    pre = term if pre is None else pre + term
            gp_s[pl.ds(rows_at(g0 + GUARD + sub), STRIDE), :] = (
                ga[sub * STRIDE:(sub + 1) * STRIDE] * gelu_slope(pre).astype(F32)).astype(BF16)
        src = pl.ds(rows_at(jnp.minimum(GROUP * i, held - GROUP)), CHUNK)
        for b in range(3):
            h_s[b, pl.ds(rows_at(GROUP * i + GUARD), CHUNK), :] = jnp.dot(
                x_s[b, src, :], wup_ref[...], preferred_element_type=F32).astype(BF16)
        return c

    lax.fori_loop(0, trips, body, 0)

    @pl.when(step == pl.num_programs(0) - 1)
    def _():
        def finish(i, c):
            base = rows_at(i * BIG + 3 + GUARD)
            right = y_s[0, pl.ds(base, tall + 8), :][1:1 + tall]
            left = y_s[2, pl.ds(base - 8, tall + 8), :][7:7 + tall]
            total = y_s[1, pl.ds(base, tall), :] + right + left

            def crop(v):
                return v.reshape(BIG, STRIDE, width)[:, :cols].reshape(BIG * cols, width)

            e = crop(total) * gain
            src = pl.ds(i * BIG, BIG)
            hat, inv = normalize(mid_ref[src].reshape(BIG * cols, width).astype(F32))
            res = gout_ref[src].reshape(BIG * cols, width).astype(F32) + inv * (
                e - jnp.mean(e, axis=-1, keepdims=True) - hat * jnp.mean(e * hat, axis=-1, keepdims=True))
            res = res.astype(BF16)
            dst = pl.ds(i * BIG, BIG)
            gm_ref[dst] = res.reshape(BIG, cols, width)
            ga = dot_nt(res, wout_ref[...]).astype(BF16)
            grow_ref[dst] = ga[:, :width // 2].reshape(BIG, cols, width // 2)
            gcol_ref[dst] = ga[:, width // 2:].reshape(BIG, cols, width // 2)
            return c
        lax.fori_loop(0, rows // BIG, finish, 0)


def mlp(mid, grad, halo, edge, gain, w_up, conv_kernel, w_down, w_out):
    rows, cols, width = mid.shape
    hidden = w_up.shape[1]
    held = rows + 8
    trips = (rows + 4 + GROUP) // GROUP + 2
    slots = (GROUP * trips + GUARD + 1) * STRIDE
    whole = pl.BlockSpec(memory_space=pltpu.VMEM)
    half = jax.ShapeDtypeStruct((rows, cols, width // 2), BF16)
    return pl.pallas_call(
        functools.partial(mlp_kernel, rows, cols),
        out_shape=(jax.ShapeDtypeStruct((rows, cols, width), BF16), half, half),
        grid=(hidden // FC,),
        in_specs=[whole, whole, whole, whole, whole,
                  pl.BlockSpec((width, FC), lambda i: (0, i)),
                  pl.BlockSpec((9, FC), lambda i: (0, i)),
                  pl.BlockSpec((FC, width), lambda i: (i, 0)),
                  whole],
        out_specs=(whole, whole, whole),
        scratch_shapes=[
            pltpu.VMEM((3, held * STRIDE, width), BF16),
            pltpu.VMEM((3, slots, FC), BF16),
            pltpu.VMEM((slots, FC), BF16),
            pltpu.VMEM((3, slots, width), F32),
            pltpu.VMEM((width, FC), BF16),
            pltpu.VMEM((FC, width), BF16),
            pltpu.VMEM(((rows + 10) * STRIDE, width), BF16),
        ],
        compiler_params=pltpu.CompilerParams(vmem_limit_bytes=60 * 1024 * 1024),
        cost_estimate=pl.CostEstimate(flops=20_000_000_000, transcendentals=4_000_000, bytes_accessed=12_000_000),
        name="mlp_backward",
    )(mid, grad, halo, edge, gain.reshape(1, -1), w_up, conv_kernel, w_down, w_out)


def attn_kernel(nl, nk, half, split, mask_ref, *refs):
    (x_ref, g_ref, gain_ref, wq_ref, wk_ref, wv_ref, out_ref, w_s, wt_s,
     q_s, k_s, v_s, g_s, kt_s, qmt_s, qm_s, gmt_s, gm_s, e_s, dp_s, st_s, dq_s, dk_s, dv_s) = refs if not split else refs[:1] + refs[:1] + refs[1:]
    heads = HEADS // 2
    hw = 128
    hd = hw // heads
    length = nk * BLK
    factor = hd ** -0.5
    gain = gain_ref[...]
    wide = heads * BLK

    qmt_s[...] = jnp.zeros_like(qmt_s)
    gmt_s[...] = jnp.zeros_like(gmt_s)
    dk_s[...] = jnp.zeros_like(dk_s)
    dv_s[...] = jnp.zeros_like(dv_s)

    for j, ref in enumerate((wq_ref, wk_ref, wv_ref)):
        part = ref[:, half * hw:(half + 1) * hw]
        w_s[:, j * hw:(j + 1) * hw] = part
        wt_s[j * hw:(j + 1) * hw, :] = part.astype(F32).T.astype(BF16)

    def prepare(line, carry):
        xv = (x_ref[:, line, :, :2 * hw] if split else x_ref[:, line]).reshape(length, 2 * hw).astype(F32)
        mean = jnp.mean(xv, axis=-1, keepdims=True)
        center = xv - mean
        inv = lax.rsqrt(jnp.mean(center * center, axis=-1, keepdims=True) + EPSILON)
        normed = (center * inv * gain).astype(BF16)
        qkv = jnp.dot(normed, w_s[...], preferred_element_type=F32)
        kf = qkv[:, hw:2 * hw]
        q_s[line] = (qkv[:, :hw] * (factor * LOG2E)).astype(BF16)
        k_s[line] = kf.astype(BF16)
        v_s[line] = qkv[:, 2 * hw:].astype(BF16)
        kt_s[line] = kf.T.astype(BF16)
        g_s[line] = (g_ref[:, line, :, 2 * hw:] if split else g_ref[:, line]).reshape(length, hw)
        return carry

    lax.fori_loop(0, nl, prepare, 0)
    lane = lax.broadcasted_iota(jnp.int32, (BLK, hw), 1)

    def query_block(qb, carry):
        qs = pl.ds(pl.multiple_of(qb * BLK, BLK), BLK)
        for line in range(nl):
            for src, dt, dm in ((q_s, qmt_s, qm_s), (g_s, gmt_s, gm_s)):
                blk = src[line, qs, :]
                blk_f = blk.astype(F32)
                blk_t = blk_f.T.astype(BF16)
                for h in range(heads):
                    dt[line, h * hd:(h + 1) * hd, h * BLK:(h + 1) * BLK] = blk_t[h * hd:(h + 1) * hd]
                    inside = (lane >= h * hd) & (lane < (h + 1) * hd)
                    dm[line, h * BLK:(h + 1) * BLK, :] = jnp.where(inside, blk_f, 0.0).astype(BF16)

        def phase_a(kb, c):
            allowed = mask_ref[qb, kb] > 0
            ks = pl.ds(pl.multiple_of(kb * BLK, BLK), BLK)

            @pl.when(jnp.logical_not(allowed))
            def _():
                for line in range(nl):
                    st_s[kb, line] = jnp.concatenate(
                        [jnp.full((1, wide), -jnp.inf, F32), jnp.zeros((7, wide), F32)], axis=0)

            @pl.when(allowed)
            def _():
                for line in range(nl):
                    s = jnp.dot(k_s[line, ks, :], qmt_s[line], preferred_element_type=F32)
                    dp = jnp.dot(v_s[line, ks, :], gmt_s[line], preferred_element_type=F32)
                    top = jnp.max(s, axis=0, keepdims=True)
                    e = jnp.exp2(s - top)
                    e_s[kb, line] = e.astype(BF16)
                    dp_s[kb, line] = dp
                    st_s[kb, line, 0:1] = top
                    st_s[kb, line, 1:2] = jnp.sum(e, axis=0, keepdims=True)
                    st_s[kb, line, 2:3] = jnp.sum(e * dp, axis=0, keepdims=True)
            return c

        lax.fori_loop(0, nk, phase_a, 0)

        for line in range(nl):
            top = st_s[0, line, 0:1]
            for kb in range(1, nk):
                top = jnp.maximum(top, st_s[kb, line, 0:1])
            total = jnp.zeros((1, wide), F32)
            moment = jnp.zeros((1, wide), F32)
            weights = []
            for kb in range(nk):
                wk = jnp.exp2(st_s[kb, line, 0:1] - top)
                weights.append(wk)
                total = total + wk * st_s[kb, line, 1:2]
                moment = moment + wk * st_s[kb, line, 2:3]
            inv = 1.0 / total
            delta = moment * inv
            for kb in range(nk):
                st_s[kb, line, 3:4] = weights[kb] * inv
                st_s[kb, line, 4:5] = delta
            dq_s[line] = jnp.zeros((hd, wide), F32)

        def phase_b(kb, c):
            ks = pl.ds(pl.multiple_of(kb * BLK, BLK), BLK)

            @pl.when(mask_ref[qb, kb] > 0)
            def _():
                for line in range(nl):
                    p = e_s[kb, line].astype(F32) * st_s[kb, line, 3:4]
                    ds = (p * (dp_s[kb, line] - st_s[kb, line, 4:5])).astype(BF16)
                    dv_s[line, ks, :] += jnp.dot(p.astype(BF16), gm_s[line], preferred_element_type=F32)
                    dk_s[line, ks, :] += jnp.dot(ds, qm_s[line], preferred_element_type=F32)
                    for h in range(heads):
                        dq_s[line, :, h * BLK:(h + 1) * BLK] += jnp.dot(
                            kt_s[line, h * hd:(h + 1) * hd, ks], ds[:, h * BLK:(h + 1) * BLK],
                            preferred_element_type=F32)
            return c

        lax.fori_loop(0, nk, phase_b, 0)
        for line in range(nl):
            full = jnp.concatenate([dq_s[line, :, h * BLK:(h + 1) * BLK] for h in range(heads)], axis=0)
            q_s[line, qs, :] = (full.T * factor).astype(BF16)
        return carry

    lax.fori_loop(0, nk, query_block, 0)

    def finish(line, carry):
        grads = jnp.concatenate(
            [q_s[line], (dk_s[line] * LN2).astype(BF16), dv_s[line].astype(BF16)], axis=1)
        res = jnp.dot(grads, wt_s[...], preferred_element_type=F32).astype(BF16)
        out_ref[:, line] = res.reshape(out_ref.shape[0], out_ref.shape[2], out_ref.shape[3])
        return carry

    lax.fori_loop(0, nl, finish, 0)


def attention(arrays, gain, w_query, w_key, w_value, mask, half):
    srcs, nl, span = arrays[0].shape[:3]
    width = w_query.shape[0]
    length = srcs * span
    nk = length // BLK
    hw = width // 2
    heads = HEADS // 2
    wide = heads * BLK
    vm = pl.BlockSpec(memory_space=pltpu.VMEM)
    pairs = nk * nk * nl
    return pl.pallas_call(
        functools.partial(attn_kernel, nl, nk, half, len(arrays) == 1),
        out_shape=jax.ShapeDtypeStruct((srcs, nl, span, width), BF16),
        in_specs=[pl.BlockSpec(memory_space=pltpu.SMEM)] + [vm] * (len(arrays) + 4),
        out_specs=vm,
        scratch_shapes=[
            pltpu.VMEM((width, 3 * hw), BF16),
            pltpu.VMEM((3 * hw, width), BF16),
            pltpu.VMEM((nl, length, hw), BF16),
            pltpu.VMEM((nl, length, hw), BF16),
            pltpu.VMEM((nl, length, hw), BF16),
            pltpu.VMEM((nl, length, hw), BF16),
            pltpu.VMEM((nl, hw, length), BF16),
            pltpu.VMEM((nl, hw, wide), BF16),
            pltpu.VMEM((nl, wide, hw), BF16),
            pltpu.VMEM((nl, hw, wide), BF16),
            pltpu.VMEM((nl, wide, hw), BF16),
            pltpu.VMEM((nk, nl, BLK, wide), BF16),
            pltpu.VMEM((nk, nl, BLK, wide), F32),
            pltpu.VMEM((nk, nl, 8, wide), F32),
            pltpu.VMEM((nl, hw // heads, wide), F32),
            pltpu.VMEM((nl, length, hw), F32),
            pltpu.VMEM((nl, length, hw), F32),
        ],
        compiler_params=pltpu.CompilerParams(vmem_limit_bytes=40 * 1024 * 1024),
        cost_estimate=pl.CostEstimate(flops=pairs * 200_000_000, transcendentals=pairs * 65536, bytes_accessed=4_000_000),
        name="axial_attention",
    )(mask, *arrays, gain.reshape(1, -1), w_query, w_key, w_value)


def final_kernel(tok_ref, mid_ref, row_ref, col_ref, gain_ref, out_ref):
    count, cols, width = tok_ref.shape

    def flat(ref):
        return ref[...].reshape(count * cols, width).astype(F32)

    hat, inv = normalize(flat(tok_ref))
    e = (flat(row_ref) + flat(col_ref)) * gain_ref[...]
    res = flat(mid_ref) + inv * (
        e - jnp.mean(e, axis=-1, keepdims=True) - hat * jnp.mean(e * hat, axis=-1, keepdims=True))
    out_ref[...] = res.astype(BF16).reshape(count, cols, width)


def final(tokens, grad_mid, row_back, col_back, gain):
    rows, cols, width = tokens.shape
    blk = pl.BlockSpec((8, cols, width), lambda i: (i, 0, 0))
    return pl.pallas_call(
        final_kernel,
        out_shape=jax.ShapeDtypeStruct(tokens.shape, BF16),
        grid=(rows // 8,),
        in_specs=[blk, blk, blk, blk, pl.BlockSpec((1, width), lambda i: (0, 0))],
        out_specs=blk,
        cost_estimate=pl.CostEstimate(flops=20_000_000, transcendentals=4_000, bytes_accessed=8_000_000),
        name="norm_backward",
    )(tokens, grad_mid, row_back, col_back, gain.reshape(1, -1))


def to_lines(blocks, axis):
    return lax.all_to_all(blocks, axis, split_axis=0, concat_axis=0, tiled=True)


def cut_cols(tile, count):
    rows, cols, width = tile.shape
    return jnp.transpose(tile.reshape(rows, count, cols // count, width), (1, 2, 0, 3))


def neighbours(ahead, behind, axis):
    count = lax.axis_size(axis)
    up = [(i, i + 1) for i in range(count - 1)]
    return lax.ppermute(ahead, axis, up), lax.ppermute(behind, axis, [(j, i) for i, j in up])


def per_device(tokens_in, saved_mid, grad_out, attn_gain, mlp_gain, w_query, w_key, w_value, w_out,
               w_up, conv_kernel, w_down, row_mask, col_mask):
    rows, cols, width = tokens_in.shape
    half = width // 2
    count_gx = lax.axis_size("gx")
    count_gy = lax.axis_size("gy")

    def both(rs, cs):
        return jnp.concatenate([saved_mid[rs, cs], grad_out[rs, cs]], axis=-1)

    every = slice(None)
    above, below = neighbours(both(slice(rows - 2, rows), every), both(slice(0, 2), every), "gy")
    row_tokens = to_lines(tokens_in.reshape(count_gx, rows // count_gx, cols, width), "gx")
    sides = [jnp.concatenate([above[:, cs], both(every, cs), below[:, cs]], axis=0)
             for cs in (slice(cols - 2, cols), slice(0, 2))]
    left, right = neighbours(sides[0], sides[1], "gx")
    edge = jnp.concatenate([
        jnp.pad(right, ((2, 4), (0, 0), (0, 0))),
        jnp.zeros((rows + 10, STRIDE - cols - 4, 2 * width), BF16),
        jnp.pad(left, ((1, 5), (0, 0), (0, 0)))], axis=1)
    halo = jnp.concatenate([above, below], axis=0)
    grad_mid, grad_row, grad_col = mlp(
        saved_mid, grad_out, halo, edge, mlp_gain, w_up, conv_kernel, w_down, w_out)
    grad_row = to_lines(grad_row.reshape(count_gx, rows // count_gx, cols, half), "gx")
    col_lines = to_lines(cut_cols(jnp.concatenate([tokens_in, grad_col], axis=-1), count_gy), "gy")
    weights = (w_query, w_key, w_value)
    row_out = attention((row_tokens, grad_row), attn_gain, *weights, row_mask, 0)
    row_back = to_lines(row_out, "gx").reshape(rows, cols, width)
    col_out = attention((col_lines,), attn_gain, *weights, col_mask, 1)
    col_back = jnp.transpose(to_lines(col_out, "gy"), (2, 0, 1, 3)).reshape(rows, cols, width)
    return final(tokens_in, grad_mid, row_back, col_back, attn_gain)


def solution(mesh):
    tile = P("gy", "gx", None)
    return jax.shard_map(per_device, mesh=mesh, in_specs=(tile,) * 3 + (P(),) * 11, out_specs=tile, check_vma=False)
```

time: 303 us -> 243 us (0.80)
  matrix products: 66 us -> 0 us
  Pallas kernels: 63.1 us -> 120 us
  other arithmetic: 33.9 us -> 3.86 us
  local copies, waits for them, and re-layouts: 24.8 us -> 7.64 us
  blocking collectives: 45.8 us -> 36.3 us
  waiting for transfers between devices: 28.6 us -> 36.4 us
    dot_general x4 -> x0, matrix products: 66 us -> none  [the longest x1 33.9 us: mlp_band(): grad_norm = jnp.dot(grad_hidden, w_up.T, preferred_element_type=jnp.float32)]
    pallas_call x2 -> x4, Pallas kernels: 63.1 us -> 120 us  [the longest x2 61.4 us: attention(): pl.pallas_call(functools.partial(attn_kernel, nl, nk, half, len(arrays) =...]
    convert_element_type x4 -> x0, other arithmetic: 14.6 us -> none  [the longest x1 4.64 us: per_device(): return (grad_mid.astype(jnp.float32) + norm_grad).astype(jnp.bfloat16)]
    unnamed x48 -> x16, local copies, waits for them, and re-layouts: 11.8 us -> 1.18 us
    reduce_sum x6 -> x0, other arithmetic: 10.1 us -> none  [the longest x1 3.32 us: norm_backward(): jnp.mean(grad_hat, axis=-1, keepdims=True)]
    all_to_all x2 -> x1, blocking collectives: 45.8 us -> 36.3 us  [to_lines(): return lax.all_to_all(blocks, axis, split_axis=0, concat_axis=0, tiled=True)]
    all_to_all x4, waiting for transfers between devices: 24.5 us -> 32.6 us  [to_lines(): return lax.all_to_all(blocks, axis, split_axis=0, concat_axis=0, tiled=True)]
    convert_element_type x2 -> x0, local copies, waits for them, and re-layouts: 6.83 us -> none  [the longest x1 4.8 us: per_device(): grad_col_in.astype(jnp.float32)]
  transfers between devices with their start and end apart: 8 -> 8, of which waited for: 6 -> 4; matrix products, arithmetic and copies ran while one was open for 7% -> 3% of each run, Pallas kernels for 21% -> 25%
where the time goes in v2:
time: 243 us
  Pallas kernels  120 us (49%)
  starting transfers between devices  37.8 us (16%)
  waiting for transfers between devices  36.4 us (15%)
  blocking collectives  36.3 us (15%)
  local copies, waits for them, and re-layouts  7.64 us (3%)
  other arithmetic  3.86 us (2%)
    pallas_call x2, Pallas kernels, attention(): pl.pallas_call(functools.partial(attn_kernel, nl, nk, half, len(arrays) =...  61.4 us
    pallas_call x1, Pallas kernels, mlp(): pl.pallas_call(functools.partial(mlp_kernel, rows, cols), out_shape=(jax....  51.2 us
    all_to_all x1, blocking collectives, to_lines(): return lax.all_to_all(blocks, axis, split_axis=0, concat_axis=0, tiled=True)  36.3 us
    all_to_all x4, waiting for transfers between devices, to_lines(): return lax.all_to_all(blocks, axis, split_axis=0, concat_axis=0, tiled=True)  32.6 us
    all_to_all x4, starting transfers between devices, to_lines(): return lax.all_to_all(blocks, axis, split_axis=0, concat_axis=0, tiled=True)  25.6 us
    ppermute x2, starting transfers between devices, neighbours(): lax.ppermute(ahead, axis, up)  8.93 us
    pallas_call x1, Pallas kernels, final(): pl.pallas_call(final_kernel, out_shape=jax.ShapeDtypeStruct(tokens.shape,...  7.75 us
  transfers between devices with their start and end apart: 8, of which 4 were waited for; matrix products, arithmetic and copies ran while one was open for 3% of the time, Pallas kernels for 25%

profile of v2, /device:TPU:1, one launch (start us, length us, event | category | flops | bytes accessed | tf_op | source)
XLA Modules:
  0.0 242.5 jit_solution(16121405672022136241)
XLA Ops:
  0.0 0.9 fusion.6
  0.9 4.9 %collective-permute-start = (bf16[2,48,512]{2,1,0:T(8,128)(2,1)S(1)}, bf16[2,48,512]{2,1,0:T(8,128)(2,1)S(1)}, u32[]{:S(2)}, u32[]{:S(2)}) collective-permute-start(bf16[2,48,512]{2,1,0:T(8,128)(2,1)S(1)} %pad_maximum_fusion.4), channel_id=1, source_target_pairs={{0,16},{16,32},{32,48},{48,64},{64,80},{80,96},{96,112},{1,17},{17... | collective-permute-start | bytes 294920 | tf_op jit(solution)/shard_map/ppermute | solution.py:409
  5.9 1.9 collective-permute-start.1
  7.8 1.4 fusion.4
  9.2 0.0 collective-permute-done
  9.2 2.6 %collective-permute-done.1 = bf16[2,48,512]{2,1,0:T(8,128)(2,1)S(1)} collective-permute-done((bf16[2,48,512]{2,1,0:T(8,128)(2,1)S(1)}, bf16[2,48,512]{2,1,0:T(8,128)(2,1)S(1)}, u32[]{:S(2)}, u32[]{:S(2)}) %collective-permute-start.1) | collective-permute-done | bytes 98336 | tf_op jit(solution)/shard_map/ppermute | solution.py:409
  11.8 0.1 pad_maximum_fusion.2
  11.9 1.3 collective-permute-start.2
  13.2 0.1 pad_maximum_fusion.3
  13.4 4.0 %collective-permute-start.3 = (bf16[68,2,512]{2,1,0:T(2,128)(2,1)S(1)}, bf16[68,2,512]{2,1,0:T(2,128)(2,1)S(1)}, u32[]{:S(2)}, u32[]{:S(2)}) collective-permute-start(bf16[68,2,512]{2,1,0:T(2,128)(2,1)S(1)} %pad_maximum_fusion.3), channel_id=1, source_target_pairs={{0,1},{1,2},{2,3},{3,4},{4,5},{5,6},{6,7},{7,8},{8,9},{9,10},{10,1... | collective-permute-start | bytes 417800 | tf_op jit(solution)/shard_map/ppermute | solution.py:409
  17.4 0.1 pad.13.clone
  17.5 0.7 pad_maximum_fusion.1.rowh_ref
  18.2 0.0 collective-permute-done.2
  18.2 1.2 collective-permute-done.3
  19.4 1.5 fusion.2.edge_ref
  20.9 51.2 %mlp_backward.1 = (bf16[64,48,256]{2,1,0:T(8,128)(2,1)}, bf16[64,48,128]{2,1,0:T(8,128)(2,1)}, bf16[64,48,128]{2,1,0:T(8,128)(2,1)}) custom-call(bf16[64,48,256]{2,1,0:T(8,128)(2,1)} %mid_ref.1, bf16[64,48,256]{2,1,0:T(8,128)(2,1)} %gout_ref.1, bf16[4,48,512]{2,1,0:T(8,128)(2,1)} %pad_maximum_fusion.1.rowh_ref, bf16[74,16,512]{2,1,0:T(8,128)(2,1)} %fusion.2.edge_ref, ...), custom_call_target="tpu_custom_call" | custom-call | flops 20000000000 | bytes 12000000 | tf_op jit(solution)/shard_map/mlp_backward/pallas_call | solution.py:175
  72.1 0.0 copy-start.7
  72.1 9.5 %all-to-all-start.1 = ((bf16[16,4,48,128]{3,2,1,0:T(8,128)(2,1)}), bf16[16,4,48,128]{3,2,1,0:T(8,128)(2,1)S(1)}, u32[]{:S(2)}, u32[]{:S(2)}) async-start(bf16[16,4,48,128]{3,2,1,0:T(8,128)(2,1)} %bitcast.17), calls=%async_computation.1 | async-start | bytes 1572864 | tf_op jit(solution)/shard_map/all_to_all | solution.py:398
  81.6 0.0 copy-done.7
  81.6 1.4 pad_maximum_fusion
  83.0 2.0 copy.17
  85.0 11.0 %all-to-all-done.1.refs_1_ = bf16[16,4,48,128]{3,2,1,0:T(8,128)(2,1)S(1)} async-done(((bf16[16,4,48,128]{3,2,1,0:T(8,128)(2,1)}), bf16[16,4,48,128]{3,2,1,0:T(8,128)(2,1)S(1)}, u32[]{:S(2)}, u32[]{:S(2)}) %all-to-all-start.1) | async-done | bytes 786464 | tf_op jit(solution)/shard_map/all_to_all | solution.py:398
  96.0 36.3 %all_to_all.25.refs_0_ = bf16[8,6,64,384]{3,2,1,0:T(8,128)(2,1)S(1)} all-to-all(bf16[8,6,64,384]{3,2,1,0:T(8,128)(2,1)} %bitcast.15), channel_id=1, replica_groups=mesh['gy'=8,'gx'=16] {'gy'}, dimensions={0} | all-to-all | bytes 4718592 | tf_op jit(solution)/shard_map/all_to_all | solution.py:398
  132.3 0.0 copy-start.1
  132.3 0.0 copy-start.2
  132.3 0.0 copy-start.3
  132.3 0.0 copy-start.4
  132.3 0.0 copy-start.6
  132.3 4.6 %all-to-all-start = ((bf16[16,4,48,256]{3,2,1,0:T(8,128)(2,1)}), bf16[16,4,48,256]{3,2,1,0:T(8,128)(2,1)}, u32[]{:S(2)}, u32[]{:S(2)}) async-start(bf16[16,4,48,256]{3,2,1,0:T(8,128)(2,1)} %bitcast.14), calls=%async_computation | async-start | bytes 3145728 | tf_op jit(solution)/shard_map/all_to_all | solution.py:398
  136.9 0.0 copy-done.1
  136.9 0.0 copy-done.2
  136.9 0.0 copy-done.3
  136.9 0.0 copy-done.4
  136.9 0.0 copy-done.6
  136.9 25.8 %axial_attention.3 = bf16[8,6,64,256]{3,2,1,0:T(8,128)(2,1)S(1)} custom-call(s32[4,4]{1,0:T(4,128)S(1)} %copy-done.6, bf16[8,6,64,384]{3,2,1,0:T(8,128)(2,1)S(1)} %all_to_all.25.refs_0_, f32[1,256]{1,0:T(1,128)S(1)} %bitcast.12, bf16[256,256]{1,0:T(8,128)(2,1)S(1)} %copy-done.2, bf16[256,256]{1,0:T(8,128)(2,1)S(1)} %copy-done.3, bf16[256,256]{1,0:T(8,128)(2,1)S(1)} %copy-done.4), custom_call_target="tpu_custom_call" | custom-call | flops 19200000000 | bytes 4000000 | tf_op jit(solution)/shard_map/axial_attention/pallas_call | solution.py:340
  162.8 0.0 copy-start
  162.8 1.2 copy-done
  163.9 0.0 copy-start.5
  163.9 0.0 all-to-all-done.refs_0_
  163.9 4.7 %all-to-all-start.4 = ((bf16[8,6,64,256]{3,2,1,0:T(8,128)(2,1)}), bf16[8,6,64,256]{3,2,1,0:T(8,128)(2,1)S(1)}, u32[]{:S(2)}, u32[]{:S(2)}) async-start(bf16[8,6,64,256]{3,2,1,0:T(8,128)(2,1)} %copy-done), calls=%async_computation.4 | async-start | bytes 3145728 | tf_op jit(solution)/shard_map/all_to_all | solution.py:398
  168.6 0.0 copy-done.5
  168.6 35.6 %axial_attention.2 = bf16[16,4,48,256]{3,2,1,0:T(8,128)(2,1)} custom-call(s32[6,6]{1,0:T(8,128)S(1)} %copy-done.5, bf16[16,4,48,256]{3,2,1,0:T(8,128)(2,1)} %all-to-all-done.refs_0_, bf16[16,4,48,128]{3,2,1,0:T(8,128)(2,1)S(1)} %all-to-all-done.1.refs_1_, f32[1,256]{1,0:T(1,128)S(1)} %bitcast.13, bf16[256,256]{1,0:T(8,128)(2,1)S(1)} %copy-done.2, ...), custom_call_target="tpu_custom_call" | custom-call | flops 28800000000 | bytes 4000000 | tf_op jit(solution)/shard_map/axial_attention/pallas_call | solution.py:340
  204.2 0.0 all-to-all-done.4
  204.2 6.9 %all-to-all-start.2 = ((bf16[16,4,48,256]{3,2,1,0:T(8,128)(2,1)}), bf16[16,4,48,256]{3,2,1,0:T(8,128)(2,1)}, u32[]{:S(2)}, u32[]{:S(2)}) async-start(bf16[16,4,48,256]{3,2,1,0:T(8,128)(2,1)} %axial_attention.2), calls=%async_computation.2 | async-start | bytes 3145728 | tf_op jit(solution)/shard_map/all_to_all | solution.py:398
  211.1 2.0 copy.18.col_ref
  213.1 21.6 %all-to-all-done.2 = bf16[16,4,48,256]{3,2,1,0:T(8,128)(2,1)} async-done(((bf16[16,4,48,256]{3,2,1,0:T(8,128)(2,1)}), bf16[16,4,48,256]{3,2,1,0:T(8,128)(2,1)}, u32[]{:S(2)}, u32[]{:S(2)}) %all-to-all-start.2) | async-done | bytes 1572896 | tf_op jit(solution)/shard_map/all_to_all | solution.py:398
  234.8 7.8 %norm_backward.1 = bf16[64,48,256]{2,1,0:T(8,128)(2,1)} custom-call(bf16[64,48,256]{2,1,0:T(8,128)(2,1)} %tok_ref.1, bf16[64,48,256]{2,1,0:T(8,128)(2,1)} %get-tuple-element.8.mid_ref, bf16[64,48,256]{2,1,0:T(8,128)(2,1)} %bitcast.4.row_ref, bf16[64,48,256]{2,1,0:T(8,128)(2,1)} %copy.18.col_ref, f32[1,256]{1,0:T(1,128)} %bitcast.11), custom_call_target="tpu_custom_call" | custom-call | flops 20000000 | bytes 8000000 | tf_op jit(solution)/shard_map/norm_backward/pallas_call | solution.py:386
  (5 shorter events, 0.0 us)
Async XLA Ops:
  0.9 8.3 %collective-permute-start = (bf16[2,48,512]{2,1,0:T(8,128)(2,1)S(1)}, bf16[2,48,512]{2,1,0:T(8,128)(2,1)S(1)}, u32[]{:S(2)}, u32[]{:S(2)}) collective-permute-start(bf16[2,48,512]{2,1,0:T(8,128)(2,1)S(1)} %pad_maximum_fusion.4), channel_id=1, source_target_pairs={{0,16},{16,32},{32,48},{48,64},{64,80},{80,96},{96,112},{1,17},{17... | collective-permute-start | bytes 294920 | tf_op jit(solution)/shard_map/ppermute | solution.py:409
  5.9 5.9 %collective-permute-start.1 = (bf16[2,48,512]{2,1,0:T(8,128)(2,1)S(1)}, bf16[2,48,512]{2,1,0:T(8,128)(2,1)S(1)}, u32[]{:S(2)}, u32[]{:S(2)}) collective-permute-start(bf16[2,48,512]{2,1,0:T(8,128)(2,1)S(1)} %pad_maximum_fusion.5), channel_id=1, source_target_pairs={{16,0},{32,16},{48,32},{64,48},{80,64},{96,80},{112,96},{17,1},{33... | collective-permute-start | bytes 294920 | tf_op jit(solution)/shard_map/ppermute | solution.py:409
  11.9 6.2 %collective-permute-start.2 = (bf16[68,2,512]{2,1,0:T(2,128)(2,1)S(1)}, bf16[68,2,512]{2,1,0:T(2,128)(2,1)S(1)}, u32[]{:S(2)}, u32[]{:S(2)}) collective-permute-start(bf16[68,2,512]{2,1,0:T(2,128)(2,1)S(1)} %pad_maximum_fusion.2), channel_id=1, source_target_pairs={{1,0},{2,1},{3,2},{4,3},{5,4},{6,5},{7,6},{8,7},{9,8},{10,9},{11,1... | collective-permute-start | bytes 417800 | tf_op jit(solution)/shard_map/ppermute | solution.py:409
  13.4 6.0 %collective-permute-start.3 = (bf16[68,2,512]{2,1,0:T(2,128)(2,1)S(1)}, bf16[68,2,512]{2,1,0:T(2,128)(2,1)S(1)}, u32[]{:S(2)}, u32[]{:S(2)}) collective-permute-start(bf16[68,2,512]{2,1,0:T(2,128)(2,1)S(1)} %pad_maximum_fusion.3), channel_id=1, source_target_pairs={{0,1},{1,2},{2,3},{3,4},{4,5},{5,6},{6,7},{7,8},{8,9},{9,10},{10,1... | collective-permute-start | bytes 417800 | tf_op jit(solution)/shard_map/ppermute | solution.py:409
  72.1 9.5 %copy-start.7 = (bf16[64,48,256]{2,1,0:T(8,128)(2,1)S(1)}, bf16[64,48,256]{2,1,0:T(8,128)(2,1)}, u32[]{:S(2)}) copy-start(bf16[64,48,256]{2,1,0:T(8,128)(2,1)} %tok_ref.1) | copy-start | bytes 4718596
  72.1 23.9 %all-to-all-start.1 = ((bf16[16,4,48,128]{3,2,1,0:T(8,128)(2,1)}), bf16[16,4,48,128]{3,2,1,0:T(8,128)(2,1)S(1)}, u32[]{:S(2)}, u32[]{:S(2)}) async-start(bf16[16,4,48,128]{3,2,1,0:T(8,128)(2,1)} %bitcast.17), calls=%async_computation.1 | async-start | bytes 1572864 | tf_op jit(solution)/shard_map/all_to_all | solution.py:398
  132.3 4.6 %copy-start.1 = (f32[256]{0:T(256)S(1)}, f32[256]{0:T(256)}, u32[]{:S(2)}) copy-start(f32[256]{0:T(256)} %param.17) | copy-start | bytes 3076
  132.3 4.6 %copy-start.2 = (bf16[256,256]{1,0:T(8,128)(2,1)S(1)}, bf16[256,256]{1,0:T(8,128)(2,1)}, u32[]{:S(2)}) copy-start(bf16[256,256]{1,0:T(8,128)(2,1)} %refs_2_.1) | copy-start | bytes 393220
  132.3 4.6 %copy-start.3 = (bf16[256,256]{1,0:T(8,128)(2,1)S(1)}, bf16[256,256]{1,0:T(8,128)(2,1)}, u32[]{:S(2)}) copy-start(bf16[256,256]{1,0:T(8,128)(2,1)} %refs_3_.3) | copy-start | bytes 393220
  132.3 4.6 %copy-start.4 = (bf16[256,256]{1,0:T(8,128)(2,1)S(1)}, bf16[256,256]{1,0:T(8,128)(2,1)}, u32[]{:S(2)}) copy-start(bf16[256,256]{1,0:T(8,128)(2,1)} %refs_4_.3) | copy-start | bytes 393220
  132.3 4.6 %copy-start.6 = (s32[4,4]{1,0:T(4,128)S(1)}, s32[4,4]{1,0:T(4,128)}, u32[]{:S(2)}) copy-start(s32[4,4]{1,0:T(4,128)} %mask_ref.3) | copy-start | bytes 196
  132.3 31.6 %all-to-all-start = ((bf16[16,4,48,256]{3,2,1,0:T(8,128)(2,1)}), bf16[16,4,48,256]{3,2,1,0:T(8,128)(2,1)}, u32[]{:S(2)}, u32[]{:S(2)}) async-start(bf16[16,4,48,256]{3,2,1,0:T(8,128)(2,1)} %bitcast.14), calls=%async_computation | async-start | bytes 3145728 | tf_op jit(solution)/shard_map/all_to_all | solution.py:398
  162.8 1.2 copy-start
  163.9 4.7 %copy-start.5 = (s32[6,6]{1,0:T(8,128)S(1)}, s32[6,6]{1,0:T(8,128)}, u32[]{:S(2)}) copy-start(s32[6,6]{1,0:T(8,128)} %mask_ref.2) | copy-start | bytes 436
  163.9 40.3 %all-to-all-start.4 = ((bf16[8,6,64,256]{3,2,1,0:T(8,128)(2,1)}), bf16[8,6,64,256]{3,2,1,0:T(8,128)(2,1)S(1)}, u32[]{:S(2)}, u32[]{:S(2)}) async-start(bf16[8,6,64,256]{3,2,1,0:T(8,128)(2,1)} %copy-done), calls=%async_computation.4 | async-start | bytes 3145728 | tf_op jit(solution)/shard_map/all_to_all | solution.py:398
  204.2 30.6 %all-to-all-start.2 = ((bf16[16,4,48,256]{3,2,1,0:T(8,128)(2,1)}), bf16[16,4,48,256]{3,2,1,0:T(8,128)(2,1)}, u32[]{:S(2)}, u32[]{:S(2)}) async-start(bf16[16,4,48,256]{3,2,1,0:T(8,128)(2,1)} %axial_attention.2), calls=%async_computation.2 | async-start | bytes 3145728 | tf_op jit(solution)/shard_map/all_to_all | solution.py:398

commit v3 on v2

--- a/solution.py
+++ b/solution.py
@@ -432,12 +432,18 @@
     halo = jnp.concatenate([above, below], axis=0)
     grad_mid, grad_row, grad_col = mlp(
         saved_mid, grad_out, halo, edge, mlp_gain, w_up, conv_kernel, w_down, w_out)
+    hold = lax.optimization_barrier
+    grad_row, row_tokens = hold((grad_row, row_tokens))
     grad_row = to_lines(grad_row.reshape(count_gx, rows // count_gx, cols, half), "gx")
-    col_lines = to_lines(cut_cols(jnp.concatenate([tokens_in, grad_col], axis=-1), count_gy), "gy")
+    col_send = cut_cols(jnp.concatenate([tokens_in, grad_col], axis=-1), count_gy)
+    grad_row, col_send = hold((grad_row, col_send))
+    col_lines = to_lines(col_send, "gy")
     weights = (w_query, w_key, w_value)
     row_out = attention((row_tokens, grad_row), attn_gain, *weights, row_mask, 0)
+    row_out, col_lines = hold((row_out, col_lines))
     row_back = to_lines(row_out, "gx").reshape(rows, cols, width)
     col_out = attention((col_lines,), attn_gain, *weights, col_mask, 1)
+    row_back, col_out = hold((row_back, col_out))
     col_back = jnp.transpose(to_lines(col_out, "gy"), (2, 0, 1, 3)).reshape(rows, cols, width)
     return final(tokens_in, grad_mid, row_back, col_back, attn_gain)
 

time: 243 us -> 207 us (0.85); the launches traced: 243 us -> 203 us
  waiting for transfers between devices: 36.4 us -> 10.2 us
  blocking collectives: 36.3 us -> 26.7 us
  Pallas kernels: 120 us -> 114 us
  local copies, waits for them, and re-layouts: 7.64 us -> 10.2 us
    all_to_all x4, waiting for transfers between devices: 32.6 us -> 10 us  [to_lines(): return lax.all_to_all(blocks, axis, split_axis=0, concat_axis=0, tiled=True)]
    all_to_all x1, blocking collectives: 36.3 us -> 26.7 us  [to_lines(): return lax.all_to_all(blocks, axis, split_axis=0, concat_axis=0, tiled=True)]
    pallas_call x2, Pallas kernels: 61.4 us -> 55.3 us  [attention(): pl.pallas_call(functools.partial(attn_kernel, nl, nk, half, len(arrays) =...]
    ppermute x2, waiting for transfers between devices: 2.57 us -> 0.01 us  [neighbours(): lax.ppermute(behind, axis, [(j, i) for i, j in up])]
    unnamed x16 -> x22, local copies, waits for them, and re-layouts: 1.18 us -> 3.74 us
  transfers between devices with their start and end apart: 8 -> 8, of which waited for: 4 -> 2; matrix products, arithmetic and copies ran while one was open for 3% -> 4% of each run, Pallas kernels for 25% -> 53%
where the time goes in v3:
time: 207 us; the launch traced here: 203 us
  Pallas kernels  114 us (55%)
  starting transfers between devices  36.8 us (18%)
  blocking collectives  26.7 us (13%)
  local copies, waits for them, and re-layouts  10.2 us (5%)
  waiting for transfers between devices  10.2 us (5%)
  other arithmetic  4.13 us (2%)
    pallas_call x2, Pallas kernels, attention(): pl.pallas_call(functools.partial(attn_kernel, nl, nk, half, len(arrays) =...  55.3 us
    pallas_call x1, Pallas kernels, mlp(): pl.pallas_call(functools.partial(mlp_kernel, rows, cols), out_shape=(jax....  51.2 us
    all_to_all x1, blocking collectives, to_lines(): return lax.all_to_all(blocks, axis, split_axis=0, concat_axis=0, tiled=True)  26.7 us
    all_to_all x4, starting transfers between devices, to_lines(): return lax.all_to_all(blocks, axis, split_axis=0, concat_axis=0, tiled=True)  25.4 us
    all_to_all x4, waiting for transfers between devices, to_lines(): return lax.all_to_all(blocks, axis, split_axis=0, concat_axis=0, tiled=True)  10 us
    pallas_call x1, Pallas kernels, final(): pl.pallas_call(final_kernel, out_shape=jax.ShapeDtypeStruct(tokens.shape,...  7.75 us
    ppermute x2, starting transfers between devices, neighbours(): lax.ppermute(ahead, axis, up)  6.73 us
    ppermute x2, starting transfers between devices, neighbours(): lax.ppermute(behind, axis, [(j, i) for i, j in up])  4.62 us
  transfers between devices with their start and end apart: 8, of which 2 were waited for; matrix products, arithmetic and copies ran while one was open for 4% of the time, Pallas kernels for 53%

profile of v3, /device:TPU:1, one launch (start us, length us, event | category | flops | bytes accessed | tf_op | source)
XLA Modules:
  0.0 202.5 jit_solution(18069359843988350751)
XLA Ops:
  0.0 0.9 fusion.6
  0.9 3.3 %collective-permute-start.1 = (bf16[2,48,512]{2,1,0:T(8,128)(2,1)S(1)}, bf16[2,48,512]{2,1,0:T(8,128)(2,1)S(1)}, u32[]{:S(2)}, u32[]{:S(2)}) collective-permute-start(bf16[2,48,512]{2,1,0:T(8,128)(2,1)S(1)} %pad_maximum_fusion.5), channel_id=1, source_target_pairs={{16,0},{32,16},{48,32},{64,48},{80,64},{96,80},{112,96},{17,1},{33... | collective-permute-start | bytes 294920 | tf_op jit(solution)/shard_map/ppermute | solution.py:409
  4.3 3.5 %collective-permute-start = (bf16[2,48,512]{2,1,0:T(8,128)(2,1)S(1)}, bf16[2,48,512]{2,1,0:T(8,128)(2,1)S(1)}, u32[]{:S(2)}, u32[]{:S(2)}) collective-permute-start(bf16[2,48,512]{2,1,0:T(8,128)(2,1)S(1)} %pad_maximum_fusion.4), channel_id=1, source_target_pairs={{0,16},{16,32},{32,48},{48,64},{64,80},{80,96},{96,112},{1,17},{17... | collective-permute-start | bytes 294920 | tf_op jit(solution)/shard_map/ppermute | solution.py:409
  7.8 1.4 fusion.4
  9.2 0.0 collective-permute-done.1
  9.2 0.2 collective-permute-done
  9.4 0.1 pad_maximum_fusion.3
  9.6 3.2 %collective-permute-start.3 = (bf16[68,2,512]{2,1,0:T(2,128)(2,1)S(1)}, bf16[68,2,512]{2,1,0:T(2,128)(2,1)S(1)}, u32[]{:S(2)}, u32[]{:S(2)}) collective-permute-start(bf16[68,2,512]{2,1,0:T(2,128)(2,1)S(1)} %pad_maximum_fusion.3), channel_id=1, source_target_pairs={{0,1},{1,2},{2,3},{3,4},{4,5},{5,6},{6,7},{7,8},{8,9},{9,10},{10,1... | collective-permute-start | bytes 417800 | tf_op jit(solution)/shard_map/ppermute | solution.py:409
  12.8 0.1 pad_maximum_fusion.2
  12.9 1.3 collective-permute-start.2
  14.2 7.5 %all-to-all-start = ((bf16[16,4,48,256]{3,2,1,0:T(8,128)(2,1)}), bf16[16,4,48,256]{3,2,1,0:T(8,128)(2,1)S(1)}, u32[]{:S(2)}, u32[]{:S(2)}) async-start(bf16[16,4,48,256]{3,2,1,0:T(8,128)(2,1)} %bitcast.1), calls=%async_computation | async-start | bytes 3145728 | tf_op jit(solution)/shard_map/all_to_all | solution.py:398
  21.8 0.1 pad.13.clone
  21.8 0.7 pad_maximum_fusion.1.rowh_ref
  22.5 0.0 collective-permute-done.3
  22.5 0.0 collective-permute-done.2
  22.5 1.5 fusion.2.edge_ref
  24.1 51.2 %mlp_backward.1 = (bf16[64,48,256]{2,1,0:T(8,128)(2,1)}, bf16[64,48,128]{2,1,0:T(8,128)(2,1)}, bf16[64,48,128]{2,1,0:T(8,128)(2,1)}) custom-call(bf16[64,48,256]{2,1,0:T(8,128)(2,1)} %mid_ref.1, bf16[64,48,256]{2,1,0:T(8,128)(2,1)} %gout_ref.1, bf16[4,48,512]{2,1,0:T(8,128)(2,1)} %pad_maximum_fusion.1.rowh_ref, bf16[74,16,512]{2,1,0:T(8,128)(2,1)} %fusion.2.edge_ref, ...), custom_call_target="tpu_custom_call" | custom-call | flops 20000000000 | bytes 12000000 | tf_op jit(solution)/shard_map/mlp_backward/pallas_call | solution.py:175
  75.3 0.0 copy-start.10
  75.3 0.0 all-to-all-done.refs_0_
  75.3 0.0 copy-start
  75.3 6.8 %all-to-all-start.1 = ((bf16[16,4,48,128]{3,2,1,0:T(8,128)(2,1)}), bf16[16,4,48,128]{3,2,1,0:T(8,128)(2,1)S(1)}, u32[]{:S(2)}, u32[]{:S(2)}) async-start(bf16[16,4,48,128]{3,2,1,0:T(8,128)(2,1)} %bitcast.16), calls=%async_computation.1 | async-start | bytes 1572864 | tf_op jit(solution)/shard_map/all_to_all | solution.py:398
  82.1 0.0 copy-done.10
  82.1 1.6 pad_maximum_fusion
  83.8 0.0 copy-done
  83.8 2.0 copy.17
  85.8 10.0 %all-to-all-done.1.refs_1_ = bf16[16,4,48,128]{3,2,1,0:T(8,128)(2,1)S(1)} async-done(((bf16[16,4,48,128]{3,2,1,0:T(8,128)(2,1)}), bf16[16,4,48,128]{3,2,1,0:T(8,128)(2,1)S(1)}, u32[]{:S(2)}, u32[]{:S(2)}) %all-to-all-start.1) | async-done | bytes 786464 | tf_op jit(solution)/shard_map/all_to_all | solution.py:398
  95.8 0.0 copy-start.4
  95.8 0.0 copy-start.5
  95.8 0.0 copy-start.6
  95.8 0.0 copy-start.7
  95.8 0.0 copy-start.8
  95.8 6.6 %all-to-all-start.2 = ((bf16[8,6,64,384]{3,2,1,0:T(8,128)(2,1)}), bf16[8,6,64,384]{3,2,1,0:T(8,128)(2,1)S(1)}, u32[]{:S(2)}, u32[]{:S(2)}) async-start(bf16[8,6,64,384]{3,2,1,0:T(8,128)(2,1)} %bitcast.14), calls=%async_computation.2 | async-start | bytes 4718592 | tf_op jit(solution)/shard_map/all_to_all | solution.py:398
  102.4 0.0 copy-done.4
  102.4 0.0 copy-done.5
  102.4 0.0 copy-done.6
  102.4 0.0 copy-done.7
  102.4 0.0 copy-done.8
  102.4 0.0 copy-start.1
  102.4 1.4 copy-done.1
  103.8 32.5 %axial_attention.2 = bf16[16,4,48,256]{3,2,1,0:T(8,128)(2,1)S(1)} custom-call(s32[6,6]{1,0:T(8,128)S(1)} %copy-done.8, bf16[16,4,48,256]{3,2,1,0:T(8,128)(2,1)S(1)} %copy-done.1, bf16[16,4,48,128]{3,2,1,0:T(8,128)(2,1)S(1)} %all-to-all-done.1.refs_1_, f32[1,256]{1,0:T(1,128)S(1)} %bitcast.12, bf16[256,256]{1,0:T(8,128)(2,1)S(1)} %copy-done.5, ...), custom_call_target="tpu_custom_call" | custom-call | flops 28800000000 | bytes 4000000 | tf_op jit(solution)/shard_map/axial_attention/pallas_call | solution.py:340
  136.4 0.0 copy-start.2
  136.4 1.1 copy-done.2
  137.5 0.0 copy-start.9
  137.5 0.0 all-to-all-done.2.refs_0_
  137.5 4.5 %all-to-all-start.3 = ((bf16[16,4,48,256]{3,2,1,0:T(8,128)(2,1)}), bf16[16,4,48,256]{3,2,1,0:T(8,128)(2,1)}, u32[]{:S(2)}, u32[]{:S(2)}) async-start(bf16[16,4,48,256]{3,2,1,0:T(8,128)(2,1)} %copy-done.2), calls=%async_computation.3 | async-start | bytes 3145728 | tf_op jit(solution)/shard_map/all_to_all | solution.py:398
  142.1 0.0 copy-done.9
  142.1 22.8 %axial_attention.3 = bf16[8,6,64,256]{3,2,1,0:T(8,128)(2,1)S(1)} custom-call(s32[4,4]{1,0:T(4,128)S(1)} %copy-done.9, bf16[8,6,64,384]{3,2,1,0:T(8,128)(2,1)S(1)} %all-to-all-done.2.refs_0_, f32[1,256]{1,0:T(1,128)S(1)} %bitcast.13, bf16[256,256]{1,0:T(8,128)(2,1)S(1)} %copy-done.5, bf16[256,256]{1,0:T(8,128)(2,1)S(1)} %copy-done.6, ...), custom_call_target="tpu_custom_call" | custom-call | flops 19200000000 | bytes 4000000 | tf_op jit(solution)/shard_map/axial_attention/pallas_call | solution.py:340
  164.8 0.0 copy-start.3
  164.9 1.2 copy-done.3
  166.0 0.0 all-to-all-done.3
  166.0 26.7 %all_to_all.25 = bf16[8,6,64,256]{3,2,1,0:T(8,128)(2,1)S(1)} all-to-all(bf16[8,6,64,256]{3,2,1,0:T(8,128)(2,1)} %copy-done.3), channel_id=1, replica_groups=mesh['gy'=8,'gx'=16] {'gy'}, dimensions={0} | all-to-all | bytes 3145728 | tf_op jit(solution)/shard_map/all_to_all | solution.py:398
  192.7 2.1 %copy.18.col_ref = bf16[64,48,256]{2,1,0:T(8,128)(2,1)} copy(bf16[64,48,256]{2,0,1:T(8,128)(2,1)S(1)} %bitcast.15) | data formatting | bytes 3145728 | tf_op jit(solution)/shard_map/reshape | solution.py:447
  194.8 7.8 %norm_backward.1 = bf16[64,48,256]{2,1,0:T(8,128)(2,1)} custom-call(bf16[64,48,256]{2,1,0:T(8,128)(2,1)} %tok_ref.1, bf16[64,48,256]{2,1,0:T(8,128)(2,1)} %get-tuple-element.16.mid_ref, bf16[64,48,256]{2,1,0:T(8,128)(2,1)} %bitcast.6.row_ref, bf16[64,48,256]{2,1,0:T(8,128)(2,1)} %copy.18.col_ref, f32[1,256]{1,0:T(1,128)} %bitcast.11), custom_call_target="tpu_custom_call" | custom-call | flops 20000000 | bytes 8000000 | tf_op jit(solution)/shard_map/norm_backward/pallas_call | solution.py:386
  (5 shorter events, 0.0 us)
Async XLA Ops:
  0.9 8.3 %collective-permute-start.1 = (bf16[2,48,512]{2,1,0:T(8,128)(2,1)S(1)}, bf16[2,48,512]{2,1,0:T(8,128)(2,1)S(1)}, u32[]{:S(2)}, u32[]{:S(2)}) collective-permute-start(bf16[2,48,512]{2,1,0:T(8,128)(2,1)S(1)} %pad_maximum_fusion.5), channel_id=1, source_target_pairs={{16,0},{32,16},{48,32},{64,48},{80,64},{96,80},{112,96},{17,1},{33... | collective-permute-start | bytes 294920 | tf_op jit(solution)/shard_map/ppermute | solution.py:409
  4.3 5.2 %collective-permute-start = (bf16[2,48,512]{2,1,0:T(8,128)(2,1)S(1)}, bf16[2,48,512]{2,1,0:T(8,128)(2,1)S(1)}, u32[]{:S(2)}, u32[]{:S(2)}) collective-permute-start(bf16[2,48,512]{2,1,0:T(8,128)(2,1)S(1)} %pad_maximum_fusion.4), channel_id=1, source_target_pairs={{0,16},{16,32},{32,48},{48,64},{64,80},{80,96},{96,112},{1,17},{17... | collective-permute-start | bytes 294920 | tf_op jit(solution)/shard_map/ppermute | solution.py:409
  9.6 13.0 %collective-permute-start.3 = (bf16[68,2,512]{2,1,0:T(2,128)(2,1)S(1)}, bf16[68,2,512]{2,1,0:T(2,128)(2,1)S(1)}, u32[]{:S(2)}, u32[]{:S(2)}) collective-permute-start(bf16[68,2,512]{2,1,0:T(2,128)(2,1)S(1)} %pad_maximum_fusion.3), channel_id=1, source_target_pairs={{0,1},{1,2},{2,3},{3,4},{4,5},{5,6},{6,7},{7,8},{8,9},{9,10},{10,1... | collective-permute-start | bytes 417800 | tf_op jit(solution)/shard_map/ppermute | solution.py:409
  12.9 9.6 %collective-permute-start.2 = (bf16[68,2,512]{2,1,0:T(2,128)(2,1)S(1)}, bf16[68,2,512]{2,1,0:T(2,128)(2,1)S(1)}, u32[]{:S(2)}, u32[]{:S(2)}) collective-permute-start(bf16[68,2,512]{2,1,0:T(2,128)(2,1)S(1)} %pad_maximum_fusion.2), channel_id=1, source_target_pairs={{1,0},{2,1},{3,2},{4,3},{5,4},{6,5},{7,6},{8,7},{9,8},{10,9},{11,1... | collective-permute-start | bytes 417800 | tf_op jit(solution)/shard_map/ppermute | solution.py:409
  14.2 61.1 %all-to-all-start = ((bf16[16,4,48,256]{3,2,1,0:T(8,128)(2,1)}), bf16[16,4,48,256]{3,2,1,0:T(8,128)(2,1)S(1)}, u32[]{:S(2)}, u32[]{:S(2)}) async-start(bf16[16,4,48,256]{3,2,1,0:T(8,128)(2,1)} %bitcast.1), calls=%async_computation | async-start | bytes 3145728 | tf_op jit(solution)/shard_map/all_to_all | solution.py:398
  75.3 6.8 %copy-start.10 = (bf16[64,48,128]{2,1,0:T(8,128)(2,1)S(1)}, bf16[64,48,128]{2,1,0:T(8,128)(2,1)}, u32[]{:S(2)}) copy-start(bf16[64,48,128]{2,1,0:T(8,128)(2,1)} %get-tuple-element.20) | copy-start | bytes 2359300
  75.3 8.5 %copy-start = (bf16[16,4,48,256]{3,2,1,0:T(8,128)(2,1)}, bf16[16,4,48,256]{3,2,1,0:T(8,128)(2,1)S(1)}, u32[]{:S(2)}) copy-start(bf16[16,4,48,256]{3,2,1,0:T(8,128)(2,1)S(1)} %all-to-all-done.refs_0_) | copy-start | bytes 4718596
  75.3 20.5 %all-to-all-start.1 = ((bf16[16,4,48,128]{3,2,1,0:T(8,128)(2,1)}), bf16[16,4,48,128]{3,2,1,0:T(8,128)(2,1)S(1)}, u32[]{:S(2)}, u32[]{:S(2)}) async-start(bf16[16,4,48,128]{3,2,1,0:T(8,128)(2,1)} %bitcast.16), calls=%async_computation.1 | async-start | bytes 1572864 | tf_op jit(solution)/shard_map/all_to_all | solution.py:398
  95.8 6.6 %copy-start.4 = (f32[256]{0:T(256)S(1)}, f32[256]{0:T(256)}, u32[]{:S(2)}) copy-start(f32[256]{0:T(256)} %param.17) | copy-start | bytes 3076
  95.8 6.6 %copy-start.5 = (bf16[256,256]{1,0:T(8,128)(2,1)S(1)}, bf16[256,256]{1,0:T(8,128)(2,1)}, u32[]{:S(2)}) copy-start(bf16[256,256]{1,0:T(8,128)(2,1)} %refs_2_.1) | copy-start | bytes 393220
  95.8 6.6 %copy-start.6 = (bf16[256,256]{1,0:T(8,128)(2,1)S(1)}, bf16[256,256]{1,0:T(8,128)(2,1)}, u32[]{:S(2)}) copy-start(bf16[256,256]{1,0:T(8,128)(2,1)} %refs_3_.3) | copy-start | bytes 393220
  95.8 6.6 %copy-start.7 = (bf16[256,256]{1,0:T(8,128)(2,1)S(1)}, bf16[256,256]{1,0:T(8,128)(2,1)}, u32[]{:S(2)}) copy-start(bf16[256,256]{1,0:T(8,128)(2,1)} %refs_4_.3) | copy-start | bytes 393220
  95.8 6.6 %copy-start.8 = (s32[6,6]{1,0:T(8,128)S(1)}, s32[6,6]{1,0:T(8,128)}, u32[]{:S(2)}) copy-start(s32[6,6]{1,0:T(8,128)} %mask_ref.2) | copy-start | bytes 436
  95.8 41.7 %all-to-all-start.2 = ((bf16[8,6,64,384]{3,2,1,0:T(8,128)(2,1)}), bf16[8,6,64,384]{3,2,1,0:T(8,128)(2,1)S(1)}, u32[]{:S(2)}, u32[]{:S(2)}) async-start(bf16[8,6,64,384]{3,2,1,0:T(8,128)(2,1)} %bitcast.14), calls=%async_computation.2 | async-start | bytes 4718592 | tf_op jit(solution)/shard_map/all_to_all | solution.py:398
  102.4 1.4 copy-start.1
  136.4 1.1 copy-start.2
  137.5 4.5 %copy-start.9 = (s32[4,4]{1,0:T(4,128)S(1)}, s32[4,4]{1,0:T(4,128)}, u32[]{:S(2)}) copy-start(s32[4,4]{1,0:T(4,128)} %mask_ref.3) | copy-start | bytes 196
  137.5 28.5 %all-to-all-start.3 = ((bf16[16,4,48,256]{3,2,1,0:T(8,128)(2,1)}), bf16[16,4,48,256]{3,2,1,0:T(8,128)(2,1)}, u32[]{:S(2)}, u32[]{:S(2)}) async-start(bf16[16,4,48,256]{3,2,1,0:T(8,128)(2,1)} %copy-done.2), calls=%async_computation.3 | async-start | bytes 3145728 | tf_op jit(solution)/shard_map/all_to_all | solution.py:398
  164.8 1.2 copy-start.3

commit v4 on v3

--- a/solution.py
+++ b/solution.py
@@ -41,7 +41,7 @@
     return center * inv, inv
 
 
-def mlp_kernel(rows, cols, mid_ref, gout_ref, rowh_ref, edge_ref, gain_ref, wup_ref, conv_ref, wdown_ref, wout_ref,
+def mlp_kernel(rows, cols, mid_ref, gout_ref, tok_ref, rowh_ref, edge_ref, gain_ref, wup_ref, conv_ref, wdown_ref, wout_ref,
                gm_ref, grow_ref, gcol_ref, x_s, h_s, gp_s, y_s, wdt_s, wut_s, grad_s):
     step = pl.program_id(0)
     width = mid_ref.shape[-1]
@@ -159,24 +159,24 @@
             gm_ref[dst] = res.reshape(BIG, cols, width)
             ga = dot_nt(res, wout_ref[...]).astype(BF16)
             grow_ref[dst] = ga[:, :width // 2].reshape(BIG, cols, width // 2)
-            gcol_ref[dst] = ga[:, width // 2:].reshape(BIG, cols, width // 2)
+            gcol_ref[dst, :, width:] = ga[:, width // 2:].reshape(BIG, cols, width // 2)
+            gcol_ref[dst, :, :width] = tok_ref[dst]
             return c
         lax.fori_loop(0, rows // BIG, finish, 0)
 
 
-def mlp(mid, grad, halo, edge, gain, w_up, conv_kernel, w_down, w_out):
+def mlp(mid, grad, tokens, halo, edge, gain, w_up, conv_kernel, w_down, w_out):
     rows, cols, width = mid.shape
     hidden = w_up.shape[1]
     held = rows + 8
     trips = (rows + 4 + GROUP) // GROUP + 2
     slots = (GROUP * trips + GUARD + 1) * STRIDE
     whole = pl.BlockSpec(memory_space=pltpu.VMEM)
-    half = jax.ShapeDtypeStruct((rows, cols, width // 2), BF16)
     return pl.pallas_call(
         functools.partial(mlp_kernel, rows, cols),
-        out_shape=(jax.ShapeDtypeStruct((rows, cols, width), BF16), half, half),
+        out_shape=tuple(jax.ShapeDtypeStruct((rows, cols, n), BF16) for n in (width, width // 2, width + width // 2)),
         grid=(hidden // FC,),
-        in_specs=[whole, whole, whole, whole, whole,
+        in_specs=[whole, whole, whole, whole, whole, whole,
                   pl.BlockSpec((width, FC), lambda i: (0, i)),
                   pl.BlockSpec((9, FC), lambda i: (0, i)),
                   pl.BlockSpec((FC, width), lambda i: (i, 0)),
@@ -194,12 +194,14 @@
         compiler_params=pltpu.CompilerParams(vmem_limit_bytes=60 * 1024 * 1024),
         cost_estimate=pl.CostEstimate(flops=20_000_000_000, transcendentals=4_000_000, bytes_accessed=12_000_000),
         name="mlp_backward",
-    )(mid, grad, halo, edge, gain.reshape(1, -1), w_up, conv_kernel, w_down, w_out)
-
-
-def attn_kernel(nl, nk, half, split, mask_ref, *refs):
-    (x_ref, g_ref, gain_ref, wq_ref, wk_ref, wv_ref, out_ref, w_s, wt_s,
-     q_s, k_s, v_s, g_s, kt_s, qmt_s, qm_s, gmt_s, gm_s, e_s, dp_s, st_s, dq_s, dk_s, dv_s) = refs if not split else refs[:1] + refs[:1] + refs[1:]
+    )(mid, grad, tokens, halo, edge, gain.reshape(1, -1), w_up, conv_kernel, w_down, w_out)
+
+
+def attn_kernel(nl, nk, half, pieces, mask_ref, at_ref, *refs):
+    x_ref, g_ref = refs[:2]
+    piece_refs = refs[:pieces]
+    (gain_ref, wq_ref, wk_ref, wv_ref, out_ref, w_s, wt_s, q_s, k_s, v_s, g_s, kt_s, qmt_s, qm_s, gmt_s, gm_s,
+     e_s, dp_s, st_s, dq_s, dk_s, dv_s) = refs[max(pieces, 2):]
     heads = HEADS // 2
     hw = 128
     hd = hw // heads
@@ -218,22 +220,34 @@
         w_s[:, j * hw:(j + 1) * hw] = part
         wt_s[j * hw:(j + 1) * hw, :] = part.astype(F32).T.astype(BF16)
 
-    def prepare(line, carry):
-        xv = (x_ref[:, line, :, :2 * hw] if split else x_ref[:, line]).reshape(length, 2 * hw).astype(F32)
-        mean = jnp.mean(xv, axis=-1, keepdims=True)
-        center = xv - mean
-        inv = lax.rsqrt(jnp.mean(center * center, axis=-1, keepdims=True) + EPSILON)
-        normed = (center * inv * gain).astype(BF16)
-        qkv = jnp.dot(normed, w_s[...], preferred_element_type=F32)
-        kf = qkv[:, hw:2 * hw]
-        q_s[line] = (qkv[:, :hw] * (factor * LOG2E)).astype(BF16)
-        k_s[line] = kf.astype(BF16)
-        v_s[line] = qkv[:, 2 * hw:].astype(BF16)
-        kt_s[line] = kf.T.astype(BF16)
-        g_s[line] = (g_ref[:, line, :, 2 * hw:] if split else g_ref[:, line]).reshape(length, hw)
+    def project(xv):
+        normed = (normalize(xv.astype(F32))[0] * gain).astype(BF16)
+        return jnp.dot(normed, w_s[...], preferred_element_type=F32)
+
+    def keep(line, where, qkv, grads):
+        q_s[line, where, :] = (qkv[:, :hw] * (factor * LOG2E)).astype(BF16)
+        k_s[line, where, :] = qkv[:, hw:2 * hw].astype(BF16)
+        v_s[line, where, :] = qkv[:, 2 * hw:].astype(BF16)
+        g_s[line, where, :] = grads
+
+    if pieces:
+        span = out_ref.shape[2]
+        for piece, ref in enumerate(piece_refs):
+            where = pl.ds(pl.multiple_of(at_ref[piece] * span, span), span)
+            qkv = project(ref[:, :, :2 * hw].reshape(nl * span, 2 * hw))
+            for line in range(nl):
+                keep(line, where, qkv[line * span:(line + 1) * span], ref[line, :, 2 * hw:])
+    else:
+        def prepare(line, carry):
+            keep(line, slice(None), project(x_ref[:, line].reshape(length, 2 * hw)),
+                 g_ref[:, line].reshape(length, hw))
+            return carry
+        lax.fori_loop(0, nl, prepare, 0)
+
+    def turn(line, carry):
+        kt_s[line] = k_s[line].astype(F32).T.astype(BF16)
         return carry
-
-    lax.fori_loop(0, nl, prepare, 0)
+    lax.fori_loop(0, nl, turn, 0)
     lane = lax.broadcasted_iota(jnp.int32, (BLK, hw), 1)
 
     def query_block(qb, carry):
@@ -327,8 +341,9 @@
     lax.fori_loop(0, nl, finish, 0)
 
 
-def attention(arrays, gain, w_query, w_key, w_value, mask, half):
-    srcs, nl, span = arrays[0].shape[:3]
+def attention(arrays, at, shape, gain, w_query, w_key, w_value, mask, half):
+    srcs, nl, span = shape
+    pieces = srcs if len(arrays) == srcs else 0
     width = w_query.shape[0]
     length = srcs * span
     nk = length // BLK
@@ -338,9 +353,9 @@
     vm = pl.BlockSpec(memory_space=pltpu.VMEM)
     pairs = nk * nk * nl
     return pl.pallas_call(
-        functools.partial(attn_kernel, nl, nk, half, len(arrays) == 1),
+        functools.partial(attn_kernel, nl, nk, half, pieces),
         out_shape=jax.ShapeDtypeStruct((srcs, nl, span, width), BF16),
-        in_specs=[pl.BlockSpec(memory_space=pltpu.SMEM)] + [vm] * (len(arrays) + 4),
+        in_specs=[pl.BlockSpec(memory_space=pltpu.SMEM)] * 2 + [vm] * (len(arrays) + 4),
         out_specs=vm,
         scratch_shapes=[
             pltpu.VMEM((width, 3 * hw), BF16),
@@ -364,7 +379,7 @@
         compiler_params=pltpu.CompilerParams(vmem_limit_bytes=40 * 1024 * 1024),
         cost_estimate=pl.CostEstimate(flops=pairs * 200_000_000, transcendentals=pairs * 65536, bytes_accessed=4_000_000),
         name="axial_attention",
-    )(mask, *arrays, gain.reshape(1, -1), w_query, w_key, w_value)
+    )(mask, at, *arrays, gain.reshape(1, -1), w_query, w_key, w_value)
 
 
 def final_kernel(tok_ref, mid_ref, row_ref, col_ref, gain_ref, out_ref):
@@ -431,18 +446,26 @@
         jnp.pad(left, ((1, 5), (0, 0), (0, 0)))], axis=1)
     halo = jnp.concatenate([above, below], axis=0)
     grad_mid, grad_row, grad_col = mlp(
-        saved_mid, grad_out, halo, edge, mlp_gain, w_up, conv_kernel, w_down, w_out)
+        saved_mid, grad_out, tokens_in, halo, edge, mlp_gain, w_up, conv_kernel, w_down, w_out)
     hold = lax.optimization_barrier
     grad_row, row_tokens = hold((grad_row, row_tokens))
     grad_row = to_lines(grad_row.reshape(count_gx, rows // count_gx, cols, half), "gx")
-    col_send = cut_cols(jnp.concatenate([tokens_in, grad_col], axis=-1), count_gy)
-    grad_row, col_send = hold((grad_row, col_send))
-    col_lines = to_lines(col_send, "gy")
+    here = lax.axis_index("gy")
+    col_send = cut_cols(grad_col, count_gy)
+    col_parts = []
+    for ahead in range(count_gy):
+        part = lax.dynamic_index_in_dim(col_send, (here + ahead) % count_gy, 0, keepdims=False)
+        if ahead:
+            part = lax.ppermute(part, "gy", [(i, (i + ahead) % count_gy) for i in range(count_gy)])
+        col_parts.append(part)
+    col_at = (here - jnp.arange(count_gy, dtype=jnp.int32)) % count_gy
     weights = (w_query, w_key, w_value)
-    row_out = attention((row_tokens, grad_row), attn_gain, *weights, row_mask, 0)
-    row_out, col_lines = hold((row_out, col_lines))
+    row_out = attention((row_tokens, grad_row), col_at, (count_gx, rows // count_gx, cols), attn_gain, *weights,
+                        row_mask, 0)
+    row_out, *col_parts = hold((row_out, *col_parts))
     row_back = to_lines(row_out, "gx").reshape(rows, cols, width)
-    col_out = attention((col_lines,), attn_gain, *weights, col_mask, 1)
+    col_out = attention(tuple(col_parts), col_at, (count_gy, cols // count_gy, rows), attn_gain, *weights,
+                        col_mask, 1)
     row_back, col_out = hold((row_back, col_out))
     col_back = jnp.transpose(to_lines(col_out, "gy"), (2, 0, 1, 3)).reshape(rows, cols, width)
     return final(tokens_in, grad_mid, row_back, col_back, attn_gain)

time: 207 us -> 206 us (level); the launches traced: 203 us -> 207 us
  waiting for transfers between devices: 10.2 us -> 4.74 us
  Pallas kernels: 114 us -> 119 us
  starting transfers between devices: 36.8 us -> 41.8 us
    all_to_all x4 -> x3, waiting for transfers between devices: 10 us -> 0.98 us  [to_lines(): return lax.all_to_all(blocks, axis, split_axis=0, concat_axis=0, tiled=True)]
    ppermute x0 -> x7, starting transfers between devices: none -> 8.23 us  [per_device(): lax.ppermute(part, 'gy', [(i, (i + ahead) % count_gy) for i in range(coun...]
    pallas_call x3, Pallas kernels: 107 us -> 112 us  [the longest x2 59.3 us: attention(): pl.pallas_call(functools.partial(attn_kernel, nl, nk, half, pieces), out_...]
    all_to_all x4 -> x3, starting transfers between devices: 25.4 us -> 21.5 us  [to_lines(): return lax.all_to_all(blocks, axis, split_axis=0, concat_axis=0, tiled=True)]
    ppermute x2, waiting for transfers between devices: 0.01 us -> 2.57 us  [neighbours(): lax.ppermute(behind, axis, [(j, i) for i, j in up])]
    pallas_call x0 -> x1, local copies, waits for them, and re-layouts: none -> 2.26 us  [mlp(): pl.pallas_call(functools.partial(mlp_kernel, rows, cols), out_shape=tuple...]
    ppermute x2, starting transfers between devices: 6.73 us -> 8.93 us  [neighbours(): lax.ppermute(ahead, axis, up)]
  transfers between devices with their start and end apart: 8 -> 14, of which waited for: 2 -> 3; matrix products, arithmetic and copies ran while one was open for 4% -> 4% of each run, Pallas kernels for 53% -> 54%
where the time goes in v4:
time: 206 us; the launch traced here: 207 us
  Pallas kernels  119 us (58%)
  starting transfers between devices  41.8 us (20%)
  blocking collectives  27.8 us (13%)
  local copies, waits for them, and re-layouts  10.7 us (5%)
  waiting for transfers between devices  4.74 us (2%)
  other arithmetic  2.49 us (1%)
    pallas_call x2, Pallas kernels, attention(): pl.pallas_call(functools.partial(attn_kernel, nl, nk, half, pieces), out_...  59.3 us
    pallas_call x1, Pallas kernels, mlp(): pl.pallas_call(functools.partial(mlp_kernel, rows, cols), out_shape=tuple...  52.3 us
    all_to_all x1, blocking collectives, to_lines(): return lax.all_to_all(blocks, axis, split_axis=0, concat_axis=0, tiled=True)  27.8 us
    all_to_all x3, starting transfers between devices, to_lines(): return lax.all_to_all(blocks, axis, split_axis=0, concat_axis=0, tiled=True)  21.5 us
    ppermute x2, starting transfers between devices, neighbours(): lax.ppermute(ahead, axis, up)  8.93 us
    ppermute x7, starting transfers between devices, per_device(): lax.ppermute(part, 'gy', [(i, (i + ahead) % count_gy) for i in range(coun...  8.23 us
    pallas_call x1, Pallas kernels, final(): pl.pallas_call(final_kernel, out_shape=jax.ShapeDtypeStruct(tokens.shape,...  7.75 us
  transfers between devices with their start and end apart: 14, of which 3 were waited for; matrix products, arithmetic and copies ran while one was open for 4% of the time, Pallas kernels for 54%

profile of v4, /device:TPU:1, one launch (start us, length us, event | category | flops | bytes accessed | tf_op | source)
XLA Modules:
  0.0 207.3 jit_solution(6255880079841629917)
XLA Ops:
  0.0 0.9 fusion.7
  0.9 4.9 %collective-permute-start = (bf16[2,48,512]{2,1,0:T(8,128)(2,1)S(1)}, bf16[2,48,512]{2,1,0:T(8,128)(2,1)S(1)}, u32[]{:S(2)}, u32[]{:S(2)}) collective-permute-start(bf16[2,48,512]{2,1,0:T(8,128)(2,1)S(1)} %pad_maximum_fusion.3), channel_id=1, source_target_pairs={{0,16},{16,32},{32,48},{48,64},{64,80},{80,96},{96,112},{1,17},{17... | collective-permute-start | bytes 294920 | tf_op jit(solution)/shard_map/ppermute | solution.py:424
  5.9 1.9 collective-permute-start.1
  7.8 1.4 fusion.5
  9.2 0.0 collective-permute-done
  9.2 2.6 %collective-permute-done.1 = bf16[2,48,512]{2,1,0:T(8,128)(2,1)S(1)} collective-permute-done((bf16[2,48,512]{2,1,0:T(8,128)(2,1)S(1)}, bf16[2,48,512]{2,1,0:T(8,128)(2,1)S(1)}, u32[]{:S(2)}, u32[]{:S(2)}) %collective-permute-start.1) | collective-permute-done | bytes 98336 | tf_op jit(solution)/shard_map/ppermute | solution.py:424
  11.8 0.1 pad_maximum_fusion.1
  11.9 1.3 collective-permute-start.2
  13.2 0.1 pad_maximum_fusion.2
  13.4 4.0 %collective-permute-start.3 = (bf16[68,2,512]{2,1,0:T(2,128)(2,1)S(1)}, bf16[68,2,512]{2,1,0:T(2,128)(2,1)S(1)}, u32[]{:S(2)}, u32[]{:S(2)}) collective-permute-start(bf16[68,2,512]{2,1,0:T(2,128)(2,1)S(1)} %pad_maximum_fusion.2), channel_id=1, source_target_pairs={{0,1},{1,2},{2,3},{3,4},{4,5},{5,6},{6,7},{7,8},{8,9},{9,10},{10,1... | collective-permute-start | bytes 417800 | tf_op jit(solution)/shard_map/ppermute | solution.py:424
  17.4 8.7 %all-to-all-start = ((bf16[16,4,48,256]{3,2,1,0:T(8,128)(2,1)}), bf16[16,4,48,256]{3,2,1,0:T(8,128)(2,1)S(1)}, u32[]{:S(2)}, u32[]{:S(2)}) async-start(bf16[16,4,48,256]{3,2,1,0:T(8,128)(2,1)} %bitcast.1), calls=%async_computation | async-start | bytes 3145728 | tf_op jit(solution)/shard_map/all_to_all | solution.py:413
  26.1 0.1 pad.11.clone
  26.2 0.7 pad_maximum_fusion.rowh_ref
  26.9 0.0 collective-permute-done.2
  26.9 0.0 collective-permute-done.3
  26.9 1.5 fusion.2.edge_ref
  28.4 52.3 %mlp_backward.1 = (bf16[64,48,256]{2,1,0:T(8,128)(2,1)}, bf16[64,48,128]{2,1,0:T(8,128)(2,1)}, bf16[64,48,384]{2,1,0:T(8,128)(2,1)}) custom-call(bf16[64,48,256]{2,1,0:T(8,128)(2,1)} %mid_ref.1, bf16[64,48,256]{2,1,0:T(8,128)(2,1)} %gout_ref.1, bf16[64,48,256]{2,1,0:T(8,128)(2,1)} %tok_ref.3, bf16[4,48,512]{2,1,0:T(8,128)(2,1)} %pad_maximum_fusion.rowh_ref, ...), custom_call_target="tpu_custom_call" | custom-call | flops 20000000000 | bytes 12000000 | tf_op jit(solution)/shard_map/mlp_backward/pallas_call | solution.py:175
  80.7 0.0 all-to-all-done.refs_0_
  80.7 6.7 %all-to-all-start.1 = ((bf16[16,4,48,128]{3,2,1,0:T(8,128)(2,1)}), bf16[16,4,48,128]{3,2,1,0:T(8,128)(2,1)S(1)}, u32[]{:S(2)}, u32[]{:S(2)}) async-start(bf16[16,4,48,128]{3,2,1,0:T(8,128)(2,1)} %bitcast.46), calls=%async_computation.1 | async-start | bytes 1572864 | tf_op jit(solution)/shard_map/all_to_all | solution.py:413
  87.5 2.3 %copy.17 = bf16[64,48,384]{2,0,1:T(8,128)(2,1)S(1)} copy(bf16[64,48,384]{2,1,0:T(8,128)(2,1)} %get-tuple-element.25) | data formatting | bytes 4718592 | tf_op jit(solution)/shard_map/mlp_backward/pallas_call | solution.py:175
  89.8 0.0 copy-start
  89.8 0.0 copy-start.7
  89.8 1.2 dynamic-slice_bitcast_fusion
  91.0 0.0 collective-permute-start.10
  91.0 1.7 collective-permute-start.4
  92.8 1.6 collective-permute-start.5
  94.4 2.1 collective-permute-start.6
  96.5 0.0 collective-permute-start.7
  96.5 1.2 collective-permute-done.10.refs_7_
  97.6 2.3 %collective-permute-start.8 = (bf16[6,64,384]{2,1,0:T(8,128)(2,1)}, bf16[6,64,384]{2,1,0:T(8,128)(2,1)}, u32[]{:S(2)}, u32[]{:S(2)}) collective-permute-start(bf16[6,64,384]{2,1,0:T(8,128)(2,1)} %get-tuple-element.39), channel_id=1, source_target_pairs={{0,80},{16,96},{32,112},{48,0},{64,16},{80,32},{96,48},{112,64},{1... | collective-permute-start | bytes 884744 | tf_op jit(solution)/shard_map/ppermute | solution.py:459
  100.0 0.0 collective-permute-done.4.refs_1_
  100.0 0.4 collective-permute-start.9
  100.4 1.0 all-to-all-done.1.refs_1_
  101.4 0.0 copy-done
  101.4 0.0 copy-done.7
  101.4 0.0 copy-start.1
  101.4 0.9 copy-done.1
  102.3 0.0 copy-start.3
  102.3 0.9 copy-done.3
  103.2 0.0 copy-start.5
  103.2 0.9 copy-done.5
  104.1 38.3 %axial_attention.2 = bf16[16,4,48,256]{3,2,1,0:T(8,128)(2,1)} custom-call(s32[6,6]{1,0:T(8,128)S(1)} %copy-done.7, s32[8]{0:T(128)S(1)} %and_select_fusion.at_ref, bf16[16,4,48,256]{3,2,1,0:T(8,128)(2,1)S(1)} %all-to-all-done.refs_0_, bf16[16,4,48,128]{3,2,1,0:T(8,128)(2,1)S(1)} %all-to-all-done.1.refs_1_, f32[1,256]{1,0:T(1,128)S(1)} %bitcast.42, ...), custom_call_target="tpu_custom_call" | custom-call | flops 28800000000 | bytes 4000000 | tf_op jit(solution)/shard_map/axial_attention/pallas_call | solution.py:355
  142.5 0.0 collective-permute-done.5.refs_2_
  142.5 0.0 collective-permute-done.6.refs_3_
  142.5 0.0 collective-permute-done.7.refs_4_
  142.5 0.0 collective-permute-done.8.refs_5_
  142.5 0.0 collective-permute-done.9.refs_6_
  142.5 0.0 copy-start.2
  142.5 0.0 copy-start.4
  142.5 0.0 copy-start.6
  142.5 0.0 copy-start.8
  142.6 6.1 %all-to-all-start.2 = ((bf16[16,4,48,256]{3,2,1,0:T(8,128)(2,1)}), bf16[16,4,48,256]{3,2,1,0:T(8,128)(2,1)}, u32[]{:S(2)}, u32[]{:S(2)}) async-start(bf16[16,4,48,256]{3,2,1,0:T(8,128)(2,1)} %axial_attention.2), calls=%async_computation.2 | async-start | bytes 3145728 | tf_op jit(solution)/shard_map/all_to_all | solution.py:413
  148.7 0.0 copy-done.2
  148.7 0.0 copy-done.4
  148.7 0.0 copy-done.6
  148.7 0.0 copy-done.8
  148.7 20.9 %axial_attention.3 = bf16[8,6,64,256]{3,2,1,0:T(8,128)(2,1)S(1)} custom-call(s32[4,4]{1,0:T(4,128)S(1)} %copy-done.8, s32[8]{0:T(128)S(1)} %and_select_fusion.at_ref, bf16[6,64,384]{2,1,0:T(8,128)(2,1)S(1)} %get-tuple-element.27.refs_0_, bf16[6,64,384]{2,1,0:T(8,128)(2,1)S(1)} %collective-permute-done.4.refs_1_, ...), custom_call_target="tpu_custom_call" | custom-call | flops 19200000000 | bytes 4000000 | tf_op jit(solution)/shard_map/axial_attention/pallas_call | solution.py:355
  169.7 0.0 all-to-all-done.2
  169.7 27.8 %all_to_all.20 = bf16[8,6,64,256]{3,2,1,0:T(8,128)(2,1)S(1)} all-to-all(bf16[8,6,64,256]{3,2,1,0:T(8,128)(2,1)S(1)} %axial_attention.3), channel_id=1, replica_groups=mesh['gy'=8,'gx'=16] {'gy'}, dimensions={0} | all-to-all | bytes 3145728 | tf_op jit(solution)/shard_map/all_to_all | solution.py:413
  197.5 2.0 copy.18.col_ref
  199.5 7.8 %norm_backward.1 = bf16[64,48,256]{2,1,0:T(8,128)(2,1)} custom-call(bf16[64,48,256]{2,1,0:T(8,128)(2,1)} %tok_ref.3, bf16[64,48,256]{2,1,0:T(8,128)(2,1)} %get-tuple-element.21.mid_ref, bf16[64,48,256]{2,1,0:T(8,128)(2,1)} %bitcast.21.row_ref, bf16[64,48,256]{2,1,0:T(8,128)(2,1)} %copy.18.col_ref, f32[1,256]{1,0:T(1,128)} %bitcast.41), custom_call_target="tpu_custom_call" | custom-call | flops 20000000 | bytes 8000000 | tf_op jit(solution)/shard_map/norm_backward/pallas_call | solution.py:401
  (6 shorter events, 0.1 us)
Async XLA Ops:
  0.9 8.3 %collective-permute-start = (bf16[2,48,512]{2,1,0:T(8,128)(2,1)S(1)}, bf16[2,48,512]{2,1,0:T(8,128)(2,1)S(1)}, u32[]{:S(2)}, u32[]{:S(2)}) collective-permute-start(bf16[2,48,512]{2,1,0:T(8,128)(2,1)S(1)} %pad_maximum_fusion.3), channel_id=1, source_target_pairs={{0,16},{16,32},{32,48},{48,64},{64,80},{80,96},{96,112},{1,17},{17... | collective-permute-start | bytes 294920 | tf_op jit(solution)/shard_map/ppermute | solution.py:424
  5.9 5.9 %collective-permute-start.1 = (bf16[2,48,512]{2,1,0:T(8,128)(2,1)S(1)}, bf16[2,48,512]{2,1,0:T(8,128)(2,1)S(1)}, u32[]{:S(2)}, u32[]{:S(2)}) collective-permute-start(bf16[2,48,512]{2,1,0:T(8,128)(2,1)S(1)} %pad_maximum_fusion.4), channel_id=1, source_target_pairs={{16,0},{32,16},{48,32},{64,48},{80,64},{96,80},{112,96},{17,1},{33... | collective-permute-start | bytes 294920 | tf_op jit(solution)/shard_map/ppermute | solution.py:424
  11.9 14.9 %collective-permute-start.2 = (bf16[68,2,512]{2,1,0:T(2,128)(2,1)S(1)}, bf16[68,2,512]{2,1,0:T(2,128)(2,1)S(1)}, u32[]{:S(2)}, u32[]{:S(2)}) collective-permute-start(bf16[68,2,512]{2,1,0:T(2,128)(2,1)S(1)} %pad_maximum_fusion.1), channel_id=1, source_target_pairs={{1,0},{2,1},{3,2},{4,3},{5,4},{6,5},{7,6},{8,7},{9,8},{10,9},{11,1... | collective-permute-start | bytes 417800 | tf_op jit(solution)/shard_map/ppermute | solution.py:424
  13.4 13.5 %collective-permute-start.3 = (bf16[68,2,512]{2,1,0:T(2,128)(2,1)S(1)}, bf16[68,2,512]{2,1,0:T(2,128)(2,1)S(1)}, u32[]{:S(2)}, u32[]{:S(2)}) collective-permute-start(bf16[68,2,512]{2,1,0:T(2,128)(2,1)S(1)} %pad_maximum_fusion.2), channel_id=1, source_target_pairs={{0,1},{1,2},{2,3},{3,4},{4,5},{5,6},{6,7},{7,8},{8,9},{9,10},{10,1... | collective-permute-start | bytes 417800 | tf_op jit(solution)/shard_map/ppermute | solution.py:424
  17.4 63.3 %all-to-all-start = ((bf16[16,4,48,256]{3,2,1,0:T(8,128)(2,1)}), bf16[16,4,48,256]{3,2,1,0:T(8,128)(2,1)S(1)}, u32[]{:S(2)}, u32[]{:S(2)}) async-start(bf16[16,4,48,256]{3,2,1,0:T(8,128)(2,1)} %bitcast.1), calls=%async_computation | async-start | bytes 3145728 | tf_op jit(solution)/shard_map/all_to_all | solution.py:413
  80.7 20.7 %all-to-all-start.1 = ((bf16[16,4,48,128]{3,2,1,0:T(8,128)(2,1)}), bf16[16,4,48,128]{3,2,1,0:T(8,128)(2,1)S(1)}, u32[]{:S(2)}, u32[]{:S(2)}) async-start(bf16[16,4,48,128]{3,2,1,0:T(8,128)(2,1)} %bitcast.46), calls=%async_computation.1 | async-start | bytes 1572864 | tf_op jit(solution)/shard_map/all_to_all | solution.py:413
  89.8 11.6 %copy-start = (f32[256]{0:T(256)S(1)}, f32[256]{0:T(256)}, u32[]{:S(2)}) copy-start(f32[256]{0:T(256)} %param.17) | copy-start | bytes 3076
  89.8 11.6 %copy-start.7 = (s32[6,6]{1,0:T(8,128)S(1)}, s32[6,6]{1,0:T(8,128)}, u32[]{:S(2)}) copy-start(s32[6,6]{1,0:T(8,128)} %mask_ref.2) | copy-start | bytes 436
  91.0 6.6 %collective-permute-start.10 = (bf16[6,64,384]{2,1,0:T(8,128)(2,1)S(1)}, bf16[6,64,384]{2,1,0:T(8,128)(2,1)S(1)}, u32[]{:S(2)}, u32[]{:S(2)}) collective-permute-start(bf16[6,64,384]{2,1,0:T(8,128)(2,1)S(1)} %get-tuple-element.37), channel_id=1, source_target_pairs={{0,112},{16,0},{32,16},{48,32},{64,48},{80,64},{96,80},{112,96},{1... | collective-permute-start | bytes 884744 | tf_op jit(solution)/shard_map/ppermute | solution.py:459
  91.0 9.0 %collective-permute-start.4 = (bf16[6,64,384]{2,1,0:T(8,128)(2,1)S(1)}, bf16[6,64,384]{2,1,0:T(8,128)(2,1)S(1)}, u32[]{:S(2)}, u32[]{:S(2)}) collective-permute-start(bf16[6,64,384]{2,1,0:T(8,128)(2,1)S(1)} %get-tuple-element.43), channel_id=1, source_target_pairs={{0,16},{16,32},{32,48},{48,64},{64,80},{80,96},{96,112},{112,0},{1... | collective-permute-start | bytes 884744 | tf_op jit(solution)/shard_map/ppermute | solution.py:459
  92.8 49.7 %collective-permute-start.5 = (bf16[6,64,384]{2,1,0:T(8,128)(2,1)}, bf16[6,64,384]{2,1,0:T(8,128)(2,1)S(1)}, u32[]{:S(2)}, u32[]{:S(2)}) collective-permute-start(bf16[6,64,384]{2,1,0:T(8,128)(2,1)} %get-tuple-element.42), channel_id=1, source_target_pairs={{0,32},{16,48},{32,64},{48,80},{64,96},{80,112},{96,0},{112,16},{1... | collective-permute-start | bytes 884744 | tf_op jit(solution)/shard_map/ppermute | solution.py:459
  94.4 48.1 %collective-permute-start.6 = (bf16[6,64,384]{2,1,0:T(8,128)(2,1)}, bf16[6,64,384]{2,1,0:T(8,128)(2,1)}, u32[]{:S(2)}, u32[]{:S(2)}) collective-permute-start(bf16[6,64,384]{2,1,0:T(8,128)(2,1)} %get-tuple-element.41), channel_id=1, source_target_pairs={{0,48},{16,64},{32,80},{48,96},{64,112},{80,0},{96,16},{112,32},{1... | collective-permute-start | bytes 884744 | tf_op jit(solution)/shard_map/ppermute | solution.py:459
  96.5 46.0 %collective-permute-start.7 = (bf16[6,64,384]{2,1,0:T(8,128)(2,1)}, bf16[6,64,384]{2,1,0:T(8,128)(2,1)}, u32[]{:S(2)}, u32[]{:S(2)}) collective-permute-start(bf16[6,64,384]{2,1,0:T(8,128)(2,1)} %get-tuple-element.40), channel_id=1, source_target_pairs={{0,64},{16,80},{32,96},{48,112},{64,0},{80,16},{96,32},{112,48},{1... | collective-permute-start | bytes 884744 | tf_op jit(solution)/shard_map/ppermute | solution.py:459
  97.6 44.8 %collective-permute-start.8 = (bf16[6,64,384]{2,1,0:T(8,128)(2,1)}, bf16[6,64,384]{2,1,0:T(8,128)(2,1)}, u32[]{:S(2)}, u32[]{:S(2)}) collective-permute-start(bf16[6,64,384]{2,1,0:T(8,128)(2,1)} %get-tuple-element.39), channel_id=1, source_target_pairs={{0,80},{16,96},{32,112},{48,0},{64,16},{80,32},{96,48},{112,64},{1... | collective-permute-start | bytes 884744 | tf_op jit(solution)/shard_map/ppermute | solution.py:459
  100.0 42.5 %collective-permute-start.9 = (bf16[6,64,384]{2,1,0:T(8,128)(2,1)}, bf16[6,64,384]{2,1,0:T(8,128)(2,1)}, u32[]{:S(2)}, u32[]{:S(2)}) collective-permute-start(bf16[6,64,384]{2,1,0:T(8,128)(2,1)} %get-tuple-element.38), channel_id=1, source_target_pairs={{0,96},{16,112},{32,0},{48,16},{64,32},{80,48},{96,64},{112,80},{1... | collective-permute-start | bytes 884744 | tf_op jit(solution)/shard_map/ppermute | solution.py:459
  101.4 0.9 copy-start.1
  102.3 0.9 copy-start.3
  103.2 0.9 copy-start.5
  142.5 6.2 %copy-start.2 = (bf16[256,256]{1,0:T(8,128)(2,1)S(1)}, bf16[256,256]{1,0:T(8,128)(2,1)}, u32[]{:S(2)}) copy-start(bf16[256,256]{1,0:T(8,128)(2,1)} %refs_9_.1) | copy-start | bytes 393220
  142.5 6.2 %copy-start.4 = (bf16[256,256]{1,0:T(8,128)(2,1)S(1)}, bf16[256,256]{1,0:T(8,128)(2,1)}, u32[]{:S(2)}) copy-start(bf16[256,256]{1,0:T(8,128)(2,1)} %refs_10_.1) | copy-start | bytes 393220
  142.5 6.2 %copy-start.6 = (bf16[256,256]{1,0:T(8,128)(2,1)S(1)}, bf16[256,256]{1,0:T(8,128)(2,1)}, u32[]{:S(2)}) copy-start(bf16[256,256]{1,0:T(8,128)(2,1)} %refs_11_.1) | copy-start | bytes 393220
  142.5 6.2 %copy-start.8 = (s32[4,4]{1,0:T(4,128)S(1)}, s32[4,4]{1,0:T(4,128)}, u32[]{:S(2)}) copy-start(s32[4,4]{1,0:T(4,128)} %mask_ref.3) | copy-start | bytes 196
  142.6 27.1 %all-to-all-start.2 = ((bf16[16,4,48,256]{3,2,1,0:T(8,128)(2,1)}), bf16[16,4,48,256]{3,2,1,0:T(8,128)(2,1)}, u32[]{:S(2)}, u32[]{:S(2)}) async-start(bf16[16,4,48,256]{3,2,1,0:T(8,128)(2,1)} %axial_attention.2), calls=%async_computation.2 | async-start | bytes 3145728 | tf_op jit(solution)/shard_map/all_to_all | solution.py:413

commit v5 on v4

--- a/solution.py
+++ b/solution.py
@@ -16,11 +16,12 @@
 F32 = jnp.float32
 BF16 = jnp.bfloat16
 STRIDE = 64
-GROUP = 4
+GROUP = 8
 CHUNK = GROUP * STRIDE
 BIG = 8
 GUARD = 2 * GROUP + 4
-FC = 256
+RING = 3 * GROUP
+FC = 512
 
 
 def dot_nt(a, b):
@@ -43,7 +44,6 @@
 
 def mlp_kernel(rows, cols, mid_ref, gout_ref, tok_ref, rowh_ref, edge_ref, gain_ref, wup_ref, conv_ref, wdown_ref, wout_ref,
                gm_ref, grow_ref, gcol_ref, x_s, h_s, gp_s, y_s, wdt_s, wut_s, grad_s):
-    step = pl.program_id(0)
     width = mid_ref.shape[-1]
     gain = gain_ref[...]
     held = rows + 8
@@ -53,116 +53,134 @@
     def rows_at(row):
         return pl.multiple_of(row * STRIDE, STRIDE)
 
-    @pl.when(step == 0)
-    def _():
-        edges = STRIDE - cols
-
-        def place(ref, lead, row, values, count):
-            for j in range(values.shape[0] // count):
-                start = (row + j) * STRIDE + (0 if count == cols else cols)
-                ref[lead + (pl.ds(pl.multiple_of(start, 16), count), slice(None))] = values[j * count:(j + 1) * count]
-
-        def scaled(values):
-            return normalize(values.astype(F32))[0] * gain
-
-        none = jnp.zeros((cols, width), F32)
-        for row in (0, 1, rows + 6, rows + 7, rows + 8, rows + 9):
-            place(y_s, (0,), row, none, cols)
-            place(grad_s, (), row, none.astype(BF16), cols)
-        halo = rowh_ref[...].reshape(4 * cols, 2 * width)
-        for part, row in ((0, 2), (1, rows + 4)):
-            values = halo[part * 2 * cols:(part + 1) * 2 * cols]
-            place(y_s, (0,), row, scaled(values[:, :width]), cols)
-            place(grad_s, (), row, values[:, width:], cols)
-
-        def edge_block(i, c):
-            n = (rows + 10) // 2
-            values = edge_ref[pl.ds(i * n, n)].reshape(n * edges, 2 * width)
-            place(y_s, (0,), i * n, scaled(values[:, :width]), edges)
-            place(grad_s, (), i * n, values[:, width:], edges)
-            return c
-        lax.fori_loop(0, 2, edge_block, 0)
-
-        def norm_block(i, c):
-            src = pl.ds(i * BIG, BIG)
-            place(y_s, (0,), i * BIG + 4, scaled(mid_ref[src].reshape(BIG * cols, width)), cols)
-            place(grad_s, (), i * BIG + 4, gout_ref[src].reshape(BIG * cols, width), cols)
-            return c
-        lax.fori_loop(0, rows // BIG, norm_block, 0)
-
-        def shift_block(i, c):
-            at = rows_at(i * BIG + 1)
-            xv = y_s[0, pl.ds(at, tall + 8), :]
-            lv = y_s[0, pl.ds(at - 8, tall + 8), :]
-            dst = pl.ds(rows_at(i * BIG), tall)
-            x_s[0, dst, :] = lv[7:7 + tall].astype(BF16)
-            x_s[1, dst, :] = xv[:tall].astype(BF16)
-            x_s[2, dst, :] = xv[1:1 + tall].astype(BF16)
-            return c
-        lax.fori_loop(0, held // BIG, shift_block, 0)
+    edges = STRIDE - cols
+
+    def place(ref, lead, row, values, count):
+        for j in range(values.shape[0] // count):
+            start = (row + j) * STRIDE + (0 if count == cols else cols)
+            ref[lead + (pl.ds(pl.multiple_of(start, 16), count), slice(None))] = values[j * count:(j + 1) * count]
+
+    def scaled(values):
+        return normalize(values.astype(F32))[0] * gain
+
+    none = jnp.zeros((cols, width), F32)
+    for row in (0, 1, rows + 6, rows + 7, rows + 8, rows + 9):
+        place(y_s, (0,), row, none, cols)
+        place(grad_s, (), row, none.astype(BF16), cols)
+    halo = rowh_ref[...].reshape(4 * cols, 2 * width)
+    for part, row in ((0, 2), (1, rows + 4)):
+        values = halo[part * 2 * cols:(part + 1) * 2 * cols]
+        place(y_s, (0,), row, scaled(values[:, :width]), cols)
+        place(grad_s, (), row, values[:, width:], cols)
+
+    def edge_block(i, c):
+        n = (rows + 10) // 2
+        values = edge_ref[pl.ds(i * n, n)].reshape(n * edges, 2 * width)
+        place(y_s, (0,), i * n, scaled(values[:, :width]), edges)
+        place(grad_s, (), i * n, values[:, width:], edges)
+        return c
+    lax.fori_loop(0, 2, edge_block, 0)
+
+    def norm_block(i, c):
+        src = pl.ds(i * BIG, BIG)
+        place(y_s, (0,), i * BIG + 4, scaled(mid_ref[src].reshape(BIG * cols, width)), cols)
+        place(grad_s, (), i * BIG + 4, gout_ref[src].reshape(BIG * cols, width), cols)
+        return c
+    lax.fori_loop(0, rows // BIG, norm_block, 0)
+
+    def shift_block(i, c):
+        at = rows_at(i * BIG + 1)
+        xv = y_s[0, pl.ds(at, tall + 8), :]
+        lv = y_s[0, pl.ds(at - 8, tall + 8), :]
+        dst = pl.ds(rows_at(i * BIG), tall)
+        x_s[0, dst, :] = lv[7:7 + tall].astype(BF16)
+        x_s[1, dst, :] = xv[:tall].astype(BF16)
+        x_s[2, dst, :] = xv[1:1 + tall].astype(BF16)
+        return c
+    lax.fori_loop(0, held // BIG, shift_block, 0)
 
     wdt_s[...] = wdown_ref[...].astype(F32).T.astype(BF16)
     wut_s[...] = wup_ref[...].astype(F32).T.astype(BF16)
     taps = [conv_ref[t:t + 1, :].astype(BF16) for t in range(9)]
-    first = step == 0
-
-    def body(i, c):
-        z0 = GROUP * (i - 2) - 2 + GUARD
+    hidden = wup_ref.shape[1]
+
+    def slot(row):
+        return pl.ds(rows_at(lax.rem(row + 2 * RING, RING)), STRIDE)
+
+    def products(i):
+        z0 = GROUP * (i - 2) - 2
         for b in range(3):
             parts = []
             for sub in range(GROUP):
                 z = None
                 for a in range(3):
-                    term = gp_s[pl.ds(rows_at(z0 + 1 - a + sub), STRIDE), :] * taps[3 * a + b]
+                    term = gp_s[slot(z0 + 1 - a + sub), :] * taps[3 * a + b]
                     z = term if z is None else z + term
                 parts.append(z)
-            old = y_s[b, pl.ds(rows_at(z0), CHUNK), :]
-            y_s[b, pl.ds(rows_at(z0), CHUNK), :] = jnp.where(first, 0.0, old) + jnp.dot(
+            y_s[b, pl.ds(rows_at(z0 + GUARD), CHUNK), :] = jnp.dot(
                 jnp.concatenate(parts, axis=0), wut_s[...], preferred_element_type=F32)
+
+    def slopes(i):
         g0 = GROUP * (i - 1) - 1
-        ga = jnp.dot(grad_s[pl.ds(rows_at(jnp.clip(g0 + 1, 0, held + 2 - GROUP)), CHUNK), :], wdt_s[...],
-                     preferred_element_type=F32)
-        for sub in range(GROUP):
-            pre = None
-            for a in range(3):
-                for b in range(3):
-                    term = h_s[b, pl.ds(rows_at(g0 + GUARD + a - 1 + sub), STRIDE), :] * taps[3 * a + b]
-                    pre = term if pre is None else pre + term
-            gp_s[pl.ds(rows_at(g0 + GUARD + sub), STRIDE), :] = (
-                ga[sub * STRIDE:(sub + 1) * STRIDE] * gelu_slope(pre).astype(F32)).astype(BF16)
+        grads = grad_s[pl.ds(rows_at(jnp.clip(g0 + 1, 0, held + 2 - GROUP)), CHUNK), :]
+        for at in range(0, hidden, FC):
+            lanes = slice(at, at + FC)
+            ga = jnp.dot(grads, wdt_s[:, lanes], preferred_element_type=F32)
+            for sub in range(GROUP):
+                pre = None
+                for a in range(3):
+                    for b in range(3):
+                        term = h_s[b, slot(g0 + a - 1 + sub), lanes] * taps[3 * a + b][:, lanes]
+                        pre = term if pre is None else pre + term
+                gp_s[slot(g0 + sub), lanes] = (
+                    ga[sub * STRIDE:(sub + 1) * STRIDE] * gelu_slope(pre).astype(F32)).astype(BF16)
+
+    def project(i):
         src = pl.ds(rows_at(jnp.minimum(GROUP * i, held - GROUP)), CHUNK)
+        dst = pl.ds(rows_at(lax.rem(GROUP * i, RING)), CHUNK)
         for b in range(3):
-            h_s[b, pl.ds(rows_at(GROUP * i + GUARD), CHUNK), :] = jnp.dot(
-                x_s[b, src, :], wup_ref[...], preferred_element_type=F32).astype(BF16)
+            for at in range(0, hidden, FC):
+                lanes = slice(at, at + FC)
+                h_s[b, dst, lanes] = jnp.dot(
+                    x_s[b, src, :], wup_ref[:, lanes], preferred_element_type=F32).astype(BF16)
+
+    def body(i, c):
+        products(i)
+        slopes(i)
+        project(i)
         return c
 
-    lax.fori_loop(0, trips, body, 0)
-
-    @pl.when(step == pl.num_programs(0) - 1)
-    def _():
-        def finish(i, c):
-            base = rows_at(i * BIG + 3 + GUARD)
-            right = y_s[0, pl.ds(base, tall + 8), :][1:1 + tall]
-            left = y_s[2, pl.ds(base - 8, tall + 8), :][7:7 + tall]
-            total = y_s[1, pl.ds(base, tall), :] + right + left
-
-            def crop(v):
-                return v.reshape(BIG, STRIDE, width)[:, :cols].reshape(BIG * cols, width)
-
-            e = crop(total) * gain
-            src = pl.ds(i * BIG, BIG)
-            hat, inv = normalize(mid_ref[src].reshape(BIG * cols, width).astype(F32))
-            res = gout_ref[src].reshape(BIG * cols, width).astype(F32) + inv * (
-                e - jnp.mean(e, axis=-1, keepdims=True) - hat * jnp.mean(e * hat, axis=-1, keepdims=True))
-            res = res.astype(BF16)
-            dst = pl.ds(i * BIG, BIG)
-            gm_ref[dst] = res.reshape(BIG, cols, width)
-            ga = dot_nt(res, wout_ref[...]).astype(BF16)
-            grow_ref[dst] = ga[:, :width // 2].reshape(BIG, cols, width // 2)
-            gcol_ref[dst, :, width:] = ga[:, width // 2:].reshape(BIG, cols, width // 2)
-            gcol_ref[dst, :, :width] = tok_ref[dst]
-            return c
-        lax.fori_loop(0, rows // BIG, finish, 0)
+    project(0)
+    slopes(1)
+    project(1)
+    lax.fori_loop(2, trips - 2, body, 0)
+    products(trips - 2)
+    slopes(trips - 2)
+    products(trips - 1)
+
+    def finish(i, c):
+        base = rows_at(i * BIG + 3 + GUARD)
+        right = y_s[0, pl.ds(base, tall + 8), :][1:1 + tall]
+        left = y_s[2, pl.ds(base - 8, tall + 8), :][7:7 + tall]
+        total = y_s[1, pl.ds(base, tall), :] + right + left
+
+        def crop(v):
+            return v.reshape(BIG, STRIDE, width)[:, :cols].reshape(BIG * cols, width)
+
+        e = crop(total) * gain
+        src = pl.ds(i * BIG, BIG)
+        hat, inv = normalize(mid_ref[src].reshape(BIG * cols, width).astype(F32))
+        res = gout_ref[src].reshape(BIG * cols, width).astype(F32) + inv * (
+            e - jnp.mean(e, axis=-1, keepdims=True) - hat * jnp.mean(e * hat, axis=-1, keepdims=True))
+        res = res.astype(BF16)
+        dst = pl.ds(i * BIG, BIG)
+        gm_ref[dst] = res.reshape(BIG, cols, width)
+        ga = dot_nt(res, wout_ref[...]).astype(BF16)
+        grow_ref[dst] = ga[:, :width // 2].reshape(BIG, cols, width // 2)
+        gcol_ref[dst, :, width:] = ga[:, width // 2:].reshape(BIG, cols, width // 2)
+        gcol_ref[dst, :, :width] = tok_ref[dst]
+        return c
+    lax.fori_loop(0, rows // BIG, finish, 0)
 
 
 def mlp(mid, grad, tokens, halo, edge, gain, w_up, conv_kernel, w_down, w_out):
@@ -175,20 +193,15 @@
     return pl.pallas_call(
         functools.partial(mlp_kernel, rows, cols),
         out_shape=tuple(jax.ShapeDtypeStruct((rows, cols, n), BF16) for n in (width, width // 2, width + width // 2)),
-        grid=(hidden // FC,),
-        in_specs=[whole, whole, whole, whole, whole, whole,
-                  pl.BlockSpec((width, FC), lambda i: (0, i)),
-                  pl.BlockSpec((9, FC), lambda i: (0, i)),
-                  pl.BlockSpec((FC, width), lambda i: (i, 0)),
-                  whole],
+        in_specs=[whole] * 10,
         out_specs=(whole, whole, whole),
         scratch_shapes=[
             pltpu.VMEM((3, held * STRIDE, width), BF16),
-            pltpu.VMEM((3, slots, FC), BF16),
-            pltpu.VMEM((slots, FC), BF16),
+            pltpu.VMEM((3, RING * STRIDE, hidden), BF16),
+            pltpu.VMEM((RING * STRIDE, hidden), BF16),
             pltpu.VMEM((3, slots, width), F32),
-            pltpu.VMEM((width, FC), BF16),
-            pltpu.VMEM((FC, width), BF16),
+            pltpu.VMEM((width, hidden), BF16),
+            pltpu.VMEM((hidden, width), BF16),
             pltpu.VMEM(((rows + 10) * STRIDE, width), BF16),
         ],
         compiler_params=pltpu.CompilerParams(vmem_limit_bytes=60 * 1024 * 1024),
@@ -397,11 +410,11 @@
 
 def final(tokens, grad_mid, row_back, col_back, gain):
     rows, cols, width = tokens.shape
-    blk = pl.BlockSpec((8, cols, width), lambda i: (i, 0, 0))
+    blk = pl.BlockSpec((16, cols, width), lambda i: (i, 0, 0))
     return pl.pallas_call(
         final_kernel,
         out_shape=jax.ShapeDtypeStruct(tokens.shape, BF16),
-        grid=(rows // 8,),
+        grid=(rows // 16,),
         in_specs=[blk, blk, blk, blk, pl.BlockSpec((1, width), lambda i: (0, 0))],
         out_specs=blk,
         cost_estimate=pl.CostEstimate(flops=20_000_000, transcendentals=4_000, bytes_accessed=8_000_000),

time: 206 us -> 193 us (0.937); the launches traced: 207 us -> 191 us
  Pallas kernels: 119 us -> 104 us
    pallas_call x1, Pallas kernels: 52.3 us -> 40.8 us  [mlp(): pl.pallas_call(functools.partial(mlp_kernel, rows, cols), out_shape=tuple...]
    pallas_call x1, Pallas kernels: 7.75 us -> 5.65 us  [final(): pl.pallas_call(final_kernel, out_shape=jax.ShapeDtypeStruct(tokens.shape,...]
  transfers between devices with their start and end apart: 14 -> 14, of which waited for: 3 -> 3; matrix products, arithmetic and copies ran while one was open for 4% -> 4% of each run, Pallas kernels for 54% -> 52%
where the time goes in v5:
time: 193 us; the launch traced here: 191 us
  Pallas kernels  104 us (54%)
  starting transfers between devices  41.9 us (22%)
  blocking collectives  26.1 us (14%)
  local copies, waits for them, and re-layouts  10.7 us (6%)
  waiting for transfers between devices  4.69 us (2%)
  other arithmetic  2.49 us (1%)
    pallas_call x2, Pallas kernels, attention(): pl.pallas_call(functools.partial(attn_kernel, nl, nk, half, pieces), out_...  57.9 us
    pallas_call x1, Pallas kernels, mlp(): pl.pallas_call(functools.partial(mlp_kernel, rows, cols), out_shape=tuple...  40.8 us
    all_to_all x1, blocking collectives, to_lines(): return lax.all_to_all(blocks, axis, split_axis=0, concat_axis=0, tiled=True)  26.1 us
    all_to_all x3, starting transfers between devices, to_lines(): return lax.all_to_all(blocks, axis, split_axis=0, concat_axis=0, tiled=True)  21.5 us
    ppermute x2, starting transfers between devices, neighbours(): lax.ppermute(ahead, axis, up)  8.93 us
    ppermute x7, starting transfers between devices, per_device(): lax.ppermute(part, 'gy', [(i, (i + ahead) % count_gy) for i in range(coun...  8.27 us
    pallas_call x1, Pallas kernels, final(): pl.pallas_call(final_kernel, out_shape=jax.ShapeDtypeStruct(tokens.shape,...  5.65 us
  transfers between devices with their start and end apart: 14, of which 3 were waited for; matrix products, arithmetic and copies ran while one was open for 4% of the time, Pallas kernels for 52%

profile of v5, /device:TPU:1, one launch (start us, length us, event | category | flops | bytes accessed | tf_op | source)
XLA Modules:
  0.0 190.6 jit_solution(8347911616136677147)
XLA Ops:
  0.0 0.9 fusion.7
  0.9 4.9 %collective-permute-start = (bf16[2,48,512]{2,1,0:T(8,128)(2,1)S(1)}, bf16[2,48,512]{2,1,0:T(8,128)(2,1)S(1)}, u32[]{:S(2)}, u32[]{:S(2)}) collective-permute-start(bf16[2,48,512]{2,1,0:T(8,128)(2,1)S(1)} %pad_maximum_fusion.3), channel_id=1, source_target_pairs={{0,16},{16,32},{32,48},{48,64},{64,80},{80,96},{96,112},{1,17},{17... | collective-permute-start | bytes 294920 | tf_op jit(solution)/shard_map/ppermute | solution.py:437
  5.9 1.9 %collective-permute-start.1 = (bf16[2,48,512]{2,1,0:T(8,128)(2,1)S(1)}, bf16[2,48,512]{2,1,0:T(8,128)(2,1)S(1)}, u32[]{:S(2)}, u32[]{:S(2)}) collective-permute-start(bf16[2,48,512]{2,1,0:T(8,128)(2,1)S(1)} %pad_maximum_fusion.4), channel_id=1, source_target_pairs={{16,0},{32,16},{48,32},{64,48},{80,64},{96,80},{112,96},{17,1},{33... | collective-permute-start | bytes 294920 | tf_op jit(solution)/shard_map/ppermute | solution.py:437
  7.8 1.4 fusion.5
  9.2 0.0 collective-permute-done
  9.2 2.6 %collective-permute-done.1 = bf16[2,48,512]{2,1,0:T(8,128)(2,1)S(1)} collective-permute-done((bf16[2,48,512]{2,1,0:T(8,128)(2,1)S(1)}, bf16[2,48,512]{2,1,0:T(8,128)(2,1)S(1)}, u32[]{:S(2)}, u32[]{:S(2)}) %collective-permute-start.1) | collective-permute-done | bytes 98336 | tf_op jit(solution)/shard_map/ppermute | solution.py:437
  11.8 0.1 pad_maximum_fusion.1
  11.9 1.3 collective-permute-start.2
  13.2 0.1 pad_maximum_fusion.2
  13.4 4.0 %collective-permute-start.3 = (bf16[68,2,512]{2,1,0:T(2,128)(2,1)S(1)}, bf16[68,2,512]{2,1,0:T(2,128)(2,1)S(1)}, u32[]{:S(2)}, u32[]{:S(2)}) collective-permute-start(bf16[68,2,512]{2,1,0:T(2,128)(2,1)S(1)} %pad_maximum_fusion.2), channel_id=1, source_target_pairs={{0,1},{1,2},{2,3},{3,4},{4,5},{5,6},{6,7},{7,8},{8,9},{9,10},{10,1... | collective-permute-start | bytes 417800 | tf_op jit(solution)/shard_map/ppermute | solution.py:437
  17.4 8.7 %all-to-all-start = ((bf16[16,4,48,256]{3,2,1,0:T(8,128)(2,1)}), bf16[16,4,48,256]{3,2,1,0:T(8,128)(2,1)S(1)}, u32[]{:S(2)}, u32[]{:S(2)}) async-start(bf16[16,4,48,256]{3,2,1,0:T(8,128)(2,1)} %bitcast.1), calls=%async_computation | async-start | bytes 3145728 | tf_op jit(solution)/shard_map/all_to_all | solution.py:426
  26.1 0.1 pad.11.clone
  26.2 0.7 pad_maximum_fusion.rowh_ref
  26.9 0.0 collective-permute-done.2
  26.9 0.0 collective-permute-done.3
  26.9 1.5 fusion.2.edge_ref
  28.4 40.8 %mlp_backward.1 = (bf16[64,48,256]{2,1,0:T(8,128)(2,1)}, bf16[64,48,128]{2,1,0:T(8,128)(2,1)}, bf16[64,48,384]{2,1,0:T(8,128)(2,1)}) custom-call(bf16[64,48,256]{2,1,0:T(8,128)(2,1)} %mid_ref.1, bf16[64,48,256]{2,1,0:T(8,128)(2,1)} %gout_ref.1, bf16[64,48,256]{2,1,0:T(8,128)(2,1)} %tok_ref.3, bf16[4,48,512]{2,1,0:T(8,128)(2,1)} %pad_maximum_fusion.rowh_ref, ...), custom_call_target="tpu_custom_call" | custom-call | flops 20000000000 | bytes 12000000 | tf_op jit(solution)/shard_map/mlp_backward/pallas_call | solution.py:193
  69.2 0.0 all-to-all-done.refs_0_
  69.2 6.7 %all-to-all-start.1 = ((bf16[16,4,48,128]{3,2,1,0:T(8,128)(2,1)}), bf16[16,4,48,128]{3,2,1,0:T(8,128)(2,1)S(1)}, u32[]{:S(2)}, u32[]{:S(2)}) async-start(bf16[16,4,48,128]{3,2,1,0:T(8,128)(2,1)} %bitcast.46), calls=%async_computation.1 | async-start | bytes 1572864 | tf_op jit(solution)/shard_map/all_to_all | solution.py:426
  76.0 2.3 %copy.17 = bf16[64,48,384]{2,0,1:T(8,128)(2,1)S(1)} copy(bf16[64,48,384]{2,1,0:T(8,128)(2,1)} %get-tuple-element.25) | data formatting | bytes 4718592 | tf_op jit(solution)/shard_map/mlp_backward/pallas_call | solution.py:193
  78.3 0.0 copy-start
  78.3 0.0 copy-start.7
  78.3 1.2 dynamic-slice_bitcast_fusion
  79.5 0.0 collective-permute-start.10
  79.5 1.7 collective-permute-start.4
  81.3 1.6 collective-permute-start.5
  82.9 2.1 %collective-permute-start.6 = (bf16[6,64,384]{2,1,0:T(8,128)(2,1)}, bf16[6,64,384]{2,1,0:T(8,128)(2,1)}, u32[]{:S(2)}, u32[]{:S(2)}) collective-permute-start(bf16[6,64,384]{2,1,0:T(8,128)(2,1)} %get-tuple-element.41), channel_id=1, source_target_pairs={{0,48},{16,64},{32,80},{48,96},{64,112},{80,0},{96,16},{112,32},{1... | collective-permute-start | bytes 884744 | tf_op jit(solution)/shard_map/ppermute | solution.py:472
  85.0 0.0 collective-permute-start.7
  85.0 1.2 collective-permute-done.10.refs_7_
  86.1 2.3 %collective-permute-start.8 = (bf16[6,64,384]{2,1,0:T(8,128)(2,1)}, bf16[6,64,384]{2,1,0:T(8,128)(2,1)}, u32[]{:S(2)}, u32[]{:S(2)}) collective-permute-start(bf16[6,64,384]{2,1,0:T(8,128)(2,1)} %get-tuple-element.39), channel_id=1, source_target_pairs={{0,80},{16,96},{32,112},{48,0},{64,16},{80,32},{96,48},{112,64},{1... | collective-permute-start | bytes 884744 | tf_op jit(solution)/shard_map/ppermute | solution.py:472
  88.5 0.0 collective-permute-done.4.refs_1_
  88.5 0.5 collective-permute-start.9
  89.0 0.9 all-to-all-done.1.refs_1_
  89.9 0.0 copy-done
  89.9 0.0 copy-done.7
  89.9 0.0 copy-start.1
  89.9 0.9 copy-done.1
  90.8 0.0 copy-start.3
  90.8 0.9 copy-done.3
  91.7 0.0 copy-start.5
  91.7 0.9 copy-done.5
  92.6 33.9 %axial_attention.2 = bf16[16,4,48,256]{3,2,1,0:T(8,128)(2,1)} custom-call(s32[6,6]{1,0:T(8,128)S(1)} %copy-done.7, s32[8]{0:T(128)S(1)} %and_select_fusion.at_ref, bf16[16,4,48,256]{3,2,1,0:T(8,128)(2,1)S(1)} %all-to-all-done.refs_0_, bf16[16,4,48,128]{3,2,1,0:T(8,128)(2,1)S(1)} %all-to-all-done.1.refs_1_, f32[1,256]{1,0:T(1,128)S(1)} %bitcast.42, ...), custom_call_target="tpu_custom_call" | custom-call | flops 28800000000 | bytes 4000000 | tf_op jit(solution)/shard_map/axial_attention/pallas_call | solution.py:368
  126.6 0.0 collective-permute-done.5.refs_2_
  126.6 0.0 collective-permute-done.6.refs_3_
  126.6 0.0 collective-permute-done.7.refs_4_
  126.6 0.0 collective-permute-done.8.refs_5_
  126.6 0.0 collective-permute-done.9.refs_6_
  126.6 0.0 copy-start.2
  126.6 0.0 copy-start.4
  126.6 0.0 copy-start.6
  126.6 0.0 copy-start.8
  126.6 6.1 %all-to-all-start.2 = ((bf16[16,4,48,256]{3,2,1,0:T(8,128)(2,1)}), bf16[16,4,48,256]{3,2,1,0:T(8,128)(2,1)}, u32[]{:S(2)}, u32[]{:S(2)}) async-start(bf16[16,4,48,256]{3,2,1,0:T(8,128)(2,1)} %axial_attention.2), calls=%async_computation.2 | async-start | bytes 3145728 | tf_op jit(solution)/shard_map/all_to_all | solution.py:426
  132.8 0.0 copy-done.2
  132.8 0.0 copy-done.4
  132.8 0.0 copy-done.6
  132.8 0.0 copy-done.8
  132.8 24.0 %axial_attention.3 = bf16[8,6,64,256]{3,2,1,0:T(8,128)(2,1)S(1)} custom-call(s32[4,4]{1,0:T(4,128)S(1)} %copy-done.8, s32[8]{0:T(128)S(1)} %and_select_fusion.at_ref, bf16[6,64,384]{2,1,0:T(8,128)(2,1)S(1)} %get-tuple-element.27.refs_0_, bf16[6,64,384]{2,1,0:T(8,128)(2,1)S(1)} %collective-permute-done.4.refs_1_, ...), custom_call_target="tpu_custom_call" | custom-call | flops 19200000000 | bytes 4000000 | tf_op jit(solution)/shard_map/axial_attention/pallas_call | solution.py:368
  156.8 0.0 all-to-all-done.2
  156.8 26.1 %all_to_all.20 = bf16[8,6,64,256]{3,2,1,0:T(8,128)(2,1)S(1)} all-to-all(bf16[8,6,64,256]{3,2,1,0:T(8,128)(2,1)S(1)} %axial_attention.3), channel_id=1, replica_groups=mesh['gy'=8,'gx'=16] {'gy'}, dimensions={0} | all-to-all | bytes 3145728 | tf_op jit(solution)/shard_map/all_to_all | solution.py:426
  182.9 2.0 %copy.18.col_ref = bf16[64,48,256]{2,1,0:T(8,128)(2,1)} copy(bf16[64,48,256]{2,0,1:T(8,128)(2,1)S(1)} %bitcast.45) | data formatting | bytes 3145728 | tf_op jit(solution)/shard_map/reshape | solution.py:483
  185.0 5.7 %norm_backward.1 = bf16[64,48,256]{2,1,0:T(8,128)(2,1)} custom-call(bf16[64,48,256]{2,1,0:T(8,128)(2,1)} %tok_ref.3, bf16[64,48,256]{2,1,0:T(8,128)(2,1)} %get-tuple-element.21.mid_ref, bf16[64,48,256]{2,1,0:T(8,128)(2,1)} %bitcast.21.row_ref, bf16[64,48,256]{2,1,0:T(8,128)(2,1)} %copy.18.col_ref, f32[1,256]{1,0:T(1,128)} %bitcast.41), custom_call_target="tpu_custom_call" | custom-call | flops 20000000 | bytes 8000000 | tf_op jit(solution)/shard_map/norm_backward/pallas_call | solution.py:414
  (6 shorter events, 0.1 us)
Async XLA Ops:
  0.9 8.3 %collective-permute-start = (bf16[2,48,512]{2,1,0:T(8,128)(2,1)S(1)}, bf16[2,48,512]{2,1,0:T(8,128)(2,1)S(1)}, u32[]{:S(2)}, u32[]{:S(2)}) collective-permute-start(bf16[2,48,512]{2,1,0:T(8,128)(2,1)S(1)} %pad_maximum_fusion.3), channel_id=1, source_target_pairs={{0,16},{16,32},{32,48},{48,64},{64,80},{80,96},{96,112},{1,17},{17... | collective-permute-start | bytes 294920 | tf_op jit(solution)/shard_map/ppermute | solution.py:437
  5.9 5.9 %collective-permute-start.1 = (bf16[2,48,512]{2,1,0:T(8,128)(2,1)S(1)}, bf16[2,48,512]{2,1,0:T(8,128)(2,1)S(1)}, u32[]{:S(2)}, u32[]{:S(2)}) collective-permute-start(bf16[2,48,512]{2,1,0:T(8,128)(2,1)S(1)} %pad_maximum_fusion.4), channel_id=1, source_target_pairs={{16,0},{32,16},{48,32},{64,48},{80,64},{96,80},{112,96},{17,1},{33... | collective-permute-start | bytes 294920 | tf_op jit(solution)/shard_map/ppermute | solution.py:437
  11.9 14.9 %collective-permute-start.2 = (bf16[68,2,512]{2,1,0:T(2,128)(2,1)S(1)}, bf16[68,2,512]{2,1,0:T(2,128)(2,1)S(1)}, u32[]{:S(2)}, u32[]{:S(2)}) collective-permute-start(bf16[68,2,512]{2,1,0:T(2,128)(2,1)S(1)} %pad_maximum_fusion.1), channel_id=1, source_target_pairs={{1,0},{2,1},{3,2},{4,3},{5,4},{6,5},{7,6},{8,7},{9,8},{10,9},{11,1... | collective-permute-start | bytes 417800 | tf_op jit(solution)/shard_map/ppermute | solution.py:437
  13.4 13.5 %collective-permute-start.3 = (bf16[68,2,512]{2,1,0:T(2,128)(2,1)S(1)}, bf16[68,2,512]{2,1,0:T(2,128)(2,1)S(1)}, u32[]{:S(2)}, u32[]{:S(2)}) collective-permute-start(bf16[68,2,512]{2,1,0:T(2,128)(2,1)S(1)} %pad_maximum_fusion.2), channel_id=1, source_target_pairs={{0,1},{1,2},{2,3},{3,4},{4,5},{5,6},{6,7},{7,8},{8,9},{9,10},{10,1... | collective-permute-start | bytes 417800 | tf_op jit(solution)/shard_map/ppermute | solution.py:437
  17.4 51.8 %all-to-all-start = ((bf16[16,4,48,256]{3,2,1,0:T(8,128)(2,1)}), bf16[16,4,48,256]{3,2,1,0:T(8,128)(2,1)S(1)}, u32[]{:S(2)}, u32[]{:S(2)}) async-start(bf16[16,4,48,256]{3,2,1,0:T(8,128)(2,1)} %bitcast.1), calls=%async_computation | async-start | bytes 3145728 | tf_op jit(solution)/shard_map/all_to_all | solution.py:426
  69.2 20.7 %all-to-all-start.1 = ((bf16[16,4,48,128]{3,2,1,0:T(8,128)(2,1)}), bf16[16,4,48,128]{3,2,1,0:T(8,128)(2,1)S(1)}, u32[]{:S(2)}, u32[]{:S(2)}) async-start(bf16[16,4,48,128]{3,2,1,0:T(8,128)(2,1)} %bitcast.46), calls=%async_computation.1 | async-start | bytes 1572864 | tf_op jit(solution)/shard_map/all_to_all | solution.py:426
  78.3 11.6 %copy-start = (f32[256]{0:T(256)S(1)}, f32[256]{0:T(256)}, u32[]{:S(2)}) copy-start(f32[256]{0:T(256)} %param.17) | copy-start | bytes 3076
  78.3 11.6 %copy-start.7 = (s32[6,6]{1,0:T(8,128)S(1)}, s32[6,6]{1,0:T(8,128)}, u32[]{:S(2)}) copy-start(s32[6,6]{1,0:T(8,128)} %mask_ref.2) | copy-start | bytes 436
  79.5 6.6 %collective-permute-start.10 = (bf16[6,64,384]{2,1,0:T(8,128)(2,1)S(1)}, bf16[6,64,384]{2,1,0:T(8,128)(2,1)S(1)}, u32[]{:S(2)}, u32[]{:S(2)}) collective-permute-start(bf16[6,64,384]{2,1,0:T(8,128)(2,1)S(1)} %get-tuple-element.37), channel_id=1, source_target_pairs={{0,112},{16,0},{32,16},{48,32},{64,48},{80,64},{96,80},{112,96},{1... | collective-permute-start | bytes 884744 | tf_op jit(solution)/shard_map/ppermute | solution.py:472
  79.5 9.0 %collective-permute-start.4 = (bf16[6,64,384]{2,1,0:T(8,128)(2,1)S(1)}, bf16[6,64,384]{2,1,0:T(8,128)(2,1)S(1)}, u32[]{:S(2)}, u32[]{:S(2)}) collective-permute-start(bf16[6,64,384]{2,1,0:T(8,128)(2,1)S(1)} %get-tuple-element.43), channel_id=1, source_target_pairs={{0,16},{16,32},{32,48},{48,64},{64,80},{80,96},{96,112},{112,0},{1... | collective-permute-start | bytes 884744 | tf_op jit(solution)/shard_map/ppermute | solution.py:472
  81.3 45.3 %collective-permute-start.5 = (bf16[6,64,384]{2,1,0:T(8,128)(2,1)}, bf16[6,64,384]{2,1,0:T(8,128)(2,1)S(1)}, u32[]{:S(2)}, u32[]{:S(2)}) collective-permute-start(bf16[6,64,384]{2,1,0:T(8,128)(2,1)} %get-tuple-element.42), channel_id=1, source_target_pairs={{0,32},{16,48},{32,64},{48,80},{64,96},{80,112},{96,0},{112,16},{1... | collective-permute-start | bytes 884744 | tf_op jit(solution)/shard_map/ppermute | solution.py:472
  82.9 43.7 %collective-permute-start.6 = (bf16[6,64,384]{2,1,0:T(8,128)(2,1)}, bf16[6,64,384]{2,1,0:T(8,128)(2,1)}, u32[]{:S(2)}, u32[]{:S(2)}) collective-permute-start(bf16[6,64,384]{2,1,0:T(8,128)(2,1)} %get-tuple-element.41), channel_id=1, source_target_pairs={{0,48},{16,64},{32,80},{48,96},{64,112},{80,0},{96,16},{112,32},{1... | collective-permute-start | bytes 884744 | tf_op jit(solution)/shard_map/ppermute | solution.py:472
  85.0 41.6 %collective-permute-start.7 = (bf16[6,64,384]{2,1,0:T(8,128)(2,1)}, bf16[6,64,384]{2,1,0:T(8,128)(2,1)}, u32[]{:S(2)}, u32[]{:S(2)}) collective-permute-start(bf16[6,64,384]{2,1,0:T(8,128)(2,1)} %get-tuple-element.40), channel_id=1, source_target_pairs={{0,64},{16,80},{32,96},{48,112},{64,0},{80,16},{96,32},{112,48},{1... | collective-permute-start | bytes 884744 | tf_op jit(solution)/shard_map/ppermute | solution.py:472
  86.1 40.4 %collective-permute-start.8 = (bf16[6,64,384]{2,1,0:T(8,128)(2,1)}, bf16[6,64,384]{2,1,0:T(8,128)(2,1)}, u32[]{:S(2)}, u32[]{:S(2)}) collective-permute-start(bf16[6,64,384]{2,1,0:T(8,128)(2,1)} %get-tuple-element.39), channel_id=1, source_target_pairs={{0,80},{16,96},{32,112},{48,0},{64,16},{80,32},{96,48},{112,64},{1... | collective-permute-start | bytes 884744 | tf_op jit(solution)/shard_map/ppermute | solution.py:472
  88.5 38.1 %collective-permute-start.9 = (bf16[6,64,384]{2,1,0:T(8,128)(2,1)}, bf16[6,64,384]{2,1,0:T(8,128)(2,1)}, u32[]{:S(2)}, u32[]{:S(2)}) collective-permute-start(bf16[6,64,384]{2,1,0:T(8,128)(2,1)} %get-tuple-element.38), channel_id=1, source_target_pairs={{0,96},{16,112},{32,0},{48,16},{64,32},{80,48},{96,64},{112,80},{1... | collective-permute-start | bytes 884744 | tf_op jit(solution)/shard_map/ppermute | solution.py:472
  89.9 0.9 copy-start.1
  90.8 0.9 copy-start.3
  91.7 0.9 copy-start.5
  126.6 6.2 %copy-start.2 = (bf16[256,256]{1,0:T(8,128)(2,1)S(1)}, bf16[256,256]{1,0:T(8,128)(2,1)}, u32[]{:S(2)}) copy-start(bf16[256,256]{1,0:T(8,128)(2,1)} %refs_9_.1) | copy-start | bytes 393220
  126.6 6.2 %copy-start.4 = (bf16[256,256]{1,0:T(8,128)(2,1)S(1)}, bf16[256,256]{1,0:T(8,128)(2,1)}, u32[]{:S(2)}) copy-start(bf16[256,256]{1,0:T(8,128)(2,1)} %refs_10_.1) | copy-start | bytes 393220
  126.6 6.2 %copy-start.6 = (bf16[256,256]{1,0:T(8,128)(2,1)S(1)}, bf16[256,256]{1,0:T(8,128)(2,1)}, u32[]{:S(2)}) copy-start(bf16[256,256]{1,0:T(8,128)(2,1)} %refs_11_.1) | copy-start | bytes 393220
  126.6 6.2 %copy-start.8 = (s32[4,4]{1,0:T(4,128)S(1)}, s32[4,4]{1,0:T(4,128)}, u32[]{:S(2)}) copy-start(s32[4,4]{1,0:T(4,128)} %mask_ref.3) | copy-start | bytes 196
  126.6 30.1 %all-to-all-start.2 = ((bf16[16,4,48,256]{3,2,1,0:T(8,128)(2,1)}), bf16[16,4,48,256]{3,2,1,0:T(8,128)(2,1)}, u32[]{:S(2)}, u32[]{:S(2)}) async-start(bf16[16,4,48,256]{3,2,1,0:T(8,128)(2,1)} %axial_attention.2), calls=%async_computation.2 | async-start | bytes 3145728 | tf_op jit(solution)/shard_map/all_to_all | solution.py:426

commit v6 on v5

--- a/solution.py
+++ b/solution.py
@@ -19,7 +19,7 @@
 GROUP = 8
 CHUNK = GROUP * STRIDE
 BIG = 8
-GUARD = 2 * GROUP + 4
+GUARD = 2
 RING = 3 * GROUP
 FC = 512
 
@@ -42,8 +42,9 @@
     return center * inv, inv
 
 
-def mlp_kernel(rows, cols, mid_ref, gout_ref, tok_ref, rowh_ref, edge_ref, gain_ref, wup_ref, conv_ref, wdown_ref, wout_ref,
-               gm_ref, grow_ref, gcol_ref, x_s, h_s, gp_s, y_s, wdt_s, wut_s, grad_s):
+def mlp_kernel(rows, cols, mid_ref, gout_ref, tok_ref, above_ref, below_ref, edge_ref, gain_ref, wup_ref, conv_ref, wdown_ref, wout_ref,
+               wq_ref, wk_ref, wv_ref,
+               gm_ref, grow_ref, gcol_ref, wide_ref, x_s, h_s, gp_s, y_s, wdt_s, wut_s, grad_s):
     width = mid_ref.shape[-1]
     gain = gain_ref[...]
     held = rows + 8
@@ -67,9 +68,8 @@
     for row in (0, 1, rows + 6, rows + 7, rows + 8, rows + 9):
         place(y_s, (0,), row, none, cols)
         place(grad_s, (), row, none.astype(BF16), cols)
-    halo = rowh_ref[...].reshape(4 * cols, 2 * width)
-    for part, row in ((0, 2), (1, rows + 4)):
-        values = halo[part * 2 * cols:(part + 1) * 2 * cols]
+    for ref, row in ((above_ref, 2), (below_ref, rows + 4)):
+        values = ref[...].reshape(2 * cols, 2 * width)
         place(y_s, (0,), row, scaled(values[:, :width]), cols)
         place(grad_s, (), row, values[:, width:], cols)
 
@@ -99,6 +99,10 @@
         return c
     lax.fori_loop(0, held // BIG, shift_block, 0)
 
+    n = width // 2
+    for half in range(2):
+        for j, ref in enumerate((wq_ref, wk_ref, wv_ref)):
+            wide_ref[half, :, j * n:(j + 1) * n] = ref[:, half * n:(half + 1) * n]
     wdt_s[...] = wdown_ref[...].astype(F32).T.astype(BF16)
     wut_s[...] = wup_ref[...].astype(F32).T.astype(BF16)
     taps = [conv_ref[t:t + 1, :].astype(BF16) for t in range(9)]
@@ -183,18 +187,19 @@
     lax.fori_loop(0, rows // BIG, finish, 0)
 
 
-def mlp(mid, grad, tokens, halo, edge, gain, w_up, conv_kernel, w_down, w_out):
+def mlp(mid, grad, tokens, above, below, edge, gain, w_up, conv_kernel, w_down, w_out, w_query, w_key, w_value):
     rows, cols, width = mid.shape
     hidden = w_up.shape[1]
     held = rows + 8
     trips = (rows + 4 + GROUP) // GROUP + 2
-    slots = (GROUP * trips + GUARD + 1) * STRIDE
+    slots = max(GROUP * (trips - 2), rows + 12) * STRIDE
     whole = pl.BlockSpec(memory_space=pltpu.VMEM)
     return pl.pallas_call(
         functools.partial(mlp_kernel, rows, cols),
-        out_shape=tuple(jax.ShapeDtypeStruct((rows, cols, n), BF16) for n in (width, width // 2, width + width // 2)),
-        in_specs=[whole] * 10,
-        out_specs=(whole, whole, whole),
+        out_shape=tuple(jax.ShapeDtypeStruct((rows, cols, n), BF16) for n in (width, width // 2, width + width // 2)) + (
+            jax.ShapeDtypeStruct((2, width, 3 * width // 2), BF16),),
+        in_specs=[whole] * 14,
+        out_specs=(whole,) * 4,
         scratch_shapes=[
             pltpu.VMEM((3, held * STRIDE, width), BF16),
             pltpu.VMEM((3, RING * STRIDE, hidden), BF16),
@@ -204,16 +209,17 @@
             pltpu.VMEM((hidden, width), BF16),
             pltpu.VMEM(((rows + 10) * STRIDE, width), BF16),
         ],
-        compiler_params=pltpu.CompilerParams(vmem_limit_bytes=60 * 1024 * 1024),
+        compiler_params=pltpu.CompilerParams(vmem_limit_bytes=54 * 1024 * 1024),
         cost_estimate=pl.CostEstimate(flops=20_000_000_000, transcendentals=4_000_000, bytes_accessed=12_000_000),
         name="mlp_backward",
-    )(mid, grad, tokens, halo, edge, gain.reshape(1, -1), w_up, conv_kernel, w_down, w_out)
+    )(mid, grad, tokens, above, below, edge, gain.reshape(1, -1), w_up, conv_kernel, w_down, w_out,
+      w_query, w_key, w_value)
 
 
 def attn_kernel(nl, nk, half, pieces, mask_ref, at_ref, *refs):
     x_ref, g_ref = refs[:2]
     piece_refs = refs[:pieces]
-    (gain_ref, wq_ref, wk_ref, wv_ref, out_ref, w_s, wt_s, q_s, k_s, v_s, g_s, kt_s, qmt_s, qm_s, gmt_s, gm_s,
+    (gain_ref, w_ref, out_ref, q_s, k_s, v_s, g_s, kt_s, qmt_s, qm_s, gmt_s, gm_s,
      e_s, dp_s, st_s, dq_s, dk_s, dv_s) = refs[max(pieces, 2):]
     heads = HEADS // 2
     hw = 128
@@ -228,14 +234,9 @@
     dk_s[...] = jnp.zeros_like(dk_s)
     dv_s[...] = jnp.zeros_like(dv_s)
 
-    for j, ref in enumerate((wq_ref, wk_ref, wv_ref)):
-        part = ref[:, half * hw:(half + 1) * hw]
-        w_s[:, j * hw:(j + 1) * hw] = part
-        wt_s[j * hw:(j + 1) * hw, :] = part.astype(F32).T.astype(BF16)
-
     def project(xv):
         normed = (normalize(xv.astype(F32))[0] * gain).astype(BF16)
-        return jnp.dot(normed, w_s[...], preferred_element_type=F32)
+        return jnp.dot(normed, w_ref[half], preferred_element_type=F32)
 
     def keep(line, where, qkv, grads):
         q_s[line, where, :] = (qkv[:, :hw] * (factor * LOG2E)).astype(BF16)
@@ -347,17 +348,17 @@
     def finish(line, carry):
         grads = jnp.concatenate(
             [q_s[line], (dk_s[line] * LN2).astype(BF16), dv_s[line].astype(BF16)], axis=1)
-        res = jnp.dot(grads, wt_s[...], preferred_element_type=F32).astype(BF16)
+        res = dot_nt(grads, w_ref[half]).astype(BF16)
         out_ref[:, line] = res.reshape(out_ref.shape[0], out_ref.shape[2], out_ref.shape[3])
         return carry
 
     lax.fori_loop(0, nl, finish, 0)
 
 
-def attention(arrays, at, shape, gain, w_query, w_key, w_value, mask, half):
+def attention(arrays, at, shape, gain, w_wide, mask, half):
     srcs, nl, span = shape
     pieces = srcs if len(arrays) == srcs else 0
-    width = w_query.shape[0]
+    width = w_wide.shape[1]
     length = srcs * span
     nk = length // BLK
     hw = width // 2
@@ -368,11 +369,9 @@
     return pl.pallas_call(
         functools.partial(attn_kernel, nl, nk, half, pieces),
         out_shape=jax.ShapeDtypeStruct((srcs, nl, span, width), BF16),
-        in_specs=[pl.BlockSpec(memory_space=pltpu.SMEM)] * 2 + [vm] * (len(arrays) + 4),
+        in_specs=[pl.BlockSpec(memory_space=pltpu.SMEM)] * 2 + [vm] * (len(arrays) + 2),
         out_specs=vm,
         scratch_shapes=[
-            pltpu.VMEM((width, 3 * hw), BF16),
-            pltpu.VMEM((3 * hw, width), BF16),
             pltpu.VMEM((nl, length, hw), BF16),
             pltpu.VMEM((nl, length, hw), BF16),
             pltpu.VMEM((nl, length, hw), BF16),
@@ -389,10 +388,10 @@
             pltpu.VMEM((nl, length, hw), F32),
             pltpu.VMEM((nl, length, hw), F32),
         ],
-        compiler_params=pltpu.CompilerParams(vmem_limit_bytes=40 * 1024 * 1024),
+        compiler_params=pltpu.CompilerParams(vmem_limit_bytes=28 * 1024 * 1024),
         cost_estimate=pl.CostEstimate(flops=pairs * 200_000_000, transcendentals=pairs * 65536, bytes_accessed=4_000_000),
         name="axial_attention",
-    )(mask, at, *arrays, gain.reshape(1, -1), w_query, w_key, w_value)
+    )(mask, at, *arrays, gain.reshape(1, -1), w_wide)
 
 
 def final_kernel(tok_ref, mid_ref, row_ref, col_ref, gain_ref, out_ref):
@@ -402,7 +401,8 @@
         return ref[...].reshape(count * cols, width).astype(F32)
 
     hat, inv = normalize(flat(tok_ref))
-    e = (flat(row_ref) + flat(col_ref)) * gain_ref[...]
+    turned = jnp.swapaxes(col_ref[...].reshape(cols, count, width).astype(F32), 0, 1).reshape(count * cols, width)
+    e = (flat(row_ref) + turned) * gain_ref[...]
     res = flat(mid_ref) + inv * (
         e - jnp.mean(e, axis=-1, keepdims=True) - hat * jnp.mean(e * hat, axis=-1, keepdims=True))
     out_ref[...] = res.astype(BF16).reshape(count, cols, width)
@@ -415,7 +415,7 @@
         final_kernel,
         out_shape=jax.ShapeDtypeStruct(tokens.shape, BF16),
         grid=(rows // 16,),
-        in_specs=[blk, blk, blk, blk, pl.BlockSpec((1, width), lambda i: (0, 0))],
+        in_specs=[blk, blk, blk, pl.BlockSpec((*col_back.shape[:2], 16, width), lambda i: (0, 0, i, 0)), pl.BlockSpec((1, width), lambda i: (0, 0))],
         out_specs=blk,
         cost_estimate=pl.CostEstimate(flops=20_000_000, transcendentals=4_000, bytes_accessed=8_000_000),
         name="norm_backward",
@@ -457,9 +457,9 @@
         jnp.pad(right, ((2, 4), (0, 0), (0, 0))),
         jnp.zeros((rows + 10, STRIDE - cols - 4, 2 * width), BF16),
         jnp.pad(left, ((1, 5), (0, 0), (0, 0)))], axis=1)
-    halo = jnp.concatenate([above, below], axis=0)
-    grad_mid, grad_row, grad_col = mlp(
-        saved_mid, grad_out, tokens_in, halo, edge, mlp_gain, w_up, conv_kernel, w_down, w_out)
+    grad_mid, grad_row, grad_col, weights = mlp(
+        saved_mid, grad_out, tokens_in, above, below, edge, mlp_gain, w_up, conv_kernel, w_down, w_out,
+        w_query, w_key, w_value)
     hold = lax.optimization_barrier
     grad_row, row_tokens = hold((grad_row, row_tokens))
     grad_row = to_lines(grad_row.reshape(count_gx, rows // count_gx, cols, half), "gx")
@@ -472,15 +472,14 @@
             part = lax.ppermute(part, "gy", [(i, (i + ahead) % count_gy) for i in range(count_gy)])
         col_parts.append(part)
     col_at = (here - jnp.arange(count_gy, dtype=jnp.int32)) % count_gy
-    weights = (w_query, w_key, w_value)
-    row_out = attention((row_tokens, grad_row), col_at, (count_gx, rows // count_gx, cols), attn_gain, *weights,
+    row_out = attention((row_tokens, grad_row), col_at, (count_gx, rows // count_gx, cols), attn_gain, weights,
                         row_mask, 0)
     row_out, *col_parts = hold((row_out, *col_parts))
     row_back = to_lines(row_out, "gx").reshape(rows, cols, width)
-    col_out = attention(tuple(col_parts), col_at, (count_gy, cols // count_gy, rows), attn_gain, *weights,
+    col_out = attention(tuple(col_parts), col_at, (count_gy, cols // count_gy, rows), attn_gain, weights,
                         col_mask, 1)
     row_back, col_out = hold((row_back, col_out))
-    col_back = jnp.transpose(to_lines(col_out, "gy"), (2, 0, 1, 3)).reshape(rows, cols, width)
+    col_back = to_lines(col_out, "gy")
     return final(tokens_in, grad_mid, row_back, col_back, attn_gain)
 
 

time: 193 us -> 185 us (0.959)
  Pallas kernels: 104 us -> 98.6 us
  starting transfers between devices: 41.9 us -> 45.9 us
  local copies, waits for them, and re-layouts: 10.7 us -> 6.87 us
  waiting for transfers between devices: 4.69 us -> 1.27 us
  blocking collectives: 26.1 us -> 28.2 us
    pallas_call x2, Pallas kernels: 57.9 us -> 51.4 us  [attention(): pl.pallas_call(functools.partial(attn_kernel, nl, nk, half, pieces), out_...]
    ppermute x7, starting transfers between devices: 8.27 us -> 11.4 us  [per_device(): lax.ppermute(part, 'gy', [(i, (i + ahead) % count_gy) for i in range(coun...]
    ppermute x2, waiting for transfers between devices: 2.57 us -> 0.01 us  [neighbours(): lax.ppermute(behind, axis, [(j, i) for i, j in up])]
    all_to_all x1, blocking collectives: 26.1 us -> 28.2 us  [to_lines(): return lax.all_to_all(blocks, axis, split_axis=0, concat_axis=0, tiled=True)]
    reshape x1 -> x0, local copies, waits for them, and re-layouts: 2.04 us -> none  [per_device(): jnp.transpose(to_lines(col_out, 'gy'), (2, 0, 1, 3))]
  transfers between devices with their start and end apart: 14 -> 14, of which waited for: 3 -> 3; matrix products, arithmetic and copies ran while one was open for 4% -> 4% of each run, Pallas kernels for 52% -> 51%
where the time goes in v6:
time: 185 us; the launch traced here: 183 us
  Pallas kernels  98.6 us (53%)
  starting transfers between devices  45.9 us (25%)
  blocking collectives  28.2 us (15%)
  local copies, waits for them, and re-layouts  6.87 us (4%)
    pallas_call x2, Pallas kernels, attention(): pl.pallas_call(functools.partial(attn_kernel, nl, nk, half, pieces), out_...  51.4 us
    pallas_call x1, Pallas kernels, mlp(): pl.pallas_call(functools.partial(mlp_kernel, rows, cols), out_shape=tuple...  41.1 us
    all_to_all x1, blocking collectives, to_lines(): return lax.all_to_all(blocks, axis, split_axis=0, concat_axis=0, tiled=True)  28.2 us
    all_to_all x3, starting transfers between devices, to_lines(): return lax.all_to_all(blocks, axis, split_axis=0, concat_axis=0, tiled=True)  22.4 us
    ppermute x7, starting transfers between devices, per_device(): lax.ppermute(part, 'gy', [(i, (i + ahead) % count_gy) for i in range(coun...  11.4 us
    ppermute x2, starting transfers between devices, neighbours(): lax.ppermute(ahead, axis, up)  7.52 us
    pallas_call x1, Pallas kernels, final(): pl.pallas_call(final_kernel, out_shape=jax.ShapeDtypeStruct(tokens.shape,...  6.15 us
    ppermute x2, starting transfers between devices, neighbours(): lax.ppermute(behind, axis, [(j, i) for i, j in up])  4.62 us
  transfers between devices with their start and end apart: 14, of which 3 were waited for; matrix products, arithmetic and copies ran while one was open for 4% of the time, Pallas kernels for 51%

profile of v6, /device:TPU:1, one launch (start us, length us, event | category | flops | bytes accessed | tf_op | source)
XLA Modules:
  0.0 183.0 jit_solution(10241310675322933667)
XLA Ops:
  0.0 0.9 fusion.7
  0.9 3.3 %collective-permute-start.1 = (bf16[2,48,512]{2,1,0:T(8,128)(2,1)S(1)}, bf16[2,48,512]{2,1,0:T(8,128)(2,1)S(1)}, u32[]{:S(2)}, u32[]{:S(2)}) collective-permute-start(bf16[2,48,512]{2,1,0:T(8,128)(2,1)S(1)} %pad_maximum_fusion.3), channel_id=1, source_target_pairs={{16,0},{32,16},{48,32},{64,48},{80,64},{96,80},{112,96},{17,1},{33... | collective-permute-start | bytes 294920 | tf_op jit(solution)/shard_map/ppermute | solution.py:437
  4.3 3.5 %collective-permute-start = (bf16[2,48,512]{2,1,0:T(8,128)(2,1)S(1)}, bf16[2,48,512]{2,1,0:T(8,128)(2,1)S(1)}, u32[]{:S(2)}, u32[]{:S(2)}) collective-permute-start(bf16[2,48,512]{2,1,0:T(8,128)(2,1)S(1)} %pad_maximum_fusion.2), channel_id=1, source_target_pairs={{0,16},{16,32},{32,48},{48,64},{64,80},{80,96},{96,112},{1,17},{17... | collective-permute-start | bytes 294920 | tf_op jit(solution)/shard_map/ppermute | solution.py:437
  7.8 1.4 fusion.5
  9.2 0.0 collective-permute-done.1.below_ref
  9.2 0.0 copy-start.5
  9.2 0.2 collective-permute-done.above_ref
  9.4 0.0 copy-start.6
  9.4 0.1 pad_maximum_fusion
  9.6 1.3 collective-permute-start.2
  10.9 0.1 pad_maximum_fusion.1
  11.0 4.0 %collective-permute-start.3 = (bf16[68,2,512]{2,1,0:T(2,128)(2,1)S(1)}, bf16[68,2,512]{2,1,0:T(2,128)(2,1)S(1)}, u32[]{:S(2)}, u32[]{:S(2)}) collective-permute-start(bf16[68,2,512]{2,1,0:T(2,128)(2,1)S(1)} %pad_maximum_fusion.1), channel_id=1, source_target_pairs={{0,1},{1,2},{2,3},{3,4},{4,5},{5,6},{6,7},{7,8},{8,9},{9,10},{10,1... | collective-permute-start | bytes 417800 | tf_op jit(solution)/shard_map/ppermute | solution.py:437
  15.0 0.0 copy-done.5
  15.0 0.0 copy-done.6
  15.0 8.7 %all-to-all-start = ((bf16[16,4,48,256]{3,2,1,0:T(8,128)(2,1)}), bf16[16,4,48,256]{3,2,1,0:T(8,128)(2,1)S(1)}, u32[]{:S(2)}, u32[]{:S(2)}) async-start(bf16[16,4,48,256]{3,2,1,0:T(8,128)(2,1)} %bitcast.1), calls=%async_computation | async-start | bytes 3145728 | tf_op jit(solution)/shard_map/all_to_all | solution.py:426
  23.7 0.1 pad.11.clone
  23.8 0.0 collective-permute-done.2
  23.8 0.0 collective-permute-done.3
  23.8 1.5 fusion.2.edge_ref
  25.3 41.1 %mlp_backward.1 = (bf16[64,48,256]{2,1,0:T(8,128)(2,1)}, bf16[64,48,128]{2,1,0:T(8,128)(2,1)}, bf16[64,48,384]{2,1,0:T(8,128)(2,1)}, bf16[2,256,384]{2,1,0:T(8,128)(2,1)}) custom-call(bf16[64,48,256]{2,1,0:T(8,128)(2,1)} %mid_ref.1, bf16[64,48,256]{2,1,0:T(8,128)(2,1)} %gout_ref.1, bf16[64,48,256]{2,1,0:T(8,128)(2,1)} %tok_ref.3, ...), custom_call_target="tpu_custom_call" | custom-call | flops 20000000000 | bytes 12000000 | tf_op jit(solution)/shard_map/mlp_backward/pallas_call | solution.py:197
  66.5 0.0 all-to-all-done.refs_0_
  66.5 6.7 %all-to-all-start.1 = ((bf16[16,4,48,128]{3,2,1,0:T(8,128)(2,1)}), bf16[16,4,48,128]{3,2,1,0:T(8,128)(2,1)S(1)}, u32[]{:S(2)}, u32[]{:S(2)}) async-start(bf16[16,4,48,128]{3,2,1,0:T(8,128)(2,1)} %bitcast.42), calls=%async_computation.1 | async-start | bytes 1572864 | tf_op jit(solution)/shard_map/all_to_all | solution.py:426
  73.3 2.3 %copy.15 = bf16[64,48,384]{2,0,1:T(8,128)(2,1)S(1)} copy(bf16[64,48,384]{2,1,0:T(8,128)(2,1)} %get-tuple-element.27) | data formatting | bytes 4718592 | tf_op jit(solution)/shard_map/mlp_backward/pallas_call | solution.py:197
  75.5 0.0 copy-start
  75.6 0.0 copy-start.1
  75.6 1.2 dynamic-slice_bitcast_fusion
  76.8 0.2 collective-permute-start.10
  77.0 3.6 %collective-permute-start.4 = (bf16[6,64,384]{2,1,0:T(8,128)(2,1)S(1)}, bf16[6,64,384]{2,1,0:T(8,128)(2,1)S(1)}, u32[]{:S(2)}, u32[]{:S(2)}) collective-permute-start(bf16[6,64,384]{2,1,0:T(8,128)(2,1)S(1)} %get-tuple-element.45), channel_id=1, source_target_pairs={{0,16},{16,32},{32,48},{48,64},{64,80},{80,96},{96,112},{112,0},{1... | collective-permute-start | bytes 884744 | tf_op jit(solution)/shard_map/ppermute | solution.py:472
  80.6 1.6 collective-permute-start.5
  82.2 2.5 %collective-permute-start.6 = (bf16[6,64,384]{2,1,0:T(8,128)(2,1)}, bf16[6,64,384]{2,1,0:T(8,128)(2,1)}, u32[]{:S(2)}, u32[]{:S(2)}) collective-permute-start(bf16[6,64,384]{2,1,0:T(8,128)(2,1)} %get-tuple-element.43), channel_id=1, source_target_pairs={{0,48},{16,64},{32,80},{48,96},{64,112},{80,0},{96,16},{112,32},{1... | collective-permute-start | bytes 884744 | tf_op jit(solution)/shard_map/ppermute | solution.py:472
  84.7 0.0 collective-permute-start.7
  84.7 0.6 collective-permute-done.10.refs_7_
  85.3 2.1 %collective-permute-start.8 = (bf16[6,64,384]{2,1,0:T(8,128)(2,1)}, bf16[6,64,384]{2,1,0:T(8,128)(2,1)}, u32[]{:S(2)}, u32[]{:S(2)}) collective-permute-start(bf16[6,64,384]{2,1,0:T(8,128)(2,1)} %get-tuple-element.41), channel_id=1, source_target_pairs={{0,80},{16,96},{32,112},{48,0},{64,16},{80,32},{96,48},{112,64},{1... | collective-permute-start | bytes 884744 | tf_op jit(solution)/shard_map/ppermute | solution.py:472
  87.4 0.0 collective-permute-done.4.refs_1_
  87.4 1.3 collective-permute-start.9
  88.7 0.0 all-to-all-done.1.refs_1_
  88.7 0.0 copy-done
  88.7 0.0 copy-done.1
  88.7 0.0 copy-start.3
  88.8 1.0 copy-done.3
  89.7 31.8 %axial_attention.2 = bf16[16,4,48,256]{3,2,1,0:T(8,128)(2,1)} custom-call(s32[6,6]{1,0:T(8,128)S(1)} %copy-done.1, s32[8]{0:T(128)S(1)} %and_select_fusion.at_ref, bf16[16,4,48,256]{3,2,1,0:T(8,128)(2,1)S(1)} %all-to-all-done.refs_0_, bf16[16,4,48,128]{3,2,1,0:T(8,128)(2,1)S(1)} %all-to-all-done.1.refs_1_, f32[1,256]{1,0:T(1,128)S(1)} %bitcast.39, ...), custom_call_target="tpu_custom_call" | custom-call | flops 28800000000 | bytes 4000000 | tf_op jit(solution)/shard_map/axial_attention/pallas_call | solution.py:369
  121.5 0.0 collective-permute-done.5.refs_2_
  121.5 0.0 collective-permute-done.6.refs_3_
  121.5 0.0 collective-permute-done.7.refs_4_
  121.5 0.0 collective-permute-done.8.refs_5_
  121.5 0.0 collective-permute-done.9.refs_6_
  121.5 0.0 copy-start.2
  121.6 0.0 copy-start.4
  121.6 7.0 %all-to-all-start.2 = ((bf16[16,4,48,256]{3,2,1,0:T(8,128)(2,1)}), bf16[16,4,48,256]{3,2,1,0:T(8,128)(2,1)}, u32[]{:S(2)}, u32[]{:S(2)}) async-start(bf16[16,4,48,256]{3,2,1,0:T(8,128)(2,1)} %axial_attention.2), calls=%async_computation.2 | async-start | bytes 3145728 | tf_op jit(solution)/shard_map/all_to_all | solution.py:426
  128.6 0.0 copy-done.2
  128.6 0.0 copy-done.4
  128.6 19.6 %axial_attention.3 = bf16[8,6,64,256]{3,2,1,0:T(8,128)(2,1)S(1)} custom-call(s32[4,4]{1,0:T(4,128)S(1)} %copy-done.2, s32[8]{0:T(128)S(1)} %and_select_fusion.at_ref, bf16[6,64,384]{2,1,0:T(8,128)(2,1)S(1)} %get-tuple-element.29.refs_0_, bf16[6,64,384]{2,1,0:T(8,128)(2,1)S(1)} %collective-permute-done.4.refs_1_, ...), custom_call_target="tpu_custom_call" | custom-call | flops 19200000000 | bytes 4000000 | tf_op jit(solution)/shard_map/axial_attention/pallas_call | solution.py:369
  148.2 0.5 all-to-all-done.2
  148.7 28.2 %all_to_all.20.col_ref = bf16[8,6,64,256]{3,2,1,0:T(8,128)(2,1)} all-to-all(bf16[8,6,64,256]{3,2,1,0:T(8,128)(2,1)S(1)} %axial_attention.3), channel_id=1, replica_groups=mesh['gy'=8,'gx'=16] {'gy'}, dimensions={0} | all-to-all | bytes 3145728 | tf_op jit(solution)/shard_map/all_to_all | solution.py:426
  176.9 6.2 %norm_backward.1 = bf16[64,48,256]{2,1,0:T(8,128)(2,1)} custom-call(bf16[64,48,256]{2,1,0:T(8,128)(2,1)} %tok_ref.3, bf16[64,48,256]{2,1,0:T(8,128)(2,1)} %get-tuple-element.22.mid_ref, bf16[64,48,256]{2,1,0:T(8,128)(2,1)} %bitcast.21.row_ref, bf16[8,6,64,256]{3,2,1,0:T(8,128)(2,1)} %all_to_all.20.col_ref, f32[1,256]{1,0:T(1,128)} %bitcast.38), custom_call_target="tpu_custom_call" | custom-call | flops 20000000 | bytes 8000000 | tf_op jit(solution)/shard_map/norm_backward/pallas_call | solution.py:414
  (6 shorter events, 0.1 us)
Async XLA Ops:
  0.9 8.3 %collective-permute-start.1 = (bf16[2,48,512]{2,1,0:T(8,128)(2,1)S(1)}, bf16[2,48,512]{2,1,0:T(8,128)(2,1)S(1)}, u32[]{:S(2)}, u32[]{:S(2)}) collective-permute-start(bf16[2,48,512]{2,1,0:T(8,128)(2,1)S(1)} %pad_maximum_fusion.3), channel_id=1, source_target_pairs={{16,0},{32,16},{48,32},{64,48},{80,64},{96,80},{112,96},{17,1},{33... | collective-permute-start | bytes 294920 | tf_op jit(solution)/shard_map/ppermute | solution.py:437
  4.3 5.2 %collective-permute-start = (bf16[2,48,512]{2,1,0:T(8,128)(2,1)S(1)}, bf16[2,48,512]{2,1,0:T(8,128)(2,1)S(1)}, u32[]{:S(2)}, u32[]{:S(2)}) collective-permute-start(bf16[2,48,512]{2,1,0:T(8,128)(2,1)S(1)} %pad_maximum_fusion.2), channel_id=1, source_target_pairs={{0,16},{16,32},{32,48},{48,64},{64,80},{80,96},{96,112},{1,17},{17... | collective-permute-start | bytes 294920 | tf_op jit(solution)/shard_map/ppermute | solution.py:437
  9.2 5.8 %copy-start.5 = (bf16[2,48,512]{2,1,0:T(8,128)(2,1)}, bf16[2,48,512]{2,1,0:T(8,128)(2,1)S(1)}, u32[]{:S(2)}) copy-start(bf16[2,48,512]{2,1,0:T(8,128)(2,1)S(1)} %collective-permute-done.1.below_ref) | copy-start | bytes 294916
  9.4 5.6 %copy-start.6 = (bf16[2,48,512]{2,1,0:T(8,128)(2,1)}, bf16[2,48,512]{2,1,0:T(8,128)(2,1)S(1)}, u32[]{:S(2)}) copy-start(bf16[2,48,512]{2,1,0:T(8,128)(2,1)S(1)} %collective-permute-done.above_ref) | copy-start | bytes 294916
  9.6 14.2 %collective-permute-start.2 = (bf16[68,2,512]{2,1,0:T(2,128)(2,1)S(1)}, bf16[68,2,512]{2,1,0:T(2,128)(2,1)S(1)}, u32[]{:S(2)}, u32[]{:S(2)}) collective-permute-start(bf16[68,2,512]{2,1,0:T(2,128)(2,1)S(1)} %pad_maximum_fusion), channel_id=1, source_target_pairs={{1,0},{2,1},{3,2},{4,3},{5,4},{6,5},{7,6},{8,7},{9,8},{10,9},{11,1... | collective-permute-start | bytes 417800 | tf_op jit(solution)/shard_map/ppermute | solution.py:437
  11.0 12.8 %collective-permute-start.3 = (bf16[68,2,512]{2,1,0:T(2,128)(2,1)S(1)}, bf16[68,2,512]{2,1,0:T(2,128)(2,1)S(1)}, u32[]{:S(2)}, u32[]{:S(2)}) collective-permute-start(bf16[68,2,512]{2,1,0:T(2,128)(2,1)S(1)} %pad_maximum_fusion.1), channel_id=1, source_target_pairs={{0,1},{1,2},{2,3},{3,4},{4,5},{5,6},{6,7},{7,8},{8,9},{9,10},{10,1... | collective-permute-start | bytes 417800 | tf_op jit(solution)/shard_map/ppermute | solution.py:437
  15.0 51.5 %all-to-all-start = ((bf16[16,4,48,256]{3,2,1,0:T(8,128)(2,1)}), bf16[16,4,48,256]{3,2,1,0:T(8,128)(2,1)S(1)}, u32[]{:S(2)}, u32[]{:S(2)}) async-start(bf16[16,4,48,256]{3,2,1,0:T(8,128)(2,1)} %bitcast.1), calls=%async_computation | async-start | bytes 3145728 | tf_op jit(solution)/shard_map/all_to_all | solution.py:426
  66.5 22.3 %all-to-all-start.1 = ((bf16[16,4,48,128]{3,2,1,0:T(8,128)(2,1)}), bf16[16,4,48,128]{3,2,1,0:T(8,128)(2,1)S(1)}, u32[]{:S(2)}, u32[]{:S(2)}) async-start(bf16[16,4,48,128]{3,2,1,0:T(8,128)(2,1)} %bitcast.42), calls=%async_computation.1 | async-start | bytes 1572864 | tf_op jit(solution)/shard_map/all_to_all | solution.py:426
  75.5 13.2 %copy-start = (f32[256]{0:T(256)S(1)}, f32[256]{0:T(256)}, u32[]{:S(2)}) copy-start(f32[256]{0:T(256)} %param.17) | copy-start | bytes 3076
  75.6 13.2 %copy-start.1 = (s32[6,6]{1,0:T(8,128)S(1)}, s32[6,6]{1,0:T(8,128)}, u32[]{:S(2)}) copy-start(s32[6,6]{1,0:T(8,128)} %mask_ref.2) | copy-start | bytes 436
  76.8 8.5 %collective-permute-start.10 = (bf16[6,64,384]{2,1,0:T(8,128)(2,1)S(1)}, bf16[6,64,384]{2,1,0:T(8,128)(2,1)S(1)}, u32[]{:S(2)}, u32[]{:S(2)}) collective-permute-start(bf16[6,64,384]{2,1,0:T(8,128)(2,1)S(1)} %get-tuple-element.39), channel_id=1, source_target_pairs={{0,112},{16,0},{32,16},{48,32},{64,48},{80,64},{96,80},{112,96},{1... | collective-permute-start | bytes 884744 | tf_op jit(solution)/shard_map/ppermute | solution.py:472
  77.0 10.4 %collective-permute-start.4 = (bf16[6,64,384]{2,1,0:T(8,128)(2,1)S(1)}, bf16[6,64,384]{2,1,0:T(8,128)(2,1)S(1)}, u32[]{:S(2)}, u32[]{:S(2)}) collective-permute-start(bf16[6,64,384]{2,1,0:T(8,128)(2,1)S(1)} %get-tuple-element.45), channel_id=1, source_target_pairs={{0,16},{16,32},{32,48},{48,64},{64,80},{80,96},{96,112},{112,0},{1... | collective-permute-start | bytes 884744 | tf_op jit(solution)/shard_map/ppermute | solution.py:472
  80.6 40.9 %collective-permute-start.5 = (bf16[6,64,384]{2,1,0:T(8,128)(2,1)}, bf16[6,64,384]{2,1,0:T(8,128)(2,1)S(1)}, u32[]{:S(2)}, u32[]{:S(2)}) collective-permute-start(bf16[6,64,384]{2,1,0:T(8,128)(2,1)} %get-tuple-element.44), channel_id=1, source_target_pairs={{0,32},{16,48},{32,64},{48,80},{64,96},{80,112},{96,0},{112,16},{1... | collective-permute-start | bytes 884744 | tf_op jit(solution)/shard_map/ppermute | solution.py:472
  82.2 39.3 %collective-permute-start.6 = (bf16[6,64,384]{2,1,0:T(8,128)(2,1)}, bf16[6,64,384]{2,1,0:T(8,128)(2,1)}, u32[]{:S(2)}, u32[]{:S(2)}) collective-permute-start(bf16[6,64,384]{2,1,0:T(8,128)(2,1)} %get-tuple-element.43), channel_id=1, source_target_pairs={{0,48},{16,64},{32,80},{48,96},{64,112},{80,0},{96,16},{112,32},{1... | collective-permute-start | bytes 884744 | tf_op jit(solution)/shard_map/ppermute | solution.py:472
  84.7 36.8 %collective-permute-start.7 = (bf16[6,64,384]{2,1,0:T(8,128)(2,1)}, bf16[6,64,384]{2,1,0:T(8,128)(2,1)}, u32[]{:S(2)}, u32[]{:S(2)}) collective-permute-start(bf16[6,64,384]{2,1,0:T(8,128)(2,1)} %get-tuple-element.42), channel_id=1, source_target_pairs={{0,64},{16,80},{32,96},{48,112},{64,0},{80,16},{96,32},{112,48},{1... | collective-permute-start | bytes 884744 | tf_op jit(solution)/shard_map/ppermute | solution.py:472
  85.3 36.3 %collective-permute-start.8 = (bf16[6,64,384]{2,1,0:T(8,128)(2,1)}, bf16[6,64,384]{2,1,0:T(8,128)(2,1)}, u32[]{:S(2)}, u32[]{:S(2)}) collective-permute-start(bf16[6,64,384]{2,1,0:T(8,128)(2,1)} %get-tuple-element.41), channel_id=1, source_target_pairs={{0,80},{16,96},{32,112},{48,0},{64,16},{80,32},{96,48},{112,64},{1... | collective-permute-start | bytes 884744 | tf_op jit(solution)/shard_map/ppermute | solution.py:472
  87.4 34.1 %collective-permute-start.9 = (bf16[6,64,384]{2,1,0:T(8,128)(2,1)}, bf16[6,64,384]{2,1,0:T(8,128)(2,1)}, u32[]{:S(2)}, u32[]{:S(2)}) collective-permute-start(bf16[6,64,384]{2,1,0:T(8,128)(2,1)} %get-tuple-element.40), channel_id=1, source_target_pairs={{0,96},{16,112},{32,0},{48,16},{64,32},{80,48},{96,64},{112,80},{1... | collective-permute-start | bytes 884744 | tf_op jit(solution)/shard_map/ppermute | solution.py:472
  88.7 1.0 copy-start.3
  121.5 7.0 %copy-start.2 = (s32[4,4]{1,0:T(4,128)S(1)}, s32[4,4]{1,0:T(4,128)}, u32[]{:S(2)}) copy-start(s32[4,4]{1,0:T(4,128)} %mask_ref.3) | copy-start | bytes 196
  121.6 7.0 %copy-start.4 = (bf16[2,256,384]{2,1,0:T(8,128)(2,1)S(1)}, bf16[2,256,384]{2,1,0:T(8,128)(2,1)}, u32[]{:S(2)}) copy-start(bf16[2,256,384]{2,1,0:T(8,128)(2,1)} %get-tuple-element.26.refs_3_.refs_9_) | copy-start | bytes 1179652
  121.6 27.1 %all-to-all-start.2 = ((bf16[16,4,48,256]{3,2,1,0:T(8,128)(2,1)}), bf16[16,4,48,256]{3,2,1,0:T(8,128)(2,1)}, u32[]{:S(2)}, u32[]{:S(2)}) async-start(bf16[16,4,48,256]{3,2,1,0:T(8,128)(2,1)} %axial_attention.2), calls=%async_computation.2 | async-start | bytes 3145728 | tf_op jit(solution)/shard_map/all_to_all | solution.py:426

commit v7 on v6

--- a/solution.py
+++ b/solution.py
@@ -21,7 +21,7 @@
 BIG = 8
 GUARD = 2
 RING = 3 * GROUP
-FC = 512
+FC = 256
 
 
 def dot_nt(a, b):
@@ -44,7 +44,7 @@
 
 def mlp_kernel(rows, cols, mid_ref, gout_ref, tok_ref, above_ref, below_ref, edge_ref, gain_ref, wup_ref, conv_ref, wdown_ref, wout_ref,
                wq_ref, wk_ref, wv_ref,
-               gm_ref, grow_ref, gcol_ref, wide_ref, x_s, h_s, gp_s, y_s, wdt_s, wut_s, grad_s):
+               gm_ref, grow_ref, gcol_ref, wide_ref, x_s, y_s, wdt_s, wut_s, grad_s, *rings):
     width = mid_ref.shape[-1]
     gain = gain_ref[...]
     held = rows + 8
@@ -107,6 +107,8 @@
     wut_s[...] = wup_ref[...].astype(F32).T.astype(BF16)
     taps = [conv_ref[t:t + 1, :].astype(BF16) for t in range(9)]
     hidden = wup_ref.shape[1]
+    parts_of = hidden // FC
+    h_parts, gp_parts = rings[:parts_of], rings[parts_of:]
 
     def slot(row):
         return pl.ds(rows_at(lax.rem(row + 2 * RING, RING)), STRIDE)
@@ -114,52 +116,59 @@
     def products(i):
         z0 = GROUP * (i - 2) - 2
         for b in range(3):
-            parts = []
-            for sub in range(GROUP):
-                z = None
-                for a in range(3):
-                    term = gp_s[slot(z0 + 1 - a + sub), :] * taps[3 * a + b]
-                    z = term if z is None else z + term
-                parts.append(z)
+            stack = []
+            for part in range(parts_of):
+                lanes = slice(part * FC, (part + 1) * FC)
+                pile = []
+                for sub in range(GROUP):
+                    z = None
+                    for a in range(3):
+                        term = gp_parts[part][slot(z0 + 1 - a + sub), :] * taps[3 * a + b][:, lanes]
+                        z = term if z is None else z + term
+                    pile.append(z)
+                stack.append(jnp.concatenate(pile, axis=0))
             y_s[b, pl.ds(rows_at(z0 + GUARD), CHUNK), :] = jnp.dot(
-                jnp.concatenate(parts, axis=0), wut_s[...], preferred_element_type=F32)
-
-    def slopes(i):
+                jnp.concatenate(stack, axis=1), wut_s[...], preferred_element_type=F32)
+
+    def slopes(i, part):
         g0 = GROUP * (i - 1) - 1
+        h_s, gp_s = h_parts[part], gp_parts[part]
         grads = grad_s[pl.ds(rows_at(jnp.clip(g0 + 1, 0, held + 2 - GROUP)), CHUNK), :]
-        for at in range(0, hidden, FC):
-            lanes = slice(at, at + FC)
-            ga = jnp.dot(grads, wdt_s[:, lanes], preferred_element_type=F32)
-            for sub in range(GROUP):
-                pre = None
-                for a in range(3):
-                    for b in range(3):
-                        term = h_s[b, slot(g0 + a - 1 + sub), lanes] * taps[3 * a + b][:, lanes]
-                        pre = term if pre is None else pre + term
-                gp_s[slot(g0 + sub), lanes] = (
-                    ga[sub * STRIDE:(sub + 1) * STRIDE] * gelu_slope(pre).astype(F32)).astype(BF16)
-
-    def project(i):
+        lanes = slice(part * FC, (part + 1) * FC)
+        ga = jnp.dot(grads, wdt_s[:, lanes], preferred_element_type=F32)
+        for sub in range(GROUP):
+            pre = None
+            for a in range(3):
+                for b in range(3):
+                    term = h_s[b, slot(g0 + a - 1 + sub), :] * taps[3 * a + b][:, lanes]
+                    pre = term if pre is None else pre + term
+            gp_s[slot(g0 + sub), :] = (
+                ga[sub * STRIDE:(sub + 1) * STRIDE] * gelu_slope(pre).astype(F32)).astype(BF16)
+
+    def project(i, part):
         src = pl.ds(rows_at(jnp.minimum(GROUP * i, held - GROUP)), CHUNK)
         dst = pl.ds(rows_at(lax.rem(GROUP * i, RING)), CHUNK)
+        lanes = slice(part * FC, (part + 1) * FC)
         for b in range(3):
-            for at in range(0, hidden, FC):
-                lanes = slice(at, at + FC)
-                h_s[b, dst, lanes] = jnp.dot(
-                    x_s[b, src, :], wup_ref[:, lanes], preferred_element_type=F32).astype(BF16)
+            h_parts[part][b, dst, :] = jnp.dot(
+                x_s[b, src, :], wup_ref[:, lanes], preferred_element_type=F32).astype(BF16)
 
     def body(i, c):
         products(i)
-        slopes(i)
-        project(i)
+        for part in range(parts_of):
+            slopes(i, part)
+            project(i, part)
         return c
 
-    project(0)
-    slopes(1)
-    project(1)
+    for part in range(parts_of):
+        project(0, part)
+    for part in range(parts_of):
+        slopes(1, part)
+        project(1, part)
     lax.fori_loop(2, trips - 2, body, 0)
     products(trips - 2)
-    slopes(trips - 2)
+    for part in range(parts_of):
+        slopes(trips - 2, part)
     products(trips - 1)
 
     def finish(i, c):
@@ -202,13 +211,12 @@
         out_specs=(whole,) * 4,
         scratch_shapes=[
             pltpu.VMEM((3, held * STRIDE, width), BF16),
-            pltpu.VMEM((3, RING * STRIDE, hidden), BF16),
-            pltpu.VMEM((RING * STRIDE, hidden), BF16),
             pltpu.VMEM((3, slots, width), F32),
             pltpu.VMEM((width, hidden), BF16),
             pltpu.VMEM((hidden, width), BF16),
             pltpu.VMEM(((rows + 10) * STRIDE, width), BF16),
-        ],
+        ] + [pltpu.VMEM((3, RING * STRIDE, FC), BF16)] * (hidden // FC)
+        + [pltpu.VMEM((RING * STRIDE, FC), BF16)] * (hidden // FC),
         compiler_params=pltpu.CompilerParams(vmem_limit_bytes=54 * 1024 * 1024),
         cost_estimate=pl.CostEstimate(flops=20_000_000_000, transcendentals=4_000_000, bytes_accessed=12_000_000),
         name="mlp_backward",

time: 185 us -> 180 us (0.973)
  Pallas kernels: 98.6 us -> 92.2 us
    pallas_call x2, Pallas kernels: 51.4 us -> 48 us  [attention(): pl.pallas_call(functools.partial(attn_kernel, nl, nk, half, pieces), out_...]
    pallas_call x1, Pallas kernels: 41.1 us -> 38.1 us  [mlp(): pl.pallas_call(functools.partial(mlp_kernel, rows, cols), out_shape=tuple...]
  transfers between devices with their start and end apart: 14 -> 14, of which waited for: 3 -> 3; matrix products, arithmetic and copies ran while one was open for 4% -> 4% of each run, Pallas kernels for 51% -> 49%
where the time goes in v7:
time: 180 us; the launch traced here: 177 us
  Pallas kernels  92.2 us (51%)
  starting transfers between devices  45.8 us (25%)
  blocking collectives  28.2 us (16%)
  local copies, waits for them, and re-layouts  6.87 us (4%)
  other arithmetic  1.8 us (1%)
    pallas_call x2, Pallas kernels, attention(): pl.pallas_call(functools.partial(attn_kernel, nl, nk, half, pieces), out_...  48 us
    pallas_call x1, Pallas kernels, mlp(): pl.pallas_call(functools.partial(mlp_kernel, rows, cols), out_shape=tuple...  38.1 us
    all_to_all x1, blocking collectives, to_lines(): return lax.all_to_all(blocks, axis, split_axis=0, concat_axis=0, tiled=True)  28.2 us
    all_to_all x3, starting transfers between devices, to_lines(): return lax.all_to_all(blocks, axis, split_axis=0, concat_axis=0, tiled=True)  22.4 us
    ppermute x7, starting transfers between devices, per_device(): lax.ppermute(part, 'gy', [(i, (i + ahead) % count_gy) for i in range(coun...  11.3 us
    ppermute x2, starting transfers between devices, neighbours(): lax.ppermute(ahead, axis, up)  7.52 us
    pallas_call x1, Pallas kernels, final(): pl.pallas_call(final_kernel, out_shape=jax.ShapeDtypeStruct(tokens.shape,...  6.15 us
    ppermute x2, starting transfers between devices, neighbours(): lax.ppermute(behind, axis, [(j, i) for i, j in up])  4.62 us
  transfers between devices with their start and end apart: 14, of which 3 were waited for; matrix products, arithmetic and copies ran while one was open for 4% of the time, Pallas kernels for 49%

profile of v7, /device:TPU:1, one launch (start us, length us, event | category | flops | bytes accessed | tf_op | source)
XLA Modules:
  0.0 176.6 jit_solution(5468685809632669190)
XLA Ops:
  0.0 0.9 fusion.7
  0.9 3.3 %collective-permute-start.1 = (bf16[2,48,512]{2,1,0:T(8,128)(2,1)S(1)}, bf16[2,48,512]{2,1,0:T(8,128)(2,1)S(1)}, u32[]{:S(2)}, u32[]{:S(2)}) collective-permute-start(bf16[2,48,512]{2,1,0:T(8,128)(2,1)S(1)} %pad_maximum_fusion.3), channel_id=1, source_target_pairs={{16,0},{32,16},{48,32},{64,48},{80,64},{96,80},{112,96},{17,1},{33... | collective-permute-start | bytes 294920 | tf_op jit(solution)/shard_map/ppermute | solution.py:445
  4.3 3.5 %collective-permute-start = (bf16[2,48,512]{2,1,0:T(8,128)(2,1)S(1)}, bf16[2,48,512]{2,1,0:T(8,128)(2,1)S(1)}, u32[]{:S(2)}, u32[]{:S(2)}) collective-permute-start(bf16[2,48,512]{2,1,0:T(8,128)(2,1)S(1)} %pad_maximum_fusion.2), channel_id=1, source_target_pairs={{0,16},{16,32},{32,48},{48,64},{64,80},{80,96},{96,112},{1,17},{17... | collective-permute-start | bytes 294920 | tf_op jit(solution)/shard_map/ppermute | solution.py:445
  7.8 1.4 fusion.5
  9.2 0.0 collective-permute-done.1.below_ref
  9.2 0.0 copy-start.5
  9.2 0.2 collective-permute-done.above_ref
  9.4 0.0 copy-start.6
  9.4 0.1 pad_maximum_fusion
  9.6 1.3 collective-permute-start.2
  10.9 0.1 pad_maximum_fusion.1
  11.0 4.0 %collective-permute-start.3 = (bf16[68,2,512]{2,1,0:T(2,128)(2,1)S(1)}, bf16[68,2,512]{2,1,0:T(2,128)(2,1)S(1)}, u32[]{:S(2)}, u32[]{:S(2)}) collective-permute-start(bf16[68,2,512]{2,1,0:T(2,128)(2,1)S(1)} %pad_maximum_fusion.1), channel_id=1, source_target_pairs={{0,1},{1,2},{2,3},{3,4},{4,5},{5,6},{6,7},{7,8},{8,9},{9,10},{10,1... | collective-permute-start | bytes 417800 | tf_op jit(solution)/shard_map/ppermute | solution.py:445
  15.0 0.0 copy-done.5
  15.0 0.0 copy-done.6
  15.0 8.7 %all-to-all-start = ((bf16[16,4,48,256]{3,2,1,0:T(8,128)(2,1)}), bf16[16,4,48,256]{3,2,1,0:T(8,128)(2,1)S(1)}, u32[]{:S(2)}, u32[]{:S(2)}) async-start(bf16[16,4,48,256]{3,2,1,0:T(8,128)(2,1)} %bitcast.1), calls=%async_computation | async-start | bytes 3145728 | tf_op jit(solution)/shard_map/all_to_all | solution.py:434
  23.7 0.1 pad.11.clone
  23.8 0.0 collective-permute-done.2
  23.8 0.0 collective-permute-done.3
  23.8 1.5 fusion.2.edge_ref
  25.3 38.1 %mlp_backward.1 = (bf16[64,48,256]{2,1,0:T(8,128)(2,1)}, bf16[64,48,128]{2,1,0:T(8,128)(2,1)}, bf16[64,48,384]{2,1,0:T(8,128)(2,1)}, bf16[2,256,384]{2,1,0:T(8,128)(2,1)}) custom-call(bf16[64,48,256]{2,1,0:T(8,128)(2,1)} %mid_ref.1, bf16[64,48,256]{2,1,0:T(8,128)(2,1)} %gout_ref.1, bf16[64,48,256]{2,1,0:T(8,128)(2,1)} %tok_ref.3, ...), custom_call_target="tpu_custom_call" | custom-call | flops 20000000000 | bytes 12000000 | tf_op jit(solution)/shard_map/mlp_backward/pallas_call | solution.py:206
  63.4 0.0 all-to-all-done.refs_0_
  63.4 6.7 %all-to-all-start.1 = ((bf16[16,4,48,128]{3,2,1,0:T(8,128)(2,1)}), bf16[16,4,48,128]{3,2,1,0:T(8,128)(2,1)S(1)}, u32[]{:S(2)}, u32[]{:S(2)}) async-start(bf16[16,4,48,128]{3,2,1,0:T(8,128)(2,1)} %bitcast.42), calls=%async_computation.1 | async-start | bytes 1572864 | tf_op jit(solution)/shard_map/all_to_all | solution.py:434
  70.2 2.3 %copy.15 = bf16[64,48,384]{2,0,1:T(8,128)(2,1)S(1)} copy(bf16[64,48,384]{2,1,0:T(8,128)(2,1)} %get-tuple-element.27) | data formatting | bytes 4718592 | tf_op jit(solution)/shard_map/mlp_backward/pallas_call | solution.py:206
  72.5 0.0 copy-start
  72.5 0.0 copy-start.1
  72.5 1.2 dynamic-slice_bitcast_fusion
  73.7 0.2 collective-permute-start.10
  73.9 3.6 %collective-permute-start.4 = (bf16[6,64,384]{2,1,0:T(8,128)(2,1)S(1)}, bf16[6,64,384]{2,1,0:T(8,128)(2,1)S(1)}, u32[]{:S(2)}, u32[]{:S(2)}) collective-permute-start(bf16[6,64,384]{2,1,0:T(8,128)(2,1)S(1)} %get-tuple-element.45), channel_id=1, source_target_pairs={{0,16},{16,32},{32,48},{48,64},{64,80},{80,96},{96,112},{112,0},{1... | collective-permute-start | bytes 884744 | tf_op jit(solution)/shard_map/ppermute | solution.py:480
  77.5 1.6 collective-permute-start.5
  79.1 2.4 %collective-permute-start.6 = (bf16[6,64,384]{2,1,0:T(8,128)(2,1)}, bf16[6,64,384]{2,1,0:T(8,128)(2,1)}, u32[]{:S(2)}, u32[]{:S(2)}) collective-permute-start(bf16[6,64,384]{2,1,0:T(8,128)(2,1)} %get-tuple-element.43), channel_id=1, source_target_pairs={{0,48},{16,64},{32,80},{48,96},{64,112},{80,0},{96,16},{112,32},{1... | collective-permute-start | bytes 884744 | tf_op jit(solution)/shard_map/ppermute | solution.py:480
  81.6 0.0 collective-permute-start.7
  81.6 0.6 collective-permute-done.10.refs_7_
  82.2 2.1 %collective-permute-start.8 = (bf16[6,64,384]{2,1,0:T(8,128)(2,1)}, bf16[6,64,384]{2,1,0:T(8,128)(2,1)}, u32[]{:S(2)}, u32[]{:S(2)}) collective-permute-start(bf16[6,64,384]{2,1,0:T(8,128)(2,1)} %get-tuple-element.41), channel_id=1, source_target_pairs={{0,80},{16,96},{32,112},{48,0},{64,16},{80,32},{96,48},{112,64},{1... | collective-permute-start | bytes 884744 | tf_op jit(solution)/shard_map/ppermute | solution.py:480
  84.3 0.0 collective-permute-done.4.refs_1_
  84.3 1.3 collective-permute-start.9
  85.6 0.0 all-to-all-done.1.refs_1_
  85.6 0.0 copy-done
  85.6 0.0 copy-done.1
  85.6 0.0 copy-start.3
  85.6 1.0 copy-done.3
  86.6 28.4 %axial_attention.2 = bf16[16,4,48,256]{3,2,1,0:T(8,128)(2,1)} custom-call(s32[6,6]{1,0:T(8,128)S(1)} %copy-done.1, s32[8]{0:T(128)S(1)} %and_select_fusion.at_ref, bf16[16,4,48,256]{3,2,1,0:T(8,128)(2,1)S(1)} %all-to-all-done.refs_0_, bf16[16,4,48,128]{3,2,1,0:T(8,128)(2,1)S(1)} %all-to-all-done.1.refs_1_, f32[1,256]{1,0:T(1,128)S(1)} %bitcast.39, ...), custom_call_target="tpu_custom_call" | custom-call | flops 28800000000 | bytes 4000000 | tf_op jit(solution)/shard_map/axial_attention/pallas_call | solution.py:377
  115.1 0.0 collective-permute-done.5.refs_2_
  115.1 0.0 collective-permute-done.6.refs_3_
  115.1 0.0 collective-permute-done.7.refs_4_
  115.1 0.0 collective-permute-done.8.refs_5_
  115.1 0.0 collective-permute-done.9.refs_6_
  115.1 0.0 copy-start.2
  115.1 0.0 copy-start.4
  115.1 7.0 %all-to-all-start.2 = ((bf16[16,4,48,256]{3,2,1,0:T(8,128)(2,1)}), bf16[16,4,48,256]{3,2,1,0:T(8,128)(2,1)}, u32[]{:S(2)}, u32[]{:S(2)}) async-start(bf16[16,4,48,256]{3,2,1,0:T(8,128)(2,1)} %axial_attention.2), calls=%async_computation.2 | async-start | bytes 3145728 | tf_op jit(solution)/shard_map/all_to_all | solution.py:434
  122.1 0.0 copy-done.2
  122.1 0.0 copy-done.4
  122.1 19.6 %axial_attention.3 = bf16[8,6,64,256]{3,2,1,0:T(8,128)(2,1)S(1)} custom-call(s32[4,4]{1,0:T(4,128)S(1)} %copy-done.2, s32[8]{0:T(128)S(1)} %and_select_fusion.at_ref, bf16[6,64,384]{2,1,0:T(8,128)(2,1)S(1)} %get-tuple-element.29.refs_0_, bf16[6,64,384]{2,1,0:T(8,128)(2,1)S(1)} %collective-permute-done.4.refs_1_, ...), custom_call_target="tpu_custom_call" | custom-call | flops 19200000000 | bytes 4000000 | tf_op jit(solution)/shard_map/axial_attention/pallas_call | solution.py:377
  141.8 0.5 all-to-all-done.2
  142.2 28.2 %all_to_all.20.col_ref = bf16[8,6,64,256]{3,2,1,0:T(8,128)(2,1)} all-to-all(bf16[8,6,64,256]{3,2,1,0:T(8,128)(2,1)S(1)} %axial_attention.3), channel_id=1, replica_groups=mesh['gy'=8,'gx'=16] {'gy'}, dimensions={0} | all-to-all | bytes 3145728 | tf_op jit(solution)/shard_map/all_to_all | solution.py:434
  170.4 6.2 %norm_backward.1 = bf16[64,48,256]{2,1,0:T(8,128)(2,1)} custom-call(bf16[64,48,256]{2,1,0:T(8,128)(2,1)} %tok_ref.3, bf16[64,48,256]{2,1,0:T(8,128)(2,1)} %get-tuple-element.22.mid_ref, bf16[64,48,256]{2,1,0:T(8,128)(2,1)} %bitcast.21.row_ref, bf16[8,6,64,256]{3,2,1,0:T(8,128)(2,1)} %all_to_all.20.col_ref, f32[1,256]{1,0:T(1,128)} %bitcast.38), custom_call_target="tpu_custom_call" | custom-call | flops 20000000 | bytes 8000000 | tf_op jit(solution)/shard_map/norm_backward/pallas_call | solution.py:422
  (6 shorter events, 0.1 us)
Async XLA Ops:
  0.9 8.3 %collective-permute-start.1 = (bf16[2,48,512]{2,1,0:T(8,128)(2,1)S(1)}, bf16[2,48,512]{2,1,0:T(8,128)(2,1)S(1)}, u32[]{:S(2)}, u32[]{:S(2)}) collective-permute-start(bf16[2,48,512]{2,1,0:T(8,128)(2,1)S(1)} %pad_maximum_fusion.3), channel_id=1, source_target_pairs={{16,0},{32,16},{48,32},{64,48},{80,64},{96,80},{112,96},{17,1},{33... | collective-permute-start | bytes 294920 | tf_op jit(solution)/shard_map/ppermute | solution.py:445
  4.3 5.2 %collective-permute-start = (bf16[2,48,512]{2,1,0:T(8,128)(2,1)S(1)}, bf16[2,48,512]{2,1,0:T(8,128)(2,1)S(1)}, u32[]{:S(2)}, u32[]{:S(2)}) collective-permute-start(bf16[2,48,512]{2,1,0:T(8,128)(2,1)S(1)} %pad_maximum_fusion.2), channel_id=1, source_target_pairs={{0,16},{16,32},{32,48},{48,64},{64,80},{80,96},{96,112},{1,17},{17... | collective-permute-start | bytes 294920 | tf_op jit(solution)/shard_map/ppermute | solution.py:445
  9.2 5.8 %copy-start.5 = (bf16[2,48,512]{2,1,0:T(8,128)(2,1)}, bf16[2,48,512]{2,1,0:T(8,128)(2,1)S(1)}, u32[]{:S(2)}) copy-start(bf16[2,48,512]{2,1,0:T(8,128)(2,1)S(1)} %collective-permute-done.1.below_ref) | copy-start | bytes 294916
  9.4 5.6 %copy-start.6 = (bf16[2,48,512]{2,1,0:T(8,128)(2,1)}, bf16[2,48,512]{2,1,0:T(8,128)(2,1)S(1)}, u32[]{:S(2)}) copy-start(bf16[2,48,512]{2,1,0:T(8,128)(2,1)S(1)} %collective-permute-done.above_ref) | copy-start | bytes 294916
  9.6 14.2 %collective-permute-start.2 = (bf16[68,2,512]{2,1,0:T(2,128)(2,1)S(1)}, bf16[68,2,512]{2,1,0:T(2,128)(2,1)S(1)}, u32[]{:S(2)}, u32[]{:S(2)}) collective-permute-start(bf16[68,2,512]{2,1,0:T(2,128)(2,1)S(1)} %pad_maximum_fusion), channel_id=1, source_target_pairs={{1,0},{2,1},{3,2},{4,3},{5,4},{6,5},{7,6},{8,7},{9,8},{10,9},{11,1... | collective-permute-start | bytes 417800 | tf_op jit(solution)/shard_map/ppermute | solution.py:445
  11.0 12.8 %collective-permute-start.3 = (bf16[68,2,512]{2,1,0:T(2,128)(2,1)S(1)}, bf16[68,2,512]{2,1,0:T(2,128)(2,1)S(1)}, u32[]{:S(2)}, u32[]{:S(2)}) collective-permute-start(bf16[68,2,512]{2,1,0:T(2,128)(2,1)S(1)} %pad_maximum_fusion.1), channel_id=1, source_target_pairs={{0,1},{1,2},{2,3},{3,4},{4,5},{5,6},{6,7},{7,8},{8,9},{9,10},{10,1... | collective-permute-start | bytes 417800 | tf_op jit(solution)/shard_map/ppermute | solution.py:445
  15.0 48.4 %all-to-all-start = ((bf16[16,4,48,256]{3,2,1,0:T(8,128)(2,1)}), bf16[16,4,48,256]{3,2,1,0:T(8,128)(2,1)S(1)}, u32[]{:S(2)}, u32[]{:S(2)}) async-start(bf16[16,4,48,256]{3,2,1,0:T(8,128)(2,1)} %bitcast.1), calls=%async_computation | async-start | bytes 3145728 | tf_op jit(solution)/shard_map/all_to_all | solution.py:434
  63.4 22.2 %all-to-all-start.1 = ((bf16[16,4,48,128]{3,2,1,0:T(8,128)(2,1)}), bf16[16,4,48,128]{3,2,1,0:T(8,128)(2,1)S(1)}, u32[]{:S(2)}, u32[]{:S(2)}) async-start(bf16[16,4,48,128]{3,2,1,0:T(8,128)(2,1)} %bitcast.42), calls=%async_computation.1 | async-start | bytes 1572864 | tf_op jit(solution)/shard_map/all_to_all | solution.py:434
  72.5 13.2 %copy-start = (f32[256]{0:T(256)S(1)}, f32[256]{0:T(256)}, u32[]{:S(2)}) copy-start(f32[256]{0:T(256)} %param.17) | copy-start | bytes 3076
  72.5 13.2 %copy-start.1 = (s32[6,6]{1,0:T(8,128)S(1)}, s32[6,6]{1,0:T(8,128)}, u32[]{:S(2)}) copy-start(s32[6,6]{1,0:T(8,128)} %mask_ref.2) | copy-start | bytes 436
  73.7 8.5 %collective-permute-start.10 = (bf16[6,64,384]{2,1,0:T(8,128)(2,1)S(1)}, bf16[6,64,384]{2,1,0:T(8,128)(2,1)S(1)}, u32[]{:S(2)}, u32[]{:S(2)}) collective-permute-start(bf16[6,64,384]{2,1,0:T(8,128)(2,1)S(1)} %get-tuple-element.39), channel_id=1, source_target_pairs={{0,112},{16,0},{32,16},{48,32},{64,48},{80,64},{96,80},{112,96},{1... | collective-permute-start | bytes 884744 | tf_op jit(solution)/shard_map/ppermute | solution.py:480
  73.9 10.4 %collective-permute-start.4 = (bf16[6,64,384]{2,1,0:T(8,128)(2,1)S(1)}, bf16[6,64,384]{2,1,0:T(8,128)(2,1)S(1)}, u32[]{:S(2)}, u32[]{:S(2)}) collective-permute-start(bf16[6,64,384]{2,1,0:T(8,128)(2,1)S(1)} %get-tuple-element.45), channel_id=1, source_target_pairs={{0,16},{16,32},{32,48},{48,64},{64,80},{80,96},{96,112},{112,0},{1... | collective-permute-start | bytes 884744 | tf_op jit(solution)/shard_map/ppermute | solution.py:480
  77.5 37.6 %collective-permute-start.5 = (bf16[6,64,384]{2,1,0:T(8,128)(2,1)}, bf16[6,64,384]{2,1,0:T(8,128)(2,1)S(1)}, u32[]{:S(2)}, u32[]{:S(2)}) collective-permute-start(bf16[6,64,384]{2,1,0:T(8,128)(2,1)} %get-tuple-element.44), channel_id=1, source_target_pairs={{0,32},{16,48},{32,64},{48,80},{64,96},{80,112},{96,0},{112,16},{1... | collective-permute-start | bytes 884744 | tf_op jit(solution)/shard_map/ppermute | solution.py:480
  79.1 35.9 %collective-permute-start.6 = (bf16[6,64,384]{2,1,0:T(8,128)(2,1)}, bf16[6,64,384]{2,1,0:T(8,128)(2,1)}, u32[]{:S(2)}, u32[]{:S(2)}) collective-permute-start(bf16[6,64,384]{2,1,0:T(8,128)(2,1)} %get-tuple-element.43), channel_id=1, source_target_pairs={{0,48},{16,64},{32,80},{48,96},{64,112},{80,0},{96,16},{112,32},{1... | collective-permute-start | bytes 884744 | tf_op jit(solution)/shard_map/ppermute | solution.py:480
  81.6 33.5 %collective-permute-start.7 = (bf16[6,64,384]{2,1,0:T(8,128)(2,1)}, bf16[6,64,384]{2,1,0:T(8,128)(2,1)}, u32[]{:S(2)}, u32[]{:S(2)}) collective-permute-start(bf16[6,64,384]{2,1,0:T(8,128)(2,1)} %get-tuple-element.42), channel_id=1, source_target_pairs={{0,64},{16,80},{32,96},{48,112},{64,0},{80,16},{96,32},{112,48},{1... | collective-permute-start | bytes 884744 | tf_op jit(solution)/shard_map/ppermute | solution.py:480
  82.2 32.9 %collective-permute-start.8 = (bf16[6,64,384]{2,1,0:T(8,128)(2,1)}, bf16[6,64,384]{2,1,0:T(8,128)(2,1)}, u32[]{:S(2)}, u32[]{:S(2)}) collective-permute-start(bf16[6,64,384]{2,1,0:T(8,128)(2,1)} %get-tuple-element.41), channel_id=1, source_target_pairs={{0,80},{16,96},{32,112},{48,0},{64,16},{80,32},{96,48},{112,64},{1... | collective-permute-start | bytes 884744 | tf_op jit(solution)/shard_map/ppermute | solution.py:480
  84.3 30.8 %collective-permute-start.9 = (bf16[6,64,384]{2,1,0:T(8,128)(2,1)}, bf16[6,64,384]{2,1,0:T(8,128)(2,1)}, u32[]{:S(2)}, u32[]{:S(2)}) collective-permute-start(bf16[6,64,384]{2,1,0:T(8,128)(2,1)} %get-tuple-element.40), channel_id=1, source_target_pairs={{0,96},{16,112},{32,0},{48,16},{64,32},{80,48},{96,64},{112,80},{1... | collective-permute-start | bytes 884744 | tf_op jit(solution)/shard_map/ppermute | solution.py:480
  85.6 1.0 copy-start.3
  115.1 7.0 %copy-start.2 = (s32[4,4]{1,0:T(4,128)S(1)}, s32[4,4]{1,0:T(4,128)}, u32[]{:S(2)}) copy-start(s32[4,4]{1,0:T(4,128)} %mask_ref.3) | copy-start | bytes 196
  115.1 7.0 %copy-start.4 = (bf16[2,256,384]{2,1,0:T(8,128)(2,1)S(1)}, bf16[2,256,384]{2,1,0:T(8,128)(2,1)}, u32[]{:S(2)}) copy-start(bf16[2,256,384]{2,1,0:T(8,128)(2,1)} %get-tuple-element.26.refs_3_.refs_9_) | copy-start | bytes 1179652
  115.1 27.1 %all-to-all-start.2 = ((bf16[16,4,48,256]{3,2,1,0:T(8,128)(2,1)}), bf16[16,4,48,256]{3,2,1,0:T(8,128)(2,1)}, u32[]{:S(2)}, u32[]{:S(2)}) async-start(bf16[16,4,48,256]{3,2,1,0:T(8,128)(2,1)} %axial_attention.2), calls=%async_computation.2 | async-start | bytes 3145728 | tf_op jit(solution)/shard_map/all_to_all | solution.py:434

commit v8 on v7

--- a/solution.py
+++ b/solution.py
@@ -19,6 +19,7 @@
 GROUP = 8
 CHUNK = GROUP * STRIDE
 BIG = 8
+FIN = 16
 GUARD = 2
 RING = 3 * GROUP
 FC = 256
@@ -171,29 +172,35 @@
         slopes(trips - 2, part)
     products(trips - 1)
 
+    deep = FIN * STRIDE
+
+    def turned(values):
+        return jnp.swapaxes(values.astype(F32).reshape(FIN, cols, values.shape[-1]), 0, 1).astype(BF16)
+
     def finish(i, c):
-        base = rows_at(i * BIG + 3 + GUARD)
-        right = y_s[0, pl.ds(base, tall + 8), :][1:1 + tall]
-        left = y_s[2, pl.ds(base - 8, tall + 8), :][7:7 + tall]
-        total = y_s[1, pl.ds(base, tall), :] + right + left
+        base = rows_at(i * FIN + 3 + GUARD)
+        right = y_s[0, pl.ds(base, deep + 8), :][1:1 + deep]
+        left = y_s[2, pl.ds(base - 8, deep + 8), :][7:7 + deep]
+        total = y_s[1, pl.ds(base, deep), :] + right + left
 
         def crop(v):
-            return v.reshape(BIG, STRIDE, width)[:, :cols].reshape(BIG * cols, width)
+            return v.reshape(FIN, STRIDE, width)[:, :cols].reshape(FIN * cols, width)
 
         e = crop(total) * gain
-        src = pl.ds(i * BIG, BIG)
-        hat, inv = normalize(mid_ref[src].reshape(BIG * cols, width).astype(F32))
-        res = gout_ref[src].reshape(BIG * cols, width).astype(F32) + inv * (
+        src = pl.ds(i * FIN, FIN)
+        hat, inv = normalize(mid_ref[src].reshape(FIN * cols, width).astype(F32))
+        res = gout_ref[src].reshape(FIN * cols, width).astype(F32) + inv * (
             e - jnp.mean(e, axis=-1, keepdims=True) - hat * jnp.mean(e * hat, axis=-1, keepdims=True))
         res = res.astype(BF16)
-        dst = pl.ds(i * BIG, BIG)
-        gm_ref[dst] = res.reshape(BIG, cols, width)
-        ga = dot_nt(res, wout_ref[...]).astype(BF16)
-        grow_ref[dst] = ga[:, :width // 2].reshape(BIG, cols, width // 2)
-        gcol_ref[dst, :, width:] = ga[:, width // 2:].reshape(BIG, cols, width // 2)
-        gcol_ref[dst, :, :width] = tok_ref[dst]
+        dst = pl.ds(i * FIN, FIN)
+        gm_ref[dst] = res.reshape(FIN, cols, width)
+        ga = dot_nt(res, wout_ref[...])
+        grow_ref[dst] = ga[:, :width // 2].astype(BF16).reshape(FIN, cols, width // 2)
+        across = pl.ds(pl.multiple_of(i * FIN, FIN), FIN)
+        gcol_ref[:, across, width:] = turned(ga[:, width // 2:])
+        gcol_ref[:, across, :width] = turned(tok_ref[dst].astype(F32).reshape(FIN * cols, width))
         return c
-    lax.fori_loop(0, rows // BIG, finish, 0)
+    lax.fori_loop(0, rows // FIN, finish, 0)
 
 
 def mlp(mid, grad, tokens, above, below, edge, gain, w_up, conv_kernel, w_down, w_out, w_query, w_key, w_value):
@@ -205,7 +212,9 @@
     whole = pl.BlockSpec(memory_space=pltpu.VMEM)
     return pl.pallas_call(
         functools.partial(mlp_kernel, rows, cols),
-        out_shape=tuple(jax.ShapeDtypeStruct((rows, cols, n), BF16) for n in (width, width // 2, width + width // 2)) + (
+        out_shape=(
+            jax.ShapeDtypeStruct((rows, cols, width), BF16), jax.ShapeDtypeStruct((rows, cols, width // 2), BF16),
+            jax.ShapeDtypeStruct((cols, rows, width + width // 2), BF16),
             jax.ShapeDtypeStruct((2, width, 3 * width // 2), BF16),),
         in_specs=[whole] * 14,
         out_specs=(whole,) * 4,
@@ -434,11 +443,6 @@
     return lax.all_to_all(blocks, axis, split_axis=0, concat_axis=0, tiled=True)
 
 
-def cut_cols(tile, count):
-    rows, cols, width = tile.shape
-    return jnp.transpose(tile.reshape(rows, count, cols // count, width), (1, 2, 0, 3))
-
-
 def neighbours(ahead, behind, axis):
     count = lax.axis_size(axis)
     up = [(i, i + 1) for i in range(count - 1)]
@@ -472,7 +476,7 @@
     grad_row, row_tokens = hold((grad_row, row_tokens))
     grad_row = to_lines(grad_row.reshape(count_gx, rows // count_gx, cols, half), "gx")
     here = lax.axis_index("gy")
-    col_send = cut_cols(grad_col, count_gy)
+    col_send = grad_col.reshape(count_gy, cols // count_gy, rows, grad_col.shape[-1])
     col_parts = []
     for ahead in range(count_gy):
         part = lax.dynamic_index_in_dim(col_send, (here + ahead) % count_gy, 0, keepdims=False)

time: 180 us -> 184 us (1.022)
  Pallas kernels: 92.2 us -> 100 us
    pallas_call x2, Pallas kernels: 48 us -> 55.9 us  [attention(): pl.pallas_call(functools.partial(attn_kernel, nl, nk, half, pieces), out_...]
    pallas_call x1 -> x0, local copies, waits for them, and re-layouts: 2.26 us -> none  [mlp(): pl.pallas_call(functools.partial(mlp_kernel, rows, cols), out_shape=tuple...]
  transfers between devices with their start and end apart: 14 -> 14, of which waited for: 3 -> 2; matrix products, arithmetic and copies ran while one was open for 4% -> 3% of each run, Pallas kernels for 49% -> 52%
where the time goes in v8:
time: 184 us; the launch traced here: 182 us
  Pallas kernels  100 us (54%)
  starting transfers between devices  45.8 us (25%)
  blocking collectives  26.5 us (14%)
  local copies, waits for them, and re-layouts  6.22 us (3%)
    pallas_call x2, Pallas kernels, attention(): pl.pallas_call(functools.partial(attn_kernel, nl, nk, half, pieces), out_...  55.9 us
    pallas_call x1, Pallas kernels, mlp(): pl.pallas_call(functools.partial(mlp_kernel, rows, cols), out_shape=(jax....  38.4 us
    all_to_all x1, blocking collectives, to_lines(): return lax.all_to_all(blocks, axis, split_axis=0, concat_axis=0, tiled=True)  26.5 us
    all_to_all x3, starting transfers between devices, to_lines(): return lax.all_to_all(blocks, axis, split_axis=0, concat_axis=0, tiled=True)  22.4 us
    ppermute x7, starting transfers between devices, per_device(): lax.ppermute(part, 'gy', [(i, (i + ahead) % count_gy) for i in range(coun...  11.3 us
    ppermute x2, starting transfers between devices, neighbours(): lax.ppermute(ahead, axis, up)  7.52 us
    pallas_call x1, Pallas kernels, final(): pl.pallas_call(final_kernel, out_shape=jax.ShapeDtypeStruct(tokens.shape,...  6.15 us
    ppermute x2, starting transfers between devices, neighbours(): lax.ppermute(behind, axis, [(j, i) for i, j in up])  4.62 us
  transfers between devices with their start and end apart: 14, of which 2 were waited for; matrix products, arithmetic and copies ran while one was open for 3% of the time, Pallas kernels for 52%

profile of v8, /device:TPU:1, one launch (start us, length us, event | category | flops | bytes accessed | tf_op | source)
XLA Modules:
  0.0 182.0 jit_solution(1570967328252230615)
XLA Ops:
  0.0 0.9 fusion.7
  0.9 3.3 %collective-permute-start.1 = (bf16[2,48,512]{2,1,0:T(8,128)(2,1)S(1)}, bf16[2,48,512]{2,1,0:T(8,128)(2,1)S(1)}, u32[]{:S(2)}, u32[]{:S(2)}) collective-permute-start(bf16[2,48,512]{2,1,0:T(8,128)(2,1)S(1)} %pad_maximum_fusion.3), channel_id=1, source_target_pairs={{16,0},{32,16},{48,32},{64,48},{80,64},{96,80},{112,96},{17,1},{33... | collective-permute-start | bytes 294920 | tf_op jit(solution)/shard_map/ppermute | solution.py:449
  4.3 3.5 %collective-permute-start = (bf16[2,48,512]{2,1,0:T(8,128)(2,1)S(1)}, bf16[2,48,512]{2,1,0:T(8,128)(2,1)S(1)}, u32[]{:S(2)}, u32[]{:S(2)}) collective-permute-start(bf16[2,48,512]{2,1,0:T(8,128)(2,1)S(1)} %pad_maximum_fusion.2), channel_id=1, source_target_pairs={{0,16},{16,32},{32,48},{48,64},{64,80},{80,96},{96,112},{1,17},{17... | collective-permute-start | bytes 294920 | tf_op jit(solution)/shard_map/ppermute | solution.py:449
  7.8 1.4 fusion.5
  9.2 0.0 collective-permute-done.1.below_ref
  9.2 0.0 copy-start.5
  9.2 0.2 collective-permute-done.above_ref
  9.4 0.0 copy-start.6
  9.4 0.1 pad_maximum_fusion
  9.6 1.3 collective-permute-start.2
  10.9 0.1 pad_maximum_fusion.1
  11.0 4.0 %collective-permute-start.3 = (bf16[68,2,512]{2,1,0:T(2,128)(2,1)S(1)}, bf16[68,2,512]{2,1,0:T(2,128)(2,1)S(1)}, u32[]{:S(2)}, u32[]{:S(2)}) collective-permute-start(bf16[68,2,512]{2,1,0:T(2,128)(2,1)S(1)} %pad_maximum_fusion.1), channel_id=1, source_target_pairs={{0,1},{1,2},{2,3},{3,4},{4,5},{5,6},{6,7},{7,8},{8,9},{9,10},{10,1... | collective-permute-start | bytes 417800 | tf_op jit(solution)/shard_map/ppermute | solution.py:449
  15.0 0.0 copy-done.5
  15.0 0.0 copy-done.6
  15.0 8.7 %all-to-all-start = ((bf16[16,4,48,256]{3,2,1,0:T(8,128)(2,1)}), bf16[16,4,48,256]{3,2,1,0:T(8,128)(2,1)S(1)}, u32[]{:S(2)}, u32[]{:S(2)}) async-start(bf16[16,4,48,256]{3,2,1,0:T(8,128)(2,1)} %bitcast.1), calls=%async_computation | async-start | bytes 3145728 | tf_op jit(solution)/shard_map/all_to_all | solution.py:443
  23.7 0.1 pad.11.clone
  23.8 0.0 collective-permute-done.2
  23.8 0.0 collective-permute-done.3
  23.8 1.5 fusion.2.edge_ref
  25.3 38.4 %mlp_backward.1 = (bf16[64,48,256]{2,1,0:T(8,128)(2,1)}, bf16[64,48,128]{2,1,0:T(8,128)(2,1)}, bf16[48,64,384]{2,1,0:T(8,128)(2,1)}, bf16[2,256,384]{2,1,0:T(8,128)(2,1)}) custom-call(bf16[64,48,256]{2,1,0:T(8,128)(2,1)} %mid_ref.1, bf16[64,48,256]{2,1,0:T(8,128)(2,1)} %gout_ref.1, bf16[64,48,256]{2,1,0:T(8,128)(2,1)} %tok_ref.3, ...), custom_call_target="tpu_custom_call" | custom-call | flops 20000000000 | bytes 12000000 | tf_op jit(solution)/shard_map/mlp_backward/pallas_call | solution.py:213
  63.8 0.0 all-to-all-done.refs_0_
  63.8 6.7 %all-to-all-start.1 = ((bf16[16,4,48,128]{3,2,1,0:T(8,128)(2,1)}), bf16[16,4,48,128]{3,2,1,0:T(8,128)(2,1)S(1)}, u32[]{:S(2)}, u32[]{:S(2)}) async-start(bf16[16,4,48,128]{3,2,1,0:T(8,128)(2,1)} %bitcast.26), calls=%async_computation.1 | async-start | bytes 1572864 | tf_op jit(solution)/shard_map/all_to_all | solution.py:443
  70.5 0.0 copy-start
  70.6 0.0 copy-start.1
  70.6 2.8 %dynamic-slice_bitcast_fusion = (bf16[6,64,384]{2,1,0:T(8,128)(2,1)S(1)}, bf16[6,64,384]{2,1,0:T(8,128)(2,1)}, bf16[6,64,384]{2,1,0:T(8,128)(2,1)}, bf16[6,64,38...) fusion(bf16[8,6,64,384]{3,2,1,0:T(8,128)(2,1)} %bitcast.25, ...), kind=kLoop, calls=%fused_computation.6 | loop fusion | bytes 4718624 | tf_op jit(solution)/shard_map/jit(dynamic_index_in_dim)/squeeze | solution.py:482
  73.4 0.2 collective-permute-start.10
  73.6 3.6 %collective-permute-start.4 = (bf16[6,64,384]{2,1,0:T(8,128)(2,1)S(1)}, bf16[6,64,384]{2,1,0:T(8,128)(2,1)S(1)}, u32[]{:S(2)}, u32[]{:S(2)}) collective-permute-start(bf16[6,64,384]{2,1,0:T(8,128)(2,1)S(1)} %get-tuple-element.45), channel_id=1, source_target_pairs={{0,16},{16,32},{32,48},{48,64},{64,80},{80,96},{96,112},{112,0},{1... | collective-permute-start | bytes 884744 | tf_op jit(solution)/shard_map/ppermute | solution.py:484
  77.2 1.6 collective-permute-start.5
  78.8 2.4 %collective-permute-start.6 = (bf16[6,64,384]{2,1,0:T(8,128)(2,1)}, bf16[6,64,384]{2,1,0:T(8,128)(2,1)}, u32[]{:S(2)}, u32[]{:S(2)}) collective-permute-start(bf16[6,64,384]{2,1,0:T(8,128)(2,1)} %get-tuple-element.43), channel_id=1, source_target_pairs={{0,48},{16,64},{32,80},{48,96},{64,112},{80,0},{96,16},{112,32},{1... | collective-permute-start | bytes 884744 | tf_op jit(solution)/shard_map/ppermute | solution.py:484
  81.3 0.0 collective-permute-start.7
  81.3 0.6 collective-permute-done.10.refs_7_
  81.9 2.1 %collective-permute-start.8 = (bf16[6,64,384]{2,1,0:T(8,128)(2,1)}, bf16[6,64,384]{2,1,0:T(8,128)(2,1)}, u32[]{:S(2)}, u32[]{:S(2)}) collective-permute-start(bf16[6,64,384]{2,1,0:T(8,128)(2,1)} %get-tuple-element.41), channel_id=1, source_target_pairs={{0,80},{16,96},{32,112},{48,0},{64,16},{80,32},{96,48},{112,64},{1... | collective-permute-start | bytes 884744 | tf_op jit(solution)/shard_map/ppermute | solution.py:484
  84.0 0.0 collective-permute-done.4.refs_1_
  84.0 1.3 collective-permute-start.9
  85.3 0.0 all-to-all-done.1.refs_1_
  85.3 0.0 copy-done
  85.3 0.0 copy-done.1
  85.3 0.0 copy-start.3
  85.4 1.0 copy-done.3
  86.3 31.8 %axial_attention.2 = bf16[16,4,48,256]{3,2,1,0:T(8,128)(2,1)} custom-call(s32[6,6]{1,0:T(8,128)S(1)} %copy-done.1, s32[8]{0:T(128)S(1)} %and_select_fusion.at_ref, bf16[16,4,48,256]{3,2,1,0:T(8,128)(2,1)S(1)} %all-to-all-done.refs_0_, bf16[16,4,48,128]{3,2,1,0:T(8,128)(2,1)S(1)} %all-to-all-done.1.refs_1_, f32[1,256]{1,0:T(1,128)S(1)} %bitcast.23, ...), custom_call_target="tpu_custom_call" | custom-call | flops 28800000000 | bytes 4000000 | tf_op jit(solution)/shard_map/axial_attention/pallas_call | solution.py:386
  118.1 0.0 collective-permute-done.5.refs_2_
  118.1 0.0 collective-permute-done.6.refs_3_
  118.1 0.0 collective-permute-done.7.refs_4_
  118.1 0.0 collective-permute-done.8.refs_5_
  118.1 0.0 collective-permute-done.9.refs_6_
  118.1 0.0 copy-start.2
  118.1 0.0 copy-start.4
  118.1 7.0 %all-to-all-start.2 = ((bf16[16,4,48,256]{3,2,1,0:T(8,128)(2,1)}), bf16[16,4,48,256]{3,2,1,0:T(8,128)(2,1)}, u32[]{:S(2)}, u32[]{:S(2)}) async-start(bf16[16,4,48,256]{3,2,1,0:T(8,128)(2,1)} %axial_attention.2), calls=%async_computation.2 | async-start | bytes 3145728 | tf_op jit(solution)/shard_map/all_to_all | solution.py:443
  125.2 0.0 copy-done.2
  125.2 0.0 copy-done.4
  125.2 24.1 %axial_attention.3 = bf16[8,6,64,256]{3,2,1,0:T(8,128)(2,1)S(1)} custom-call(s32[4,4]{1,0:T(4,128)S(1)} %copy-done.2, s32[8]{0:T(128)S(1)} %and_select_fusion.at_ref, bf16[6,64,384]{2,1,0:T(8,128)(2,1)S(1)} %get-tuple-element.29.refs_0_, bf16[6,64,384]{2,1,0:T(8,128)(2,1)S(1)} %collective-permute-done.4.refs_1_, ...), custom_call_target="tpu_custom_call" | custom-call | flops 19200000000 | bytes 4000000 | tf_op jit(solution)/shard_map/axial_attention/pallas_call | solution.py:386
  149.3 0.0 all-to-all-done.2
  149.3 26.5 %all_to_all.20.col_ref = bf16[8,6,64,256]{3,2,1,0:T(8,128)(2,1)} all-to-all(bf16[8,6,64,256]{3,2,1,0:T(8,128)(2,1)S(1)} %axial_attention.3), channel_id=1, replica_groups=mesh['gy'=8,'gx'=16] {'gy'}, dimensions={0} | all-to-all | bytes 3145728 | tf_op jit(solution)/shard_map/all_to_all | solution.py:443
  175.8 6.2 %norm_backward.1 = bf16[64,48,256]{2,1,0:T(8,128)(2,1)} custom-call(bf16[64,48,256]{2,1,0:T(8,128)(2,1)} %tok_ref.3, bf16[64,48,256]{2,1,0:T(8,128)(2,1)} %get-tuple-element.22.mid_ref, bf16[64,48,256]{2,1,0:T(8,128)(2,1)} %bitcast.13.row_ref, bf16[8,6,64,256]{3,2,1,0:T(8,128)(2,1)} %all_to_all.20.col_ref, f32[1,256]{1,0:T(1,128)} %bitcast.22), custom_call_target="tpu_custom_call" | custom-call | flops 20000000 | bytes 8000000 | tf_op jit(solution)/shard_map/norm_backward/pallas_call | solution.py:431
  (6 shorter events, 0.1 us)
Async XLA Ops:
  0.9 8.3 %collective-permute-start.1 = (bf16[2,48,512]{2,1,0:T(8,128)(2,1)S(1)}, bf16[2,48,512]{2,1,0:T(8,128)(2,1)S(1)}, u32[]{:S(2)}, u32[]{:S(2)}) collective-permute-start(bf16[2,48,512]{2,1,0:T(8,128)(2,1)S(1)} %pad_maximum_fusion.3), channel_id=1, source_target_pairs={{16,0},{32,16},{48,32},{64,48},{80,64},{96,80},{112,96},{17,1},{33... | collective-permute-start | bytes 294920 | tf_op jit(solution)/shard_map/ppermute | solution.py:449
  4.3 5.2 %collective-permute-start = (bf16[2,48,512]{2,1,0:T(8,128)(2,1)S(1)}, bf16[2,48,512]{2,1,0:T(8,128)(2,1)S(1)}, u32[]{:S(2)}, u32[]{:S(2)}) collective-permute-start(bf16[2,48,512]{2,1,0:T(8,128)(2,1)S(1)} %pad_maximum_fusion.2), channel_id=1, source_target_pairs={{0,16},{16,32},{32,48},{48,64},{64,80},{80,96},{96,112},{1,17},{17... | collective-permute-start | bytes 294920 | tf_op jit(solution)/shard_map/ppermute | solution.py:449
  9.2 5.8 %copy-start.5 = (bf16[2,48,512]{2,1,0:T(8,128)(2,1)}, bf16[2,48,512]{2,1,0:T(8,128)(2,1)S(1)}, u32[]{:S(2)}) copy-start(bf16[2,48,512]{2,1,0:T(8,128)(2,1)S(1)} %collective-permute-done.1.below_ref) | copy-start | bytes 294916
  9.4 5.6 %copy-start.6 = (bf16[2,48,512]{2,1,0:T(8,128)(2,1)}, bf16[2,48,512]{2,1,0:T(8,128)(2,1)S(1)}, u32[]{:S(2)}) copy-start(bf16[2,48,512]{2,1,0:T(8,128)(2,1)S(1)} %collective-permute-done.above_ref) | copy-start | bytes 294916
  9.6 14.2 %collective-permute-start.2 = (bf16[68,2,512]{2,1,0:T(2,128)(2,1)S(1)}, bf16[68,2,512]{2,1,0:T(2,128)(2,1)S(1)}, u32[]{:S(2)}, u32[]{:S(2)}) collective-permute-start(bf16[68,2,512]{2,1,0:T(2,128)(2,1)S(1)} %pad_maximum_fusion), channel_id=1, source_target_pairs={{1,0},{2,1},{3,2},{4,3},{5,4},{6,5},{7,6},{8,7},{9,8},{10,9},{11,1... | collective-permute-start | bytes 417800 | tf_op jit(solution)/shard_map/ppermute | solution.py:449
  11.0 12.8 %collective-permute-start.3 = (bf16[68,2,512]{2,1,0:T(2,128)(2,1)S(1)}, bf16[68,2,512]{2,1,0:T(2,128)(2,1)S(1)}, u32[]{:S(2)}, u32[]{:S(2)}) collective-permute-start(bf16[68,2,512]{2,1,0:T(2,128)(2,1)S(1)} %pad_maximum_fusion.1), channel_id=1, source_target_pairs={{0,1},{1,2},{2,3},{3,4},{4,5},{5,6},{6,7},{7,8},{8,9},{9,10},{10,1... | collective-permute-start | bytes 417800 | tf_op jit(solution)/shard_map/ppermute | solution.py:449
  15.0 48.7 %all-to-all-start = ((bf16[16,4,48,256]{3,2,1,0:T(8,128)(2,1)}), bf16[16,4,48,256]{3,2,1,0:T(8,128)(2,1)S(1)}, u32[]{:S(2)}, u32[]{:S(2)}) async-start(bf16[16,4,48,256]{3,2,1,0:T(8,128)(2,1)} %bitcast.1), calls=%async_computation | async-start | bytes 3145728 | tf_op jit(solution)/shard_map/all_to_all | solution.py:443
  63.8 21.6 %all-to-all-start.1 = ((bf16[16,4,48,128]{3,2,1,0:T(8,128)(2,1)}), bf16[16,4,48,128]{3,2,1,0:T(8,128)(2,1)S(1)}, u32[]{:S(2)}, u32[]{:S(2)}) async-start(bf16[16,4,48,128]{3,2,1,0:T(8,128)(2,1)} %bitcast.26), calls=%async_computation.1 | async-start | bytes 1572864 | tf_op jit(solution)/shard_map/all_to_all | solution.py:443
  70.5 14.8 %copy-start = (f32[256]{0:T(256)S(1)}, f32[256]{0:T(256)}, u32[]{:S(2)}) copy-start(f32[256]{0:T(256)} %param.17) | copy-start | bytes 3076
  70.6 14.8 %copy-start.1 = (s32[6,6]{1,0:T(8,128)S(1)}, s32[6,6]{1,0:T(8,128)}, u32[]{:S(2)}) copy-start(s32[6,6]{1,0:T(8,128)} %mask_ref.2) | copy-start | bytes 436
  73.4 8.5 %collective-permute-start.10 = (bf16[6,64,384]{2,1,0:T(8,128)(2,1)S(1)}, bf16[6,64,384]{2,1,0:T(8,128)(2,1)S(1)}, u32[]{:S(2)}, u32[]{:S(2)}) collective-permute-start(bf16[6,64,384]{2,1,0:T(8,128)(2,1)S(1)} %get-tuple-element.39), channel_id=1, source_target_pairs={{0,112},{16,0},{32,16},{48,32},{64,48},{80,64},{96,80},{112,96},{1... | collective-permute-start | bytes 884744 | tf_op jit(solution)/shard_map/ppermute | solution.py:484
  73.6 10.4 %collective-permute-start.4 = (bf16[6,64,384]{2,1,0:T(8,128)(2,1)S(1)}, bf16[6,64,384]{2,1,0:T(8,128)(2,1)S(1)}, u32[]{:S(2)}, u32[]{:S(2)}) collective-permute-start(bf16[6,64,384]{2,1,0:T(8,128)(2,1)S(1)} %get-tuple-element.45), channel_id=1, source_target_pairs={{0,16},{16,32},{32,48},{48,64},{64,80},{80,96},{96,112},{112,0},{1... | collective-permute-start | bytes 884744 | tf_op jit(solution)/shard_map/ppermute | solution.py:484
  77.2 40.9 %collective-permute-start.5 = (bf16[6,64,384]{2,1,0:T(8,128)(2,1)}, bf16[6,64,384]{2,1,0:T(8,128)(2,1)S(1)}, u32[]{:S(2)}, u32[]{:S(2)}) collective-permute-start(bf16[6,64,384]{2,1,0:T(8,128)(2,1)} %get-tuple-element.44), channel_id=1, source_target_pairs={{0,32},{16,48},{32,64},{48,80},{64,96},{80,112},{96,0},{112,16},{1... | collective-permute-start | bytes 884744 | tf_op jit(solution)/shard_map/ppermute | solution.py:484
  78.8 39.3 %collective-permute-start.6 = (bf16[6,64,384]{2,1,0:T(8,128)(2,1)}, bf16[6,64,384]{2,1,0:T(8,128)(2,1)}, u32[]{:S(2)}, u32[]{:S(2)}) collective-permute-start(bf16[6,64,384]{2,1,0:T(8,128)(2,1)} %get-tuple-element.43), channel_id=1, source_target_pairs={{0,48},{16,64},{32,80},{48,96},{64,112},{80,0},{96,16},{112,32},{1... | collective-permute-start | bytes 884744 | tf_op jit(solution)/shard_map/ppermute | solution.py:484
  81.3 36.8 %collective-permute-start.7 = (bf16[6,64,384]{2,1,0:T(8,128)(2,1)}, bf16[6,64,384]{2,1,0:T(8,128)(2,1)}, u32[]{:S(2)}, u32[]{:S(2)}) collective-permute-start(bf16[6,64,384]{2,1,0:T(8,128)(2,1)} %get-tuple-element.42), channel_id=1, source_target_pairs={{0,64},{16,80},{32,96},{48,112},{64,0},{80,16},{96,32},{112,48},{1... | collective-permute-start | bytes 884744 | tf_op jit(solution)/shard_map/ppermute | solution.py:484
  81.9 36.2 %collective-permute-start.8 = (bf16[6,64,384]{2,1,0:T(8,128)(2,1)}, bf16[6,64,384]{2,1,0:T(8,128)(2,1)}, u32[]{:S(2)}, u32[]{:S(2)}) collective-permute-start(bf16[6,64,384]{2,1,0:T(8,128)(2,1)} %get-tuple-element.41), channel_id=1, source_target_pairs={{0,80},{16,96},{32,112},{48,0},{64,16},{80,32},{96,48},{112,64},{1... | collective-permute-start | bytes 884744 | tf_op jit(solution)/shard_map/ppermute | solution.py:484
  84.0 34.1 %collective-permute-start.9 = (bf16[6,64,384]{2,1,0:T(8,128)(2,1)}, bf16[6,64,384]{2,1,0:T(8,128)(2,1)}, u32[]{:S(2)}, u32[]{:S(2)}) collective-permute-start(bf16[6,64,384]{2,1,0:T(8,128)(2,1)} %get-tuple-element.40), channel_id=1, source_target_pairs={{0,96},{16,112},{32,0},{48,16},{64,32},{80,48},{96,64},{112,80},{1... | collective-permute-start | bytes 884744 | tf_op jit(solution)/shard_map/ppermute | solution.py:484
  85.3 1.0 copy-start.3
  118.1 7.0 %copy-start.2 = (s32[4,4]{1,0:T(4,128)S(1)}, s32[4,4]{1,0:T(4,128)}, u32[]{:S(2)}) copy-start(s32[4,4]{1,0:T(4,128)} %mask_ref.3) | copy-start | bytes 196
  118.1 7.0 %copy-start.4 = (bf16[2,256,384]{2,1,0:T(8,128)(2,1)S(1)}, bf16[2,256,384]{2,1,0:T(8,128)(2,1)}, u32[]{:S(2)}) copy-start(bf16[2,256,384]{2,1,0:T(8,128)(2,1)} %get-tuple-element.26.refs_3_.refs_9_) | copy-start | bytes 1179652
  118.1 31.2 %all-to-all-start.2 = ((bf16[16,4,48,256]{3,2,1,0:T(8,128)(2,1)}), bf16[16,4,48,256]{3,2,1,0:T(8,128)(2,1)}, u32[]{:S(2)}, u32[]{:S(2)}) async-start(bf16[16,4,48,256]{3,2,1,0:T(8,128)(2,1)} %axial_attention.2), calls=%async_computation.2 | async-start | bytes 3145728 | tf_op jit(solution)/shard_map/all_to_all | solution.py:443
